TPU v7x, 128 devices: a whole 4x4x4 slice. The times are simulated.
128 devices in a mesh: task: 4 (over y), shard: 32 (over x, z, core).
Axes of the slice: x: 4, y: 4, z: 4, core: 2. Of those that a mesh axis runs over, the one named last changes fastest.
Arguments:
- tokens: bfloat16 [4096, 4096], P(('task', 'shard')), may hold values from -600 to 600
- gain: float32 [4096], replicated, may hold values from 0.5 to 1.5
- task_ids: int32 [4096], P(('task', 'shard')), may hold values from 0 to 7, as said below
- order: int32 [4096], P(('task', 'shard')), may hold values from 0 to 31, as said below
- w_gate: bfloat16 [8, 4096, 14336], P('task', None, 'shard'), may hold values from -0.09375 to 0.09375
- w_up: bfloat16 [8, 4096, 14336], P('task', None, 'shard'), may hold values from -0.09375 to 0.09375
- w_down: bfloat16 [8, 14336, 4096], P('task', 'shard'), may hold values from -0.046875 to 0.046875
Outputs:
- mixed: bfloat16 [4096, 4096], P(('task', 'shard'))
Inputs may be any that keep to these rules, and one draw needn't show every extreme that they name: `task_ids`: in each aligned block of 32 rows (the rows of one device) at most 8 rows name any one task; one task, the same for all blocks, is named by exactly 8 rows of every block. `order`: each aligned block of 32 entries is a permutation of 0 to 31.
All inputs are finite; a program needn't handle non-finite values.
Results may differ from a plain program's by a relative error of at most 0.015.
Values may be sent and summed in bfloat16 or wider, within the bound.
No kernel may reach another device: no remote copies, remote signals or barrier semaphores. Data moves between devices by JAX's collectives and lax.ppermute only.
A program may use at most 128 MiB of HBM per device.

v0:
```python
import functools
import jax
import jax.numpy as jnp
from jax import lax
from jax.experimental import pallas as pl
from jax.experimental.pallas import tpu as pltpu
from jax.sharding import Mesh, PartitionSpec as P

CAP = 8
RING = 4
CORES = 2
EPSILON = 1e-06
F32 = jnp.float32
BF16 = jnp.bfloat16


def shift(v, axis, step):
    return lax.ppermute(v, axis, [(i, (i + step) % RING) for i in range(RING)])


def swap_cores(v):
    return lax.ppermute(v, "core", [(0, 1), (1, 0)])


CHUNK = 256
WIDE = 1024
ANYWHERE = pl.BlockSpec(memory_space=pl.ANY)
IN_VMEM = pl.BlockSpec(memory_space=pltpu.VMEM)


def in_vmem(v):
    return pltpu.with_memory_space_constraint(v, pltpu.VMEM)


def in_hbm(v):
    return pltpu.with_memory_space_constraint(v, pltpu.HBM)


def run_copies(copies):
    for copy in copies:
        copy.start()
    for copy in copies:
        copy.wait()


def dispatch_kernel(
    task_hbm, order_hbm, tokens_hbm, gain_hbm, out, select, tokens, gain, task_ref, order_ref,
    count, slot, sem,
):
    sources = (task_hbm, order_hbm, tokens_hbm, gain_hbm)
    places = (task_ref, order_ref, tokens, gain)
    copies = [
        pltpu.make_async_copy(v, w, sem.at[i]) for i, (v, w) in enumerate(zip(sources, places))
    ]
    for copy in copies:
        copy.start()
    group = lax.axis_index("task")
    core = lax.axis_index("core")
    rows = tokens.shape[0]
    slots = out.shape[0]
    experts = count.shape[0]
    for e in range(experts):
        count[e] = 0
    copies[0].wait()
    lanes = lax.broadcasted_iota(jnp.int32, (slots, rows), 1)
    targets = jnp.zeros((slots, rows), jnp.int32)
    for r in range(rows):
        task = task_ref[r]
        position = count[task]
        count[task] = position + 1
        far = (task // CORES - group) & (RING - 1)
        other = (task + core) & (CORES - 1)
        at = (other * RING + far) * CAP + position
        slot[r] = at
        targets = jnp.where(lanes == r, at, targets)
    placing = (lax.broadcasted_iota(jnp.int32, (slots, rows), 0) == targets).astype(BF16)
    copies[2].wait()
    copies[3].wait()
    values = tokens[...].astype(F32)
    mean_square = jnp.mean(values * values, axis=-1, keepdims=True)
    normed = (values * lax.rsqrt(mean_square + EPSILON) * gain[...]).astype(BF16)
    out[...] = jnp.dot(placing, normed, preferred_element_type=F32).astype(BF16)
    copies[1].wait()
    sublanes = lax.broadcasted_iota(jnp.int32, (rows, slots), 0)
    wanted = jnp.zeros((rows, slots), jnp.int32)
    for r in range(rows):
        wanted = jnp.where(sublanes == r, slot[order_ref[r]], wanted)
    chosen = lax.broadcasted_iota(jnp.int32, (rows, slots), 1) == wanted
    select[...] = chosen.astype(BF16)


def dispatch(task_ids, order, tokens, gain, experts):
    rows, width = tokens.shape
    slots = experts * CAP
    arrays = (task_ids, order, tokens, gain.reshape(1, width))
    return pl.pallas_call(
        dispatch_kernel,
        out_shape=[pltpu.VMEM((slots, width), BF16), pltpu.VMEM((rows, slots), BF16)],
        in_specs=[ANYWHERE] * 4,
        out_specs=[IN_VMEM] * 2,
        scratch_shapes=[
            pltpu.VMEM((rows, width), BF16),
            pltpu.VMEM((1, width), F32),
            pltpu.SMEM((rows,), jnp.int32),
            pltpu.SMEM((rows,), jnp.int32),
            pltpu.SMEM((experts,), jnp.int32),
            pltpu.SMEM((rows,), jnp.int32),
            pltpu.SemaphoreType.DMA((4,)),
        ],
        compiler_params=pltpu.CompilerParams(vmem_limit_bytes=8 * 1024 * 1024),
        name="dispatch",
    )(*[in_hbm(v) for v in arrays])


def pick_kernel(which_ref, wg, wu, wd, og, ou, od, sem):
    which = which_ref[0]
    run_copies(
        [
            pltpu.make_async_copy(w.at[which], o, sem.at[i])
            for i, (w, o) in enumerate(((wg, og), (wu, ou), (wd, od)))
        ]
    )


def pick(which, w_gate, w_up, w_down):
    return pl.pallas_call(
        pick_kernel,
        out_shape=[pltpu.VMEM(w.shape[1:], BF16) for w in (w_gate, w_up, w_down)],
        in_specs=[pl.BlockSpec(memory_space=pltpu.SMEM)] + [ANYWHERE] * 3,
        out_specs=[IN_VMEM] * 3,
        scratch_shapes=[pltpu.SemaphoreType.DMA((3,))],
        compiler_params=pltpu.CompilerParams(vmem_limit_bytes=1024 * 1024),
        name="pick",
    )(which, in_hbm(w_gate), in_hbm(w_up), in_hbm(w_down))


def load_kernel(core_ref, wg, wpg, wu, wpu, wd, wpd, w1, w2, sem):
    core = core_ref[0]
    part = wpd.shape[0]
    run_copies(
        [
            pltpu.make_async_copy(wg.at[core], w1.at[pl.ds(0, part)], sem.at[0]),
            pltpu.make_async_copy(wpg, w1.at[pl.ds(part, part)], sem.at[1]),
            pltpu.make_async_copy(wu.at[core], w1.at[pl.ds(2 * part, part)], sem.at[2]),
            pltpu.make_async_copy(wpu, w1.at[pl.ds(3 * part, part)], sem.at[3]),
            pltpu.make_async_copy(wd.at[core], w2.at[pl.ds(0, part)], sem.at[4]),
            pltpu.make_async_copy(wpd, w2.at[pl.ds(part, part)], sem.at[5]),
        ]
    )


def load(core, *weights):
    part, width = weights[-1].shape
    return pl.pallas_call(
        load_kernel,
        out_shape=[
            pltpu.VMEM((2 * CORES * part, width), BF16),
            pltpu.VMEM((CORES * part, width), BF16),
        ],
        in_specs=[pl.BlockSpec(memory_space=pltpu.SMEM)] + [ANYWHERE] * 6,
        out_specs=[IN_VMEM] * 2,
        scratch_shapes=[pltpu.SemaphoreType.DMA((6,))],
        compiler_params=pltpu.CompilerParams(vmem_limit_bytes=1024 * 1024),
        name="load",
    )(core, *[in_hbm(w) if w.ndim == 3 else in_vmem(w) for w in weights])


def ffn_kernel(rows, looped, *refs):
    n = len(rows)
    xs, (w1, w2), outs = refs[:n], refs[n : n + 2], refs[n + 2 : 2 * n + 2]
    x, gu, h = refs[2 * n + 2 :]
    width = w1.shape[1]
    hidden = w2.shape[0]
    starts = [sum(rows[:i]) for i in range(n)]
    for i in range(n):
        x[starts[i] : starts[i] + rows[i], :] = xs[i][...]

    def gate_and_up(at):
        gu[:, at] = lax.dot_general(
            x[...], w1[at, :], (((1,), (1,)), ((), ())), preferred_element_type=F32
        )

    if looped:

        @pl.loop(0, 2 * hidden // CHUNK)
        def _(j):
            gate_and_up(pl.ds(pl.multiple_of(j * CHUNK, CHUNK), CHUNK))

    else:
        for j in range(2 * hidden // CHUNK):
            gate_and_up(slice(j * CHUNK, (j + 1) * CHUNK))

    gate = gu[:, :hidden]
    h[...] = (gate / (1.0 + jnp.exp(-gate)) * gu[:, hidden:]).astype(BF16)

    @pl.loop(0, width // WIDE)
    def _(j):
        cols = pl.ds(pl.multiple_of(j * WIDE, WIDE), WIDE)
        y = jnp.dot(h[...], w2[:, cols], preferred_element_type=F32).astype(BF16)
        for i in range(n):
            outs[i][:, cols] = y[starts[i] : starts[i] + rows[i]]


def ffn(xs, w1, w2, looped=False):
    rows = tuple(v.shape[0] for v in xs)
    total = sum(rows)
    hidden, width = w2.shape
    n = len(xs)
    return pl.pallas_call(
        functools.partial(ffn_kernel, rows, looped),
        out_shape=[pltpu.VMEM(v.shape, BF16) for v in xs],
        in_specs=[IN_VMEM] * (n + 2),
        out_specs=[IN_VMEM] * n,
        scratch_shapes=[
            pltpu.VMEM((total, width), BF16),
            pltpu.VMEM((total, 2 * hidden), F32),
            pltpu.VMEM((total, hidden), BF16),
        ],
        compiler_params=pltpu.CompilerParams(vmem_limit_bytes=10 * 1024 * 1024),
        cost_estimate=pl.CostEstimate(
            flops=6 * total * width * hidden, transcendentals=total * hidden, bytes_accessed=0
        ),
        name="ffn",
    )(*[in_vmem(v) for v in xs], in_vmem(w1), in_vmem(w2))


def ring_gather(v, axis):
    half = v.shape[0] // 2
    plus, minus = shift(v, axis, 1), shift(v, axis, -1)
    plus2, minus2 = shift(plus[:half], axis, 1), shift(minus[half:], axis, -1)
    return jnp.concatenate([v, plus, minus, plus2, minus2], axis=0)


def add(*terms):
    total = terms[0].astype(F32)
    for term in terms[1:]:
        total = total + term.astype(F32)
    return total.astype(BF16)


def ring_scatter(v, axis):
    unit = v.shape[0] // RING
    half = unit // 2
    own, plus, minus = v[:unit], v[unit : 2 * unit], v[2 * unit : 3 * unit]
    plus2, minus2 = v[3 * unit : 3 * unit + half], v[3 * unit + half :]
    from_next, from_last = shift(plus2, axis, -1), shift(minus2, axis, 1)
    plus = jnp.concatenate([add(plus[:half], from_next), plus[half:]], axis=0)
    minus = jnp.concatenate([minus[:half], add(minus[half:], from_last)], axis=0)
    return add(own, shift(plus, axis, -1), shift(minus, axis, 1))


def first_halves(v, axis):
    half = v.shape[0] // 2
    return [shift(v[:half], axis, 1), shift(v[half:], axis, -1)]


def second_halves(v, axis):
    half = v.shape[0] // 2
    return [shift(v[half:], axis, 1), shift(v[:half], axis, -1)]


def onward(pair, axis):
    return [shift(pair[0], axis, 1), shift(pair[1], axis, -1)]


def backward(pair, axis):
    return [shift(pair[0], axis, -1), shift(pair[1], axis, 1)]


def after(*lists):
    flat = lax.optimization_barrier([v for part in lists for v in part])
    cut, out = 0, []
    for part in lists:
        out.append(flat[cut : cut + len(part)])
        cut += len(part)
    return out


def collect(own, early, late):
    half = own.shape[0] // 2
    return jnp.concatenate(
        [add(own[:half], early[1], late[0]), add(own[half:], early[0], late[1])], axis=0
    )


def layer(tokens, gain, task_ids, order, w_gate, w_up, w_down):
    local_experts = w_gate.shape[0]
    expert_count = RING * local_experts
    core = lax.axis_index("core")

    core_arg = core.astype(jnp.int32).reshape(1)
    outgoing, selecting = dispatch(task_ids, order, tokens, gain, expert_count)
    slot_count = expert_count * CAP
    per_core = slot_count // CORES
    kept, swapped = outgoing[:per_core], swap_cores(outgoing[per_core:])

    w_gate = jnp.swapaxes(w_gate, 1, 2)
    w_up = jnp.swapaxes(w_up, 1, 2)
    swapped, which = lax.optimization_barrier((swapped, 1 - core_arg))
    sent = pick(which, w_gate, w_up, w_down)
    peers = [swap_cores(w) for w in sent]

    def for_group(k):
        at = slice(k * CAP, (k + 1) * CAP)
        return jnp.concatenate([kept[at], swapped[at]], axis=0)

    groups = [for_group(0)] + [shift(for_group(k), "task", k) for k in range(1, RING)]
    a0 = ring_gather(jnp.concatenate(groups[:2], axis=0), "x")
    b0 = ring_gather(jnp.concatenate(groups[2:], axis=0), "z")
    lead_a, lead_b = first_halves(a0, "z"), first_halves(b0, "x")
    rest_a, rest_b = second_halves(a0, "z"), second_halves(b0, "x")
    (a0, b0), peers = after([a0, b0], peers)
    w1, w2 = load(core_arg, w_gate, peers[0], w_up, peers[1], w_down, peers[2])
    (w1, w2), lead_a, lead_b = after([w1, w2], lead_a, lead_b)
    far_a, far_b = onward(lead_a, "z"), onward(lead_b, "x")
    early = ffn(rest_a + rest_b, w1, w2)
    early_a, early_b = backward(early[:2], "z"), backward(early[2:], "x")
    far = ffn(far_a + far_b, w1, w2)
    far, lead_a, lead_b = after(far, lead_a, lead_b)
    far_a, far_b = backward(far[:2], "z"), backward(far[2:], "x")
    late = ffn(lead_a + lead_b, w1, w2)
    far_a, late_a = after(far_a, late[:2])
    far_b, late_b, (a0, b0) = after(far_b, late[2:], [a0, b0])
    late_a = backward([add(v, w) for v, w in zip(late_a, far_a)], "z")
    late_b = backward([add(v, w) for v, w in zip(late_b, far_b)], "x")
    y0 = ffn([a0, b0], w1, w2, looped=True)
    ya = collect(y0[0], early_a, late_a)
    yb = collect(y0[1], early_b, late_b)
    done_a = ring_scatter(ya, "x")
    done_b = ring_scatter(yb, "z")

    both = 2 * CAP
    groups = [done_a[:both], done_a[both:], done_b[:both], done_b[both:]]
    groups = [groups[0]] + [shift(groups[k], "task", -k) for k in range(1, RING)]
    kept = jnp.concatenate([v[:CAP] for v in groups], axis=0)
    swapped = swap_cores(jnp.concatenate([v[CAP:] for v in groups], axis=0))
    returned = jnp.concatenate([kept, swapped], axis=0)
    return jnp.dot(selecting, returned, preferred_element_type=F32).astype(BF16)


def solution(mesh):
    devices = mesh.devices.reshape(RING, RING, RING, CORES)
    fine = Mesh(devices, ("task", "x", "z", "core"))
    shard = ("x", "z", "core")
    every = ("task",) + shard
    placed = (
        P(every, None),
        P(),
        P(every),
        P(every),
        P("task", None, shard),
        P("task", None, shard),
        P("task", shard, None),
    )
    return jax.shard_map(
        layer, mesh=fine, in_specs=placed, out_specs=P(every, None), check_vma=False
    )
```

profile of v0, /device:TPU:0, one launch (start us, length us, event | category | flops | bytes accessed | tf_op | source)
XLA Modules:
  0.0 190.0 jit_solution(3686921993266038509)
XLA Ops:
  4.9 3.0 %collective-permute-start.6 = (bf16[16,4096]{1,0:T(8,128)(2,1)S(1)}, bf16[16,4096]{1,0:T(8,128)(2,1)S(1)}, u32[]{:S(2)}, u32[]{:S(2)}) collective-permute-start(bf16[16,4096]{1,0:T(8,128)(2,1)S(1)} %pad_maximum_fusion.8), channel_id=1, source_target_pairs={{0,64},{32,96},{64,0},{96,32},{1,65},{33,97},{65,1},{97,33},{2,66}... | collective-permute-start | bytes 393224 | tf_op jit(solution)/shard_map/ppermute | solution.py:18
  9.3 4.2 %pick.1 = (bf16[448,4096]{1,0:T(8,128)(2,1)S(1)}, bf16[448,4096]{1,0:T(8,128)(2,1)S(1)}, bf16[448,4096]{1,0:T(8,128)(2,1)S(1)}) custom-call(s32[1]{0:T(128)S(6)} %sub.3.which_ref, bf16[2,448,4096]{2,1,0:T(8,128)(2,1)} %bitcast.6, bf16[2,448,4096]{2,1,0:T(8,128)(2,1)} %bitcast.8, bf16[2,448,4096]{2,1,0:T(8,128)(2,1)} %wd.3), custom_call_target="tpu_custom_call" | custom-call | tf_op jit(solution)/shard_map/pick/pallas_call | solution.py:126
  14.3 2.8 %collective-permute-start.3 = (bf16[32,4096]{1,0:T(8,128)(2,1)S(1)}, bf16[32,4096]{1,0:T(8,128)(2,1)S(1)}, u32[]{:S(2)}, u32[]{:S(2)}) collective-permute-start(bf16[32,4096]{1,0:T(8,128)(2,1)S(1)} %pad_maximum_fusion.1), channel_id=1, source_target_pairs={{0,24},{8,0},{16,8},{24,16},{1,25},{9,1},{17,9},{25,17},{2,26},{10... | collective-permute-start | bytes 786440 | tf_op jit(solution)/shard_map/ppermute | solution.py:18
  17.3 9.5 %collective-permute-done.2 = bf16[32,4096]{1,0:T(8,128)(2,1)S(1)} collective-permute-done((bf16[32,4096]{1,0:T(8,128)(2,1)S(1)}, bf16[32,4096]{1,0:T(8,128)(2,1)S(1)}, u32[]{:S(2)}, u32[]{:S(2)}) %collective-permute-start.2) | collective-permute-done | bytes 262176 | tf_op jit(solution)/shard_map/ppermute | solution.py:18
  26.8 4.0 %collective-permute-start.9 = (bf16[32,4096]{1,0:T(8,128)(2,1)S(1)}, bf16[32,4096]{1,0:T(8,128)(2,1)S(1)}, u32[]{:S(2)}, u32[]{:S(2)}) collective-permute-start(bf16[32,4096]{1,0:T(8,128)(2,1)S(1)} %get-tuple-element.151), channel_id=1, source_target_pairs={{0,6},{2,0},{4,2},{6,4},{1,7},{3,1},{5,3},{7,5},{8,14},{10,8},{12,... | collective-permute-start | bytes 786440 | tf_op jit(solution)/shard_map/ppermute | solution.py:18
  31.1 8.3 %collective-permute-done.8 = bf16[32,4096]{1,0:T(8,128)(2,1)S(1)} collective-permute-done((bf16[32,4096]{1,0:T(8,128)(2,1)S(1)}, bf16[32,4096]{1,0:T(8,128)(2,1)S(1)}, u32[]{:S(2)}, u32[]{:S(2)}) %collective-permute-start.8) | collective-permute-done | bytes 262176 | tf_op jit(solution)/shard_map/ppermute | solution.py:18
  39.4 3.3 %collective-permute-start.5 = (bf16[16,4096]{1,0:T(8,128)(2,1)S(1)}, bf16[16,4096]{1,0:T(8,128)(2,1)S(1)}, u32[]{:S(2)}, u32[]{:S(2)}) collective-permute-start(bf16[16,4096]{1,0:T(8,128)(2,1)S(1)} %slice.201), channel_id=1, source_target_pairs={{0,24},{8,0},{16,8},{24,16},{1,25},{9,1},{17,9},{25,17},{2,26},{10... | collective-permute-start | bytes 393224 | tf_op jit(solution)/shard_map/ppermute | solution.py:18
  42.8 2.7 %collective-permute-done.4 = bf16[16,4096]{1,0:T(8,128)(2,1)S(1)} collective-permute-done((bf16[16,4096]{1,0:T(8,128)(2,1)S(1)}, bf16[16,4096]{1,0:T(8,128)(2,1)S(1)}, u32[]{:S(2)}, u32[]{:S(2)}) %collective-permute-start.4) | collective-permute-done | bytes 131104 | tf_op jit(solution)/shard_map/ppermute | solution.py:18
  45.6 7.5 %collective-permute-done.10 = bf16[16,4096]{1,0:T(8,128)(2,1)S(1)} collective-permute-done((bf16[16,4096]{1,0:T(8,128)(2,1)S(1)}, bf16[16,4096]{1,0:T(8,128)(2,1)S(1)}, u32[]{:S(2)}, u32[]{:S(2)}) %collective-permute-start.10) | collective-permute-done | bytes 131104 | tf_op jit(solution)/shard_map/ppermute | solution.py:18
  53.1 4.9 %collective-permute-done.11 = bf16[16,4096]{1,0:T(8,128)(2,1)S(1)} collective-permute-done((bf16[16,4096]{1,0:T(8,128)(2,1)S(1)}, bf16[16,4096]{1,0:T(8,128)(2,1)S(1)}, u32[]{:S(2)}, u32[]{:S(2)}) %collective-permute-start.11) | collective-permute-done | bytes 131104 | tf_op jit(solution)/shard_map/ppermute | solution.py:18
  58.1 2.3 %collective-permute-done.15.refs_0_ = bf16[64,4096]{1,0:T(8,128)(2,1)S(1)} collective-permute-done((bf16[64,4096]{1,0:T(8,128)(2,1)S(1)}, bf16[64,4096]{1,0:T(8,128)(2,1)S(1)}, u32[]{:S(2)}, u32[]{:S(2)}) %collective-permute-start.15) | collective-permute-done | bytes 524320 | tf_op jit(solution)/shard_map/ppermute | solution.py:18
  60.8 7.7 %collective-permute-done.17.refs_2_ = bf16[64,4096]{1,0:T(8,128)(2,1)S(1)} collective-permute-done((bf16[64,4096]{1,0:T(8,128)(2,1)S(1)}, bf16[64,4096]{1,0:T(8,128)(2,1)S(1)}, u32[]{:S(2)}, u32[]{:S(2)}) %collective-permute-start.17) | collective-permute-done | bytes 524320 | tf_op jit(solution)/shard_map/ppermute | solution.py:18
  68.5 3.9 %collective-permute-done.16.refs_1_ = bf16[64,4096]{1,0:T(8,128)(2,1)S(1)} collective-permute-done((bf16[64,4096]{1,0:T(8,128)(2,1)S(1)}, bf16[64,4096]{1,0:T(8,128)(2,1)S(1)}, u32[]{:S(2)}, u32[]{:S(2)}) %collective-permute-start.16) | collective-permute-done | bytes 524320 | tf_op jit(solution)/shard_map/ppermute | solution.py:18
  76.4 4.4 %load.1 = (bf16[1792,4096]{1,0:T(8,128)(2,1)S(1)}, bf16[896,4096]{1,0:T(8,128)(2,1)S(1)}) custom-call(s32[1]{0:T(128)} %bitcast.1.core_ref, bf16[2,448,4096]{2,1,0:T(8,128)(2,1)} %bitcast.7, bf16[448,4096]{1,0:T(8,128)(2,1)S(1)} %collective-permute-done.12.wpg, bf16[2,448,4096]{2,1,0:T(8,128)(2,1)} %bitcast.9, ...), custom_call_target="tpu_custom_call" | custom-call | tf_op jit(solution)/shard_map/load/pallas_call | solution.py:154
  86.2 5.6 %collective-permute-done.28.refs_3_ = bf16[64,4096]{1,0:T(8,128)(2,1)S(1)} collective-permute-done((bf16[64,4096]{1,0:T(8,128)(2,1)S(1)}, bf16[64,4096]{1,0:T(8,128)(2,1)S(1)}, u32[]{:S(2)}, u32[]{:S(2)}) %collective-permute-start.28) | collective-permute-done | bytes 524320 | tf_op jit(solution)/shard_map/ppermute | solution.py:18
  91.8 3.2 %collective-permute-start.22 = (bf16[64,4096]{1,0:T(8,128)(2,1)S(1)}, bf16[64,4096]{1,0:T(8,128)(2,1)S(1)}, u32[]{:S(2)}, u32[]{:S(2)}) collective-permute-start(bf16[64,4096]{1,0:T(8,128)(2,1)S(1)} %collective-permute-done.18.refs_3_), channel_id=1, source_target_pairs={{0,24},{8,0},{16,8},{24,16},{1,25},{9,1},{17,9},{25,17},{2,26},{10... | collective-permute-start | bytes 1572872 | tf_op jit(solution)/shard_map/ppermute | solution.py:18
  95.0 6.8 %ffn.7 = (bf16[64,4096]{1,0:T(8,128)(2,1)S(1)}, bf16[64,4096]{1,0:T(8,128)(2,1)S(1)}, bf16[64,4096]{1,0:T(8,128)(2,1)S(1)}, bf16[64,4096]{1,0:T(8,128)(2,1)S(1)}) custom-call(bf16[64,4096]{1,0:T(8,128)(2,1)S(1)} %collective-permute-done.25.refs_0_, bf16[64,4096]{1,0:T(8,128)(2,1)S(1)} %collective-permute-done.26.refs_1_, ...), custom_call_target="tpu_custom_call" | custom-call | flops 5637144576 | tf_op jit(solution)/shard_map/ffn/pallas_call | solution.py:209
  102.0 3.2 %collective-permute-start.42 = (bf16[64,4096]{1,0:T(8,128)(2,1)S(1)}, bf16[64,4096]{1,0:T(8,128)(2,1)S(1)}, u32[]{:S(2)}, u32[]{:S(2)}) collective-permute-start(bf16[64,4096]{1,0:T(8,128)(2,1)S(1)} %get-tuple-element.106), channel_id=1, source_target_pairs={{0,24},{8,0},{16,8},{24,16},{1,25},{9,1},{17,9},{25,17},{2,26},{10... | collective-permute-start | bytes 1572872 | tf_op jit(solution)/shard_map/ppermute | solution.py:18
  107.8 6.9 %ffn.4 = (bf16[64,4096]{1,0:T(8,128)(2,1)S(1)}, bf16[64,4096]{1,0:T(8,128)(2,1)S(1)}, bf16[64,4096]{1,0:T(8,128)(2,1)S(1)}, bf16[64,4096]{1,0:T(8,128)(2,1)S(1)}) custom-call(bf16[64,4096]{1,0:T(8,128)(2,1)S(1)} %collective-permute-done.19.refs_0_, bf16[64,4096]{1,0:T(8,128)(2,1)S(1)} %collective-permute-done.20.refs_1_, ...), custom_call_target="tpu_custom_call" | custom-call | flops 5637144576 | tf_op jit(solution)/shard_map/ffn/pallas_call | solution.py:209
  114.7 3.3 %collective-permute-start.23 = (bf16[64,4096]{1,0:T(8,128)(2,1)S(1)}, bf16[64,4096]{1,0:T(8,128)(2,1)S(1)}, u32[]{:S(2)}, u32[]{:S(2)}) collective-permute-start(bf16[64,4096]{1,0:T(8,128)(2,1)S(1)} %get-tuple-element.79), channel_id=1, source_target_pairs={{0,24},{8,0},{16,8},{24,16},{1,25},{9,1},{17,9},{25,17},{2,26},{10... | collective-permute-start | bytes 1572872 | tf_op jit(solution)/shard_map/ppermute | solution.py:18
  118.0 6.9 %ffn.5 = (bf16[64,4096]{1,0:T(8,128)(2,1)S(1)}, bf16[64,4096]{1,0:T(8,128)(2,1)S(1)}, bf16[64,4096]{1,0:T(8,128)(2,1)S(1)}, bf16[64,4096]{1,0:T(8,128)(2,1)S(1)}) custom-call(bf16[64,4096]{1,0:T(8,128)(2,1)S(1)} %collective-permute-done.15.refs_0_, bf16[64,4096]{1,0:T(8,128)(2,1)S(1)} %collective-permute-done.16.refs_1_, ...), custom_call_target="tpu_custom_call" | custom-call | flops 5637144576 | tf_op jit(solution)/shard_map/ffn/pallas_call | solution.py:209
  125.9 2.5 %collective-permute-done.24 = bf16[64,4096]{1,0:T(8,128)(2,1)S(1)} collective-permute-done((bf16[64,4096]{1,0:T(8,128)(2,1)S(1)}, bf16[64,4096]{1,0:T(8,128)(2,1)S(1)}, u32[]{:S(2)}, u32[]{:S(2)}) %collective-permute-start.24) | collective-permute-done | bytes 524320 | tf_op jit(solution)/shard_map/ppermute | solution.py:18
  128.5 5.9 %collective-permute-done.30 = bf16[64,4096]{1,0:T(8,128)(2,1)S(1)} collective-permute-done((bf16[64,4096]{1,0:T(8,128)(2,1)S(1)}, bf16[64,4096]{1,0:T(8,128)(2,1)S(1)}, u32[]{:S(2)}, u32[]{:S(2)}) %collective-permute-start.30) | collective-permute-done | bytes 524320 | tf_op jit(solution)/shard_map/ppermute | solution.py:18
  134.4 10.0 %collective-permute-done.31 = bf16[64,4096]{1,0:T(8,128)(2,1)S(1)} collective-permute-done((bf16[64,4096]{1,0:T(8,128)(2,1)S(1)}, bf16[64,4096]{1,0:T(8,128)(2,1)S(1)}, u32[]{:S(2)}, u32[]{:S(2)}) %collective-permute-start.31) | collective-permute-done | bytes 524320 | tf_op jit(solution)/shard_map/ppermute | solution.py:18
  146.9 3.2 %collective-permute-start.32 = (bf16[64,4096]{1,0:T(8,128)(2,1)S(1)}, bf16[64,4096]{1,0:T(8,128)(2,1)S(1)}, u32[]{:S(2)}, u32[]{:S(2)}) collective-permute-start(bf16[64,4096]{1,0:T(8,128)(2,1)S(1)} %add_convert_fusion.7), channel_id=1, source_target_pairs={{0,6},{2,0},{4,2},{6,4},{1,7},{3,1},{5,3},{7,5},{8,14},{10,8},{12,... | collective-permute-start | bytes 1572872 | tf_op jit(solution)/shard_map/ppermute | solution.py:18
  150.1 8.4 %ffn.6 = (bf16[128,4096]{1,0:T(8,128)(2,1)S(1)}, bf16[128,4096]{1,0:T(8,128)(2,1)S(1)}) custom-call(bf16[128,4096]{1,0:T(8,128)(2,1)S(1)} %get-tuple-element.89.refs_0_, bf16[128,4096]{1,0:T(8,128)(2,1)S(1)} %get-tuple-element.90.refs_1_, bf16[1792,4096]{1,0:T(8,128)(2,1)S(1)} %get-tuple-element.73.refs_4_.refs_2_, ...), custom_call_target="tpu_custom_call" | custom-call | flops 5637144576 | tf_op jit(solution)/shard_map/ffn/pallas_call | solution.py:209
  160.4 3.3 %collective-permute-start.44 = (bf16[16,4096]{1,0:T(8,128)(2,1)S(1)}, bf16[16,4096]{1,0:T(8,128)(2,1)S(1)}, u32[]{:S(2)}, u32[]{:S(2)}) collective-permute-start(bf16[16,4096]{1,0:T(8,128)(2,1)S(1)} %get-tuple-element.113), channel_id=1, source_target_pairs={{0,6},{2,0},{4,2},{6,4},{1,7},{3,1},{5,3},{7,5},{8,14},{10,8},{12,... | collective-permute-start | bytes 393224 | tf_op jit(solution)/shard_map/ppermute | solution.py:18
  163.8 3.4 %collective-permute-start.35 = (bf16[16,4096]{1,0:T(8,128)(2,1)S(1)}, bf16[16,4096]{1,0:T(8,128)(2,1)S(1)}, u32[]{:S(2)}, u32[]{:S(2)}) collective-permute-start(bf16[16,4096]{1,0:T(8,128)(2,1)S(1)} %get-tuple-element.116), channel_id=1, source_target_pairs={{0,24},{8,0},{16,8},{24,16},{1,25},{9,1},{17,9},{25,17},{2,26},{10... | collective-permute-start | bytes 393224 | tf_op jit(solution)/shard_map/ppermute | solution.py:18
  167.5 3.3 %collective-permute-start.45 = (bf16[32,4096]{1,0:T(8,128)(2,1)S(1)}, bf16[32,4096]{1,0:T(8,128)(2,1)S(1)}, u32[]{:S(2)}, u32[]{:S(2)}) collective-permute-start(bf16[32,4096]{1,0:T(8,128)(2,1)S(1)} %pad_maximum_fusion.4), channel_id=1, source_target_pairs={{0,6},{2,0},{4,2},{6,4},{1,7},{3,1},{5,3},{7,5},{8,14},{10,8},{12,... | collective-permute-start | bytes 786440 | tf_op jit(solution)/shard_map/ppermute | solution.py:18
  171.0 3.4 %collective-permute-start.36 = (bf16[32,4096]{1,0:T(8,128)(2,1)S(1)}, bf16[32,4096]{1,0:T(8,128)(2,1)S(1)}, u32[]{:S(2)}, u32[]{:S(2)}) collective-permute-start(bf16[32,4096]{1,0:T(8,128)(2,1)S(1)} %pad_maximum_fusion.2), channel_id=1, source_target_pairs={{0,24},{8,0},{16,8},{24,16},{1,25},{9,1},{17,9},{25,17},{2,26},{10... | collective-permute-start | bytes 786440 | tf_op jit(solution)/shard_map/ppermute | solution.py:18
  175.1 3.5 %collective-permute-done.38 = bf16[32,4096]{1,0:T(8,128)(2,1)S(1)} collective-permute-done((bf16[32,4096]{1,0:T(8,128)(2,1)S(1)}, bf16[32,4096]{1,0:T(8,128)(2,1)S(1)}, u32[]{:S(2)}, u32[]{:S(2)}) %collective-permute-start.38) | collective-permute-done | bytes 262176 | tf_op jit(solution)/shard_map/ppermute | solution.py:18
  183.8 3.6 %collective-permute-done.48 = bf16[16,4096]{1,0:T(8,128)(2,1)S(1)} collective-permute-done((bf16[16,4096]{1,0:T(8,128)(2,1)S(1)}, bf16[16,4096]{1,0:T(8,128)(2,1)S(1)}, u32[]{:S(2)}, u32[]{:S(2)}) %collective-permute-start.48) | collective-permute-done | bytes 131104 | tf_op jit(solution)/shard_map/ppermute | solution.py:18
  (128 shorter events, 34.3 us)
Async XLA Ops:
  3.1 11.0 %collective-permute-start.1 = (bf16[16,4096]{1,0:T(8,128)(2,1)S(1)}, bf16[16,4096]{1,0:T(8,128)(2,1)S(1)}, u32[]{:S(2)}, u32[]{:S(2)}) collective-permute-start(bf16[16,4096]{1,0:T(8,128)(2,1)S(1)} %pad_maximum_fusion.7), channel_id=1, source_target_pairs={{0,32},{32,64},{64,96},{96,0},{1,33},{33,65},{65,97},{97,1},{2,34}... | collective-permute-start | bytes 393224 | tf_op jit(solution)/shard_map/ppermute | solution.py:18
  4.9 9.4 %collective-permute-start.6 = (bf16[16,4096]{1,0:T(8,128)(2,1)S(1)}, bf16[16,4096]{1,0:T(8,128)(2,1)S(1)}, u32[]{:S(2)}, u32[]{:S(2)}) collective-permute-start(bf16[16,4096]{1,0:T(8,128)(2,1)S(1)} %pad_maximum_fusion.8), channel_id=1, source_target_pairs={{0,64},{32,96},{64,0},{96,32},{1,65},{33,97},{65,1},{97,33},{2,66}... | collective-permute-start | bytes 393224 | tf_op jit(solution)/shard_map/ppermute | solution.py:18
  13.6 59.5 %collective-permute-start.12 = (bf16[448,4096]{1,0:T(8,128)(2,1)S(1)}, bf16[448,4096]{1,0:T(8,128)(2,1)S(1)}, u32[]{:S(2)}, u32[]{:S(2)}) collective-permute-start(bf16[448,4096]{1,0:T(8,128)(2,1)S(1)} %get-tuple-element.61), channel_id=1, source_target_pairs={{0,1},{1,0},{2,3},{3,2},{4,5},{5,4},{6,7},{7,6},{8,9},{9,8},{10,11... | collective-permute-start | bytes 11010056 | tf_op jit(solution)/shard_map/ppermute | solution.py:22
  13.7 61.0 %collective-permute-start.13 = (bf16[448,4096]{1,0:T(8,128)(2,1)S(1)}, bf16[448,4096]{1,0:T(8,128)(2,1)S(1)}, u32[]{:S(2)}, u32[]{:S(2)}) collective-permute-start(bf16[448,4096]{1,0:T(8,128)(2,1)S(1)} %get-tuple-element.62), channel_id=1, source_target_pairs={{0,1},{1,0},{2,3},{3,2},{4,5},{5,4},{6,7},{7,6},{8,9},{9,8},{10,11... | collective-permute-start | bytes 11010056 | tf_op jit(solution)/shard_map/ppermute | solution.py:22
  14.2 62.0 %collective-permute-start.14 = (bf16[448,4096]{1,0:T(8,128)(2,1)S(1)}, bf16[448,4096]{1,0:T(8,128)(2,1)S(1)}, u32[]{:S(2)}, u32[]{:S(2)}) collective-permute-start(bf16[448,4096]{1,0:T(8,128)(2,1)S(1)} %get-tuple-element.63), channel_id=1, source_target_pairs={{0,1},{1,0},{2,3},{3,2},{4,5},{5,4},{6,7},{7,6},{8,9},{9,8},{10,11... | collective-permute-start | bytes 11010056 | tf_op jit(solution)/shard_map/ppermute | solution.py:22
  14.3 16.6 %collective-permute-start.3 = (bf16[32,4096]{1,0:T(8,128)(2,1)S(1)}, bf16[32,4096]{1,0:T(8,128)(2,1)S(1)}, u32[]{:S(2)}, u32[]{:S(2)}) collective-permute-start(bf16[32,4096]{1,0:T(8,128)(2,1)S(1)} %pad_maximum_fusion.1), channel_id=1, source_target_pairs={{0,24},{8,0},{16,8},{24,16},{1,25},{9,1},{17,9},{25,17},{2,26},{10... | collective-permute-start | bytes 786440 | tf_op jit(solution)/shard_map/ppermute | solution.py:18
  17.2 9.6 %collective-permute-start.2 = (bf16[32,4096]{1,0:T(8,128)(2,1)S(1)}, bf16[32,4096]{1,0:T(8,128)(2,1)S(1)}, u32[]{:S(2)}, u32[]{:S(2)}) collective-permute-start(bf16[32,4096]{1,0:T(8,128)(2,1)S(1)} %pad_maximum_fusion.1), channel_id=1, source_target_pairs={{0,8},{8,16},{16,24},{24,0},{1,9},{9,17},{17,25},{25,1},{2,10},{10... | collective-permute-start | bytes 786440 | tf_op jit(solution)/shard_map/ppermute | solution.py:18
  26.8 12.6 %collective-permute-start.9 = (bf16[32,4096]{1,0:T(8,128)(2,1)S(1)}, bf16[32,4096]{1,0:T(8,128)(2,1)S(1)}, u32[]{:S(2)}, u32[]{:S(2)}) collective-permute-start(bf16[32,4096]{1,0:T(8,128)(2,1)S(1)} %get-tuple-element.151), channel_id=1, source_target_pairs={{0,6},{2,0},{4,2},{6,4},{1,7},{3,1},{5,3},{7,5},{8,14},{10,8},{12,... | collective-permute-start | bytes 786440 | tf_op jit(solution)/shard_map/ppermute | solution.py:18
  45.5 14.8 %collective-permute-start.15 = (bf16[64,4096]{1,0:T(8,128)(2,1)S(1)}, bf16[64,4096]{1,0:T(8,128)(2,1)S(1)}, u32[]{:S(2)}, u32[]{:S(2)}) collective-permute-start(bf16[64,4096]{1,0:T(8,128)(2,1)S(1)} %pad_maximum_fusion), channel_id=1, source_target_pairs={{0,2},{2,4},{4,6},{6,0},{1,3},{3,5},{5,7},{7,1},{8,10},{10,12},{12... | collective-permute-start | bytes 1572872 | tf_op jit(solution)/shard_map/ppermute | solution.py:18
  58.1 10.4 %collective-permute-start.17 = (bf16[64,4096]{1,0:T(8,128)(2,1)S(1)}, bf16[64,4096]{1,0:T(8,128)(2,1)S(1)}, u32[]{:S(2)}, u32[]{:S(2)}) collective-permute-start(bf16[64,4096]{1,0:T(8,128)(2,1)S(1)} %get-tuple-element.130), channel_id=1, source_target_pairs={{0,8},{8,16},{16,24},{24,0},{1,9},{9,17},{17,25},{25,1},{2,10},{10... | collective-permute-start | bytes 1572872 | tf_op jit(solution)/shard_map/ppermute | solution.py:18
  60.4 12.0 %collective-permute-start.16 = (bf16[64,4096]{1,0:T(8,128)(2,1)S(1)}, bf16[64,4096]{1,0:T(8,128)(2,1)S(1)}, u32[]{:S(2)}, u32[]{:S(2)}) collective-permute-start(bf16[64,4096]{1,0:T(8,128)(2,1)S(1)} %get-tuple-element.155), channel_id=1, source_target_pairs={{0,6},{2,0},{4,2},{6,4},{1,7},{3,1},{5,3},{7,5},{8,14},{10,8},{12,... | collective-permute-start | bytes 1572872 | tf_op jit(solution)/shard_map/ppermute | solution.py:18
  68.5 14.5 %collective-permute-start.18 = (bf16[64,4096]{1,0:T(8,128)(2,1)S(1)}, bf16[64,4096]{1,0:T(8,128)(2,1)S(1)}, u32[]{:S(2)}, u32[]{:S(2)}) collective-permute-start(bf16[64,4096]{1,0:T(8,128)(2,1)S(1)} %get-tuple-element.145), channel_id=1, source_target_pairs={{0,24},{8,0},{16,8},{24,16},{1,25},{9,1},{17,9},{25,17},{2,26},{10... | collective-permute-start | bytes 1572872 | tf_op jit(solution)/shard_map/ppermute | solution.py:18
  72.4 11.9 %collective-permute-start.26 = (bf16[64,4096]{1,0:T(8,128)(2,1)S(1)}, bf16[64,4096]{1,0:T(8,128)(2,1)S(1)}, u32[]{:S(2)}, u32[]{:S(2)}) collective-permute-start(bf16[64,4096]{1,0:T(8,128)(2,1)S(1)} %pad_maximum_fusion), channel_id=1, source_target_pairs={{0,6},{2,0},{4,2},{6,4},{1,7},{3,1},{5,3},{7,5},{8,14},{10,8},{12,... | collective-permute-start | bytes 1572872 | tf_op jit(solution)/shard_map/ppermute | solution.py:18
  73.0 18.8 %collective-permute-start.28 = (bf16[64,4096]{1,0:T(8,128)(2,1)S(1)}, bf16[64,4096]{1,0:T(8,128)(2,1)S(1)}, u32[]{:S(2)}, u32[]{:S(2)}) collective-permute-start(bf16[64,4096]{1,0:T(8,128)(2,1)S(1)} %get-tuple-element.130), channel_id=1, source_target_pairs={{0,24},{8,0},{16,8},{24,16},{1,25},{9,1},{17,9},{25,17},{2,26},{10... | collective-permute-start | bytes 1572872 | tf_op jit(solution)/shard_map/ppermute | solution.py:18
  74.6 17.2 %collective-permute-start.25 = (bf16[64,4096]{1,0:T(8,128)(2,1)S(1)}, bf16[64,4096]{1,0:T(8,128)(2,1)S(1)}, u32[]{:S(2)}, u32[]{:S(2)}) collective-permute-start(bf16[64,4096]{1,0:T(8,128)(2,1)S(1)} %get-tuple-element.155), channel_id=1, source_target_pairs={{0,2},{2,4},{4,6},{6,0},{1,3},{3,5},{5,7},{7,1},{8,10},{10,12},{12... | collective-permute-start | bytes 1572872 | tf_op jit(solution)/shard_map/ppermute | solution.py:18
  76.2 18.9 %collective-permute-start.27 = (bf16[64,4096]{1,0:T(8,128)(2,1)S(1)}, bf16[64,4096]{1,0:T(8,128)(2,1)S(1)}, u32[]{:S(2)}, u32[]{:S(2)}) collective-permute-start(bf16[64,4096]{1,0:T(8,128)(2,1)S(1)} %get-tuple-element.145), channel_id=1, source_target_pairs={{0,8},{8,16},{16,24},{24,0},{1,9},{9,17},{17,25},{25,1},{2,10},{10... | collective-permute-start | bytes 1572872 | tf_op jit(solution)/shard_map/ppermute | solution.py:18
  83.0 19.0 %collective-permute-start.19 = (bf16[64,4096]{1,0:T(8,128)(2,1)S(1)}, bf16[64,4096]{1,0:T(8,128)(2,1)S(1)}, u32[]{:S(2)}, u32[]{:S(2)}) collective-permute-start(bf16[64,4096]{1,0:T(8,128)(2,1)S(1)} %collective-permute-done.15.refs_0_), channel_id=1, source_target_pairs={{0,2},{2,4},{4,6},{6,0},{1,3},{3,5},{5,7},{7,1},{8,10},{10,12},{12... | collective-permute-start | bytes 1572872 | tf_op jit(solution)/shard_map/ppermute | solution.py:18
  84.2 21.0 %collective-permute-start.20 = (bf16[64,4096]{1,0:T(8,128)(2,1)S(1)}, bf16[64,4096]{1,0:T(8,128)(2,1)S(1)}, u32[]{:S(2)}, u32[]{:S(2)}) collective-permute-start(bf16[64,4096]{1,0:T(8,128)(2,1)S(1)} %collective-permute-done.16.refs_1_), channel_id=1, source_target_pairs={{0,6},{2,0},{4,2},{6,4},{1,7},{3,1},{5,3},{7,5},{8,14},{10,8},{12,... | collective-permute-start | bytes 1572872 | tf_op jit(solution)/shard_map/ppermute | solution.py:18
  91.8 16.0 %collective-permute-start.21 = (bf16[64,4096]{1,0:T(8,128)(2,1)S(1)}, bf16[64,4096]{1,0:T(8,128)(2,1)S(1)}, u32[]{:S(2)}, u32[]{:S(2)}) collective-permute-start(bf16[64,4096]{1,0:T(8,128)(2,1)S(1)} %collective-permute-done.17.refs_2_), channel_id=1, source_target_pairs={{0,8},{8,16},{16,24},{24,0},{1,9},{9,17},{17,25},{25,1},{2,10},{10... | collective-permute-start | bytes 1572872 | tf_op jit(solution)/shard_map/ppermute | solution.py:18
  91.8 16.0 %collective-permute-start.22 = (bf16[64,4096]{1,0:T(8,128)(2,1)S(1)}, bf16[64,4096]{1,0:T(8,128)(2,1)S(1)}, u32[]{:S(2)}, u32[]{:S(2)}) collective-permute-start(bf16[64,4096]{1,0:T(8,128)(2,1)S(1)} %collective-permute-done.18.refs_3_), channel_id=1, source_target_pairs={{0,24},{8,0},{16,8},{24,16},{1,25},{9,1},{17,9},{25,17},{2,26},{10... | collective-permute-start | bytes 1572872 | tf_op jit(solution)/shard_map/ppermute | solution.py:18
  101.9 43.8 %collective-permute-start.40 = (bf16[64,4096]{1,0:T(8,128)(2,1)S(1)}, bf16[64,4096]{1,0:T(8,128)(2,1)S(1)}, u32[]{:S(2)}, u32[]{:S(2)}) collective-permute-start(bf16[64,4096]{1,0:T(8,128)(2,1)S(1)} %get-tuple-element.103), channel_id=1, source_target_pairs={{0,8},{8,16},{16,24},{24,0},{1,9},{9,17},{17,25},{25,1},{2,10},{10... | collective-permute-start | bytes 1572872 | tf_op jit(solution)/shard_map/ppermute | solution.py:18
  102.0 44.9 %collective-permute-start.42 = (bf16[64,4096]{1,0:T(8,128)(2,1)S(1)}, bf16[64,4096]{1,0:T(8,128)(2,1)S(1)}, u32[]{:S(2)}, u32[]{:S(2)}) collective-permute-start(bf16[64,4096]{1,0:T(8,128)(2,1)S(1)} %get-tuple-element.106), channel_id=1, source_target_pairs={{0,24},{8,0},{16,8},{24,16},{1,25},{9,1},{17,9},{25,17},{2,26},{10... | collective-permute-start | bytes 1572872 | tf_op jit(solution)/shard_map/ppermute | solution.py:18
  105.2 41.7 %collective-permute-start.33 = (bf16[64,4096]{1,0:T(8,128)(2,1)S(1)}, bf16[64,4096]{1,0:T(8,128)(2,1)S(1)}, u32[]{:S(2)}, u32[]{:S(2)}) collective-permute-start(bf16[64,4096]{1,0:T(8,128)(2,1)S(1)} %get-tuple-element.99), channel_id=1, source_target_pairs={{0,6},{2,0},{4,2},{6,4},{1,7},{3,1},{5,3},{7,5},{8,14},{10,8},{12,... | collective-permute-start | bytes 1572872 | tf_op jit(solution)/shard_map/ppermute | solution.py:18
  114.7 10.2 %collective-permute-start.23 = (bf16[64,4096]{1,0:T(8,128)(2,1)S(1)}, bf16[64,4096]{1,0:T(8,128)(2,1)S(1)}, u32[]{:S(2)}, u32[]{:S(2)}) collective-permute-start(bf16[64,4096]{1,0:T(8,128)(2,1)S(1)} %get-tuple-element.79), channel_id=1, source_target_pairs={{0,24},{8,0},{16,8},{24,16},{1,25},{9,1},{17,9},{25,17},{2,26},{10... | collective-permute-start | bytes 1572872 | tf_op jit(solution)/shard_map/ppermute | solution.py:18
  118.0 10.4 %collective-permute-start.24 = (bf16[64,4096]{1,0:T(8,128)(2,1)S(1)}, bf16[64,4096]{1,0:T(8,128)(2,1)S(1)}, u32[]{:S(2)}, u32[]{:S(2)}) collective-permute-start(bf16[64,4096]{1,0:T(8,128)(2,1)S(1)} %get-tuple-element.80), channel_id=1, source_target_pairs={{0,8},{8,16},{16,24},{24,0},{1,9},{9,17},{17,25},{25,1},{2,10},{10... | collective-permute-start | bytes 1572872 | tf_op jit(solution)/shard_map/ppermute | solution.py:18
  124.9 9.5 %collective-permute-start.30 = (bf16[64,4096]{1,0:T(8,128)(2,1)S(1)}, bf16[64,4096]{1,0:T(8,128)(2,1)S(1)}, u32[]{:S(2)}, u32[]{:S(2)}) collective-permute-start(bf16[64,4096]{1,0:T(8,128)(2,1)S(1)} %get-tuple-element.93), channel_id=1, source_target_pairs={{0,6},{2,0},{4,2},{6,4},{1,7},{3,1},{5,3},{7,5},{8,14},{10,8},{12,... | collective-permute-start | bytes 1572872 | tf_op jit(solution)/shard_map/ppermute | solution.py:18
  128.4 16.0 %collective-permute-start.31 = (bf16[64,4096]{1,0:T(8,128)(2,1)S(1)}, bf16[64,4096]{1,0:T(8,128)(2,1)S(1)}, u32[]{:S(2)}, u32[]{:S(2)}) collective-permute-start(bf16[64,4096]{1,0:T(8,128)(2,1)S(1)} %get-tuple-element.94), channel_id=1, source_target_pairs={{0,2},{2,4},{4,6},{6,0},{1,3},{3,5},{5,7},{7,1},{8,10},{10,12},{12... | collective-permute-start | bytes 1572872 | tf_op jit(solution)/shard_map/ppermute | solution.py:18
  134.4 24.1 %collective-permute-start.29 = (bf16[64,4096]{1,0:T(8,128)(2,1)S(1)}, bf16[64,4096]{1,0:T(8,128)(2,1)S(1)}, u32[]{:S(2)}, u32[]{:S(2)}) collective-permute-start(bf16[64,4096]{1,0:T(8,128)(2,1)S(1)} %get-tuple-element.92), channel_id=1, source_target_pairs={{0,2},{2,4},{4,6},{6,0},{1,3},{3,5},{5,7},{7,1},{8,10},{10,12},{12... | collective-permute-start | bytes 1572872 | tf_op jit(solution)/shard_map/ppermute | solution.py:18
  144.4 14.2 %collective-permute-start.41 = (bf16[64,4096]{1,0:T(8,128)(2,1)S(1)}, bf16[64,4096]{1,0:T(8,128)(2,1)S(1)}, u32[]{:S(2)}, u32[]{:S(2)}) collective-permute-start(bf16[64,4096]{1,0:T(8,128)(2,1)S(1)} %add_convert_fusion.3), channel_id=1, source_target_pairs={{0,24},{8,0},{16,8},{24,16},{1,25},{9,1},{17,9},{25,17},{2,26},{10... | collective-permute-start | bytes 1572872 | tf_op jit(solution)/shard_map/ppermute | solution.py:18
  145.7 12.8 %collective-permute-start.43 = (bf16[64,4096]{1,0:T(8,128)(2,1)S(1)}, bf16[64,4096]{1,0:T(8,128)(2,1)S(1)}, u32[]{:S(2)}, u32[]{:S(2)}) collective-permute-start(bf16[64,4096]{1,0:T(8,128)(2,1)S(1)} %add_convert_fusion.1), channel_id=1, source_target_pairs={{0,8},{8,16},{16,24},{24,0},{1,9},{9,17},{17,25},{25,1},{2,10},{10... | collective-permute-start | bytes 1572872 | tf_op jit(solution)/shard_map/ppermute | solution.py:18
  146.9 12.2 %collective-permute-start.34 = (bf16[64,4096]{1,0:T(8,128)(2,1)S(1)}, bf16[64,4096]{1,0:T(8,128)(2,1)S(1)}, u32[]{:S(2)}, u32[]{:S(2)}) collective-permute-start(bf16[64,4096]{1,0:T(8,128)(2,1)S(1)} %add_convert_fusion.5), channel_id=1, source_target_pairs={{0,2},{2,4},{4,6},{6,0},{1,3},{3,5},{5,7},{7,1},{8,10},{10,12},{12... | collective-permute-start | bytes 1572872 | tf_op jit(solution)/shard_map/ppermute | solution.py:18
  146.9 12.2 %collective-permute-start.32 = (bf16[64,4096]{1,0:T(8,128)(2,1)S(1)}, bf16[64,4096]{1,0:T(8,128)(2,1)S(1)}, u32[]{:S(2)}, u32[]{:S(2)}) collective-permute-start(bf16[64,4096]{1,0:T(8,128)(2,1)S(1)} %add_convert_fusion.7), channel_id=1, source_target_pairs={{0,6},{2,0},{4,2},{6,4},{1,7},{3,1},{5,3},{7,5},{8,14},{10,8},{12,... | collective-permute-start | bytes 1572872 | tf_op jit(solution)/shard_map/ppermute | solution.py:18
  (19 other events, 124.6 us)
where the time goes:
time: 191 us; the launch traced here: 190 us
  waiting for transfers between devices  88 us (46%)
  starting transfers between devices  58.8 us (31%)
  Pallas kernels  39 us (20%)
  other arithmetic  2.16 us (1%)
    ppermute x46, waiting for transfers between devices, shift(): return lax.ppermute(v, axis, [(i, (i + step) % RING) for i in range(RING)])  85 us
    ppermute x46, starting transfers between devices, shift(): return lax.ppermute(v, axis, [(i, (i + step) % RING) for i in range(RING)])  57.9 us
    pallas_call x4, Pallas kernels, ffn(): pl.pallas_call(functools.partial(ffn_kernel, rows, looped), out_shape=[pl...  29 us
    pallas_call x1, Pallas kernels, load(): pl.pallas_call(load_kernel, out_shape=[pltpu.VMEM((2 * CORES * part, widt...  4.38 us
    pallas_call x1, Pallas kernels, pick(): pl.pallas_call(pick_kernel, out_shape=[pltpu.VMEM(w.shape[1:], BF16) for...  4.23 us
  transfers between devices with their start and end apart: 51, of which 22 were waited for; matrix products, arithmetic and copies ran while one was open for 1% of the time, Pallas kernels for 20%

commit v1 on v0

--- a/solution.py
+++ b/solution.py
@@ -112,45 +112,23 @@
     )(*[in_hbm(v) for v in arrays])
 
 
-def pick_kernel(which_ref, wg, wu, wd, og, ou, od, sem):
-    which = which_ref[0]
-    run_copies(
-        [
-            pltpu.make_async_copy(w.at[which], o, sem.at[i])
-            for i, (w, o) in enumerate(((wg, og), (wu, ou), (wd, od)))
-        ]
-    )
-
-
-def pick(which, w_gate, w_up, w_down):
-    return pl.pallas_call(
-        pick_kernel,
-        out_shape=[pltpu.VMEM(w.shape[1:], BF16) for w in (w_gate, w_up, w_down)],
-        in_specs=[pl.BlockSpec(memory_space=pltpu.SMEM)] + [ANYWHERE] * 3,
-        out_specs=[IN_VMEM] * 3,
-        scratch_shapes=[pltpu.SemaphoreType.DMA((3,))],
-        compiler_params=pltpu.CompilerParams(vmem_limit_bytes=1024 * 1024),
-        name="pick",
-    )(which, in_hbm(w_gate), in_hbm(w_up), in_hbm(w_down))
-
-
 def load_kernel(core_ref, wg, wpg, wu, wpu, wd, wpd, w1, w2, sem):
     core = core_ref[0]
-    part = wpd.shape[0]
+    part = wpd.shape[1]
     run_copies(
         [
             pltpu.make_async_copy(wg.at[core], w1.at[pl.ds(0, part)], sem.at[0]),
-            pltpu.make_async_copy(wpg, w1.at[pl.ds(part, part)], sem.at[1]),
+            pltpu.make_async_copy(wpg.at[core], w1.at[pl.ds(part, part)], sem.at[1]),
             pltpu.make_async_copy(wu.at[core], w1.at[pl.ds(2 * part, part)], sem.at[2]),
-            pltpu.make_async_copy(wpu, w1.at[pl.ds(3 * part, part)], sem.at[3]),
+            pltpu.make_async_copy(wpu.at[core], w1.at[pl.ds(3 * part, part)], sem.at[3]),
             pltpu.make_async_copy(wd.at[core], w2.at[pl.ds(0, part)], sem.at[4]),
-            pltpu.make_async_copy(wpd, w2.at[pl.ds(part, part)], sem.at[5]),
+            pltpu.make_async_copy(wpd.at[core], w2.at[pl.ds(part, part)], sem.at[5]),
         ]
     )
 
 
 def load(core, *weights):
-    part, width = weights[-1].shape
+    part, width = weights[-1].shape[1:]
     return pl.pallas_call(
         load_kernel,
         out_shape=[
@@ -162,7 +140,7 @@
         scratch_shapes=[pltpu.SemaphoreType.DMA((6,))],
         compiler_params=pltpu.CompilerParams(vmem_limit_bytes=1024 * 1024),
         name="load",
-    )(core, *[in_hbm(w) if w.ndim == 3 else in_vmem(w) for w in weights])
+    )(core, *[w if i % 2 else in_hbm(w) for i, w in enumerate(weights)])
 
 
 def ffn_kernel(rows, looped, *refs):
@@ -246,7 +224,8 @@
     from_next, from_last = shift(plus2, axis, -1), shift(minus2, axis, 1)
     plus = jnp.concatenate([add(plus[:half], from_next), plus[half:]], axis=0)
     minus = jnp.concatenate([minus[:half], add(minus[half:], from_last)], axis=0)
-    return add(own, shift(plus, axis, -1), shift(minus, axis, 1))
+    from_next, from_last = shift(plus, axis, -1), shift(minus, axis, 1)
+    return add(own, from_next, from_last)
 
 
 def first_halves(v, axis):
@@ -296,8 +275,7 @@
 
     w_gate = jnp.swapaxes(w_gate, 1, 2)
     w_up = jnp.swapaxes(w_up, 1, 2)
-    swapped, which = lax.optimization_barrier((swapped, 1 - core_arg))
-    sent = pick(which, w_gate, w_up, w_down)
+    swapped, *sent = lax.optimization_barrier((swapped, w_gate, w_up, w_down))
     peers = [swap_cores(w) for w in sent]
 
     def for_group(k):
@@ -311,7 +289,6 @@
     rest_a, rest_b = second_halves(a0, "z"), second_halves(b0, "x")
     (a0, b0), peers = after([a0, b0], peers)
     w1, w2 = load(core_arg, w_gate, peers[0], w_up, peers[1], w_down, peers[2])
-    (w1, w2), lead_a, lead_b = after([w1, w2], lead_a, lead_b)
     far_a, far_b = onward(lead_a, "z"), onward(lead_b, "x")
     early = ffn(rest_a + rest_b, w1, w2)
     early_a, early_b = backward(early[:2], "z"), backward(early[2:], "x")
@@ -331,7 +308,9 @@
 
     both = 2 * CAP
     groups = [done_a[:both], done_a[both:], done_b[:both], done_b[both:]]
-    groups = [groups[0]] + [shift(groups[k], "task", -k) for k in range(1, RING)]
+    first = shift(groups[1], "task", -1)
+    last = [shift(groups[k], "task", -k) for k in range(2, RING)]
+    groups = [groups[0], first] + last
     kept = jnp.concatenate([v[:CAP] for v in groups], axis=0)
     swapped = swap_cores(jnp.concatenate([v[CAP:] for v in groups], axis=0))
     returned = jnp.concatenate([kept, swapped], axis=0)

time: 191 us -> 183 us (0.958)
  waiting for transfers between devices: 88 us -> 57.2 us
  local copies, waits for them, and re-layouts: 0.54 us -> 12.7 us
  starting transfers between devices: 58.8 us -> 68.9 us
    ppermute x46, waiting for transfers between devices: 85 us -> 54.2 us  [shift(): return lax.ppermute(v, axis, [(i, (i + step) % RING) for i in range(RING)])]
    unnamed x8 -> x33, local copies, waits for them, and re-layouts: 0.19 us -> 12.4 us
    ppermute x46, starting transfers between devices: 57.9 us -> 68.2 us  [shift(): return lax.ppermute(v, axis, [(i, (i + step) % RING) for i in range(RING)])]
    pallas_call x1 -> x0, Pallas kernels: 4.23 us -> none  [pick(): pl.pallas_call(pick_kernel, out_shape=[pltpu.VMEM(w.shape[1:], BF16) for...]
    pallas_call x4, Pallas kernels: 29 us -> 31.9 us  [ffn(): pl.pallas_call(functools.partial(ffn_kernel, rows, looped), out_shape=[pl...]
  transfers between devices with their start and end apart: 51 -> 51, of which waited for: 22 -> 22; matrix products, arithmetic and copies ran while one was open for 1% -> 1% of each run, Pallas kernels for 20% -> 21%
where the time goes in v1:
time: 183 us; the launch traced here: 181 us
  starting transfers between devices  68.9 us (38%)
  waiting for transfers between devices  57.2 us (31%)
  Pallas kernels  38.9 us (21%)
  local copies, waits for them, and re-layouts  12.7 us (7%)
  other arithmetic  2.14 us (1%)
    ppermute x46, starting transfers between devices, shift(): return lax.ppermute(v, axis, [(i, (i + step) % RING) for i in range(RING)])  68.2 us
    ppermute x46, waiting for transfers between devices, shift(): return lax.ppermute(v, axis, [(i, (i + step) % RING) for i in range(RING)])  54.2 us
    pallas_call x4, Pallas kernels, ffn(): pl.pallas_call(functools.partial(ffn_kernel, rows, looped), out_shape=[pl...  31.9 us
    unnamed x33, local copies, waits for them, and re-layouts  12.4 us
    pallas_call x1, Pallas kernels, load(): pl.pallas_call(load_kernel, out_shape=[pltpu.VMEM((2 * CORES * part, widt...  5.51 us
  transfers between devices with their start and end apart: 51, of which 22 were waited for; matrix products, arithmetic and copies ran while one was open for 1% of the time, Pallas kernels for 21%

profile of v1, /device:TPU:0, one launch (start us, length us, event | category | flops | bytes accessed | tf_op | source)
XLA Modules:
  0.0 181.3 jit_solution(13385825905235353364)
XLA Ops:
  3.1 3.4 %collective-permute-start.10 = (bf16[16,4096]{1,0:T(8,128)(2,1)S(1)}, bf16[16,4096]{1,0:T(8,128)(2,1)S(1)}, u32[]{:S(2)}, u32[]{:S(2)}) collective-permute-start(bf16[16,4096]{1,0:T(8,128)(2,1)S(1)} %pad_maximum_fusion.8), channel_id=1, source_target_pairs={{0,64},{32,96},{64,0},{96,32},{1,65},{33,97},{65,1},{97,33},{2,66}... | collective-permute-start | bytes 393224 | tf_op jit(solution)/shard_map/ppermute | solution.py:18
  10.3 2.5 %collective-permute-start.1 = (bf16[16,4096]{1,0:T(8,128)(2,1)S(1)}, bf16[16,4096]{1,0:T(8,128)(2,1)S(1)}, u32[]{:S(2)}, u32[]{:S(2)}) collective-permute-start(bf16[16,4096]{1,0:T(8,128)(2,1)S(1)} %pad_maximum_fusion.7), channel_id=1, source_target_pairs={{0,32},{32,64},{64,96},{96,0},{1,33},{33,65},{65,97},{97,1},{2,34}... | collective-permute-start | bytes 393224 | tf_op jit(solution)/shard_map/ppermute | solution.py:18
  17.2 4.0 %collective-permute-start.15 = (bf16[32,4096]{1,0:T(8,128)(2,1)S(1)}, bf16[32,4096]{1,0:T(8,128)(2,1)S(1)}, u32[]{:S(2)}, u32[]{:S(2)}) collective-permute-start(bf16[32,4096]{1,0:T(8,128)(2,1)S(1)} %get-tuple-element.137), channel_id=1, source_target_pairs={{0,6},{2,0},{4,2},{6,4},{1,7},{3,1},{5,3},{7,5},{8,14},{10,8},{12,... | collective-permute-start | bytes 786440 | tf_op jit(solution)/shard_map/ppermute | solution.py:18
  25.1 2.8 %collective-permute-start.5 = (bf16[32,4096]{1,0:T(8,128)(2,1)S(1)}, bf16[32,4096]{1,0:T(8,128)(2,1)S(1)}, u32[]{:S(2)}, u32[]{:S(2)}) collective-permute-start(bf16[32,4096]{1,0:T(8,128)(2,1)S(1)} %pad_maximum_fusion.1), channel_id=1, source_target_pairs={{0,24},{8,0},{16,8},{24,16},{1,25},{9,1},{17,9},{25,17},{2,26},{10... | collective-permute-start | bytes 786440 | tf_op jit(solution)/shard_map/ppermute | solution.py:18
  28.0 3.6 %collective-permute-done.2 = bf16[32,4096]{1,0:T(8,128)(2,1)S(1)} collective-permute-done((bf16[32,4096]{1,0:T(8,128)(2,1)S(1)}, bf16[32,4096]{1,0:T(8,128)(2,1)S(1)}, u32[]{:S(2)}, u32[]{:S(2)}) %collective-permute-start.2) | collective-permute-done | bytes 262176 | tf_op jit(solution)/shard_map/ppermute | solution.py:18
  31.7 3.7 %collective-permute-start.17 = (bf16[16,4096]{1,0:T(8,128)(2,1)S(1)}, bf16[16,4096]{1,0:T(8,128)(2,1)S(1)}, u32[]{:S(2)}, u32[]{:S(2)}) collective-permute-start(bf16[16,4096]{1,0:T(8,128)(2,1)S(1)} %slice.203), channel_id=1, source_target_pairs={{0,6},{2,0},{4,2},{6,4},{1,7},{3,1},{5,3},{7,5},{8,14},{10,8},{12,... | collective-permute-start | bytes 393224 | tf_op jit(solution)/shard_map/ppermute | solution.py:18
  35.5 2.2 %collective-permute-done.16 = bf16[16,4096]{1,0:T(8,128)(2,1)S(1)} collective-permute-done((bf16[16,4096]{1,0:T(8,128)(2,1)S(1)}, bf16[16,4096]{1,0:T(8,128)(2,1)S(1)}, u32[]{:S(2)}, u32[]{:S(2)}) %collective-permute-start.16) | collective-permute-done | bytes 131104 | tf_op jit(solution)/shard_map/ppermute | solution.py:18
  38.0 3.6 %collective-permute-start.7 = (bf16[16,4096]{1,0:T(8,128)(2,1)S(1)}, bf16[16,4096]{1,0:T(8,128)(2,1)S(1)}, u32[]{:S(2)}, u32[]{:S(2)}) collective-permute-start(bf16[16,4096]{1,0:T(8,128)(2,1)S(1)} %slice.201), channel_id=1, source_target_pairs={{0,24},{8,0},{16,8},{24,16},{1,25},{9,1},{17,9},{25,17},{2,26},{10... | collective-permute-start | bytes 393224 | tf_op jit(solution)/shard_map/ppermute | solution.py:18
  41.7 2.9 %collective-permute-done.6 = bf16[16,4096]{1,0:T(8,128)(2,1)S(1)} collective-permute-done((bf16[16,4096]{1,0:T(8,128)(2,1)S(1)}, bf16[16,4096]{1,0:T(8,128)(2,1)S(1)}, u32[]{:S(2)}, u32[]{:S(2)}) %collective-permute-start.6) | collective-permute-done | bytes 131104 | tf_op jit(solution)/shard_map/ppermute | solution.py:18
  44.6 10.5 %collective-permute-done.13.refs_2_ = bf16[64,4096]{1,0:T(8,128)(2,1)S(1)} collective-permute-done((bf16[64,4096]{1,0:T(8,128)(2,1)S(1)}, bf16[64,4096]{1,0:T(8,128)(2,1)S(1)}, u32[]{:S(2)}, u32[]{:S(2)}) %collective-permute-start.13) | collective-permute-done | bytes 524320 | tf_op jit(solution)/shard_map/ppermute | solution.py:18
  57.0 7.7 %collective-permute-done.18.refs_3_ = bf16[64,4096]{1,0:T(8,128)(2,1)} collective-permute-done((bf16[64,4096]{1,0:T(8,128)(2,1)S(1)}, bf16[64,4096]{1,0:T(8,128)(2,1)}, u32[]{:S(2)}, u32[]{:S(2)}) %collective-permute-start.18) | collective-permute-done | bytes 524320 | tf_op jit(solution)/shard_map/ppermute | solution.py:18
  64.7 3.0 %copy-done = bf16[2,448,4096]{2,1,0:T(8,128)(2,1)} copy-done((bf16[2,448,4096]{2,1,0:T(8,128)(2,1)}, bf16[2,448,4096]{2,1,0:T(8,128)(2,1)S(1)}, u32[]{:S(2)}) %copy-start) | copy-done | bytes 7340056
  67.7 3.2 %collective-permute-start.19 = (bf16[64,4096]{1,0:T(8,128)(2,1)}, bf16[64,4096]{1,0:T(8,128)(2,1)}, u32[]{:S(2)}, u32[]{:S(2)}) collective-permute-start(bf16[64,4096]{1,0:T(8,128)(2,1)} %collective-permute-done.18.refs_3_), channel_id=1, source_target_pairs={{0,24},{8,0},{16,8},{24,16},{1,25},{9,1},{17,9},{25,17},{2,26},{10... | collective-permute-start | bytes 1572872 | tf_op jit(solution)/shard_map/ppermute | solution.py:18
  70.9 3.0 %copy-done.2 = bf16[2,448,4096]{2,1,0:T(8,128)(2,1)} copy-done((bf16[2,448,4096]{2,1,0:T(8,128)(2,1)}, bf16[2,448,4096]{2,1,0:T(8,128)(2,1)S(1)}, u32[]{:S(2)}) %copy-start.2) | copy-done | bytes 7340056
  73.9 3.2 %collective-permute-start.9 = (bf16[64,4096]{1,0:T(8,128)(2,1)}, bf16[64,4096]{1,0:T(8,128)(2,1)}, u32[]{:S(2)}, u32[]{:S(2)}) collective-permute-start(bf16[64,4096]{1,0:T(8,128)(2,1)} %collective-permute-done.8.refs_1_), channel_id=1, source_target_pairs={{0,6},{2,0},{4,2},{6,4},{1,7},{3,1},{5,3},{7,5},{8,14},{10,8},{12,... | collective-permute-start | bytes 1572872 | tf_op jit(solution)/shard_map/ppermute | solution.py:18
  77.2 3.1 %copy-done.1 = bf16[2,448,4096]{2,1,0:T(8,128)(2,1)S(1)} copy-done((bf16[2,448,4096]{2,1,0:T(8,128)(2,1)S(1)}, bf16[2,448,4096]{2,1,0:T(8,128)(2,1)}, u32[]{:S(2)}) %copy-start.1) | copy-done | bytes 7340056
  80.3 3.1 %copy-done.3 = bf16[2,448,4096]{2,1,0:T(8,128)(2,1)S(1)} copy-done((bf16[2,448,4096]{2,1,0:T(8,128)(2,1)S(1)}, bf16[2,448,4096]{2,1,0:T(8,128)(2,1)}, u32[]{:S(2)}) %copy-start.3) | copy-done | bytes 7340056
  83.4 5.5 %load.1 = (bf16[1792,4096]{1,0:T(8,128)(2,1)S(1)}, bf16[896,4096]{1,0:T(8,128)(2,1)S(1)}) custom-call(s32[1]{0:T(128)} %bitcast.3.core_ref, bf16[2,448,4096]{2,1,0:T(8,128)(2,1)} %bitcast.7, bf16[2,448,4096]{2,1,0:T(8,128)(2,1)S(1)} %copy-done.1, bf16[2,448,4096]{2,1,0:T(8,128)(2,1)} %bitcast.9, bf16[2,448,4096]{2,1,0:T(8,128)(2,1)S(1)} %copy-done.3, ...), custom_call_target="tpu_custom_call" | custom-call | tf_op jit(solution)/shard_map/load/pallas_call | solution.py:132
  93.1 8.4 %ffn.4 = (bf16[64,4096]{1,0:T(8,128)(2,1)S(1)}, bf16[64,4096]{1,0:T(8,128)(2,1)S(1)}, bf16[64,4096]{1,0:T(8,128)(2,1)S(1)}, bf16[64,4096]{1,0:T(8,128)(2,1)S(1)}) custom-call(bf16[64,4096]{1,0:T(8,128)(2,1)} %collective-permute-done.4.refs_0_, bf16[64,4096]{1,0:T(8,128)(2,1)} %collective-permute-done.9.refs_1_, ...), custom_call_target="tpu_custom_call" | custom-call | flops 5637144576 | tf_op jit(solution)/shard_map/ffn/pallas_call | solution.py:187
  101.5 3.3 %collective-permute-start.30 = (bf16[64,4096]{1,0:T(8,128)(2,1)S(1)}, bf16[64,4096]{1,0:T(8,128)(2,1)S(1)}, u32[]{:S(2)}, u32[]{:S(2)}) collective-permute-start(bf16[64,4096]{1,0:T(8,128)(2,1)S(1)} %get-tuple-element.79), channel_id=1, source_target_pairs={{0,6},{2,0},{4,2},{6,4},{1,7},{3,1},{5,3},{7,5},{8,14},{10,8},{12,... | collective-permute-start | bytes 1572872 | tf_op jit(solution)/shard_map/ppermute | solution.py:18
  109.0 6.9 %ffn.7 = (bf16[64,4096]{1,0:T(8,128)(2,1)S(1)}, bf16[64,4096]{1,0:T(8,128)(2,1)S(1)}, bf16[64,4096]{1,0:T(8,128)(2,1)S(1)}, bf16[64,4096]{1,0:T(8,128)(2,1)S(1)}) custom-call(bf16[64,4096]{1,0:T(8,128)(2,1)S(1)} %collective-permute-done.25.refs_0_, bf16[64,4096]{1,0:T(8,128)(2,1)S(1)} %collective-permute-done.26.refs_1_, ...), custom_call_target="tpu_custom_call" | custom-call | flops 5637144576 | tf_op jit(solution)/shard_map/ffn/pallas_call | solution.py:187
  116.2 8.1 %ffn.5 = (bf16[64,4096]{1,0:T(8,128)(2,1)S(1)}, bf16[64,4096]{1,0:T(8,128)(2,1)S(1)}, bf16[64,4096]{1,0:T(8,128)(2,1)S(1)}, bf16[64,4096]{1,0:T(8,128)(2,1)S(1)}) custom-call(bf16[64,4096]{1,0:T(8,128)(2,1)S(1)} %collective-permute-done.3.refs_0_, bf16[64,4096]{1,0:T(8,128)(2,1)} %collective-permute-done.8.refs_1_, ...), custom_call_target="tpu_custom_call" | custom-call | flops 5637144576 | tf_op jit(solution)/shard_map/ffn/pallas_call | solution.py:187
  124.3 3.3 %collective-permute-start.33 = (bf16[64,4096]{1,0:T(8,128)(2,1)S(1)}, bf16[64,4096]{1,0:T(8,128)(2,1)S(1)}, u32[]{:S(2)}, u32[]{:S(2)}) collective-permute-start(bf16[64,4096]{1,0:T(8,128)(2,1)S(1)} %get-tuple-element.85), channel_id=1, source_target_pairs={{0,6},{2,0},{4,2},{6,4},{1,7},{3,1},{5,3},{7,5},{8,14},{10,8},{12,... | collective-permute-start | bytes 1572872 | tf_op jit(solution)/shard_map/ppermute | solution.py:18
  127.7 3.3 %collective-permute-start.42 = (bf16[64,4096]{1,0:T(8,128)(2,1)S(1)}, bf16[64,4096]{1,0:T(8,128)(2,1)S(1)}, u32[]{:S(2)}, u32[]{:S(2)}) collective-permute-start(bf16[64,4096]{1,0:T(8,128)(2,1)S(1)} %get-tuple-element.92), channel_id=1, source_target_pairs={{0,24},{8,0},{16,8},{24,16},{1,25},{9,1},{17,9},{25,17},{2,26},{10... | collective-permute-start | bytes 1572872 | tf_op jit(solution)/shard_map/ppermute | solution.py:18
  134.3 3.7 %collective-permute-done.40 = bf16[64,4096]{1,0:T(8,128)(2,1)S(1)} collective-permute-done((bf16[64,4096]{1,0:T(8,128)(2,1)S(1)}, bf16[64,4096]{1,0:T(8,128)(2,1)S(1)}, u32[]{:S(2)}, u32[]{:S(2)}) %collective-permute-start.40) | collective-permute-done | bytes 524320 | tf_op jit(solution)/shard_map/ppermute | solution.py:18
  138.0 8.5 %ffn.6 = (bf16[128,4096]{1,0:T(8,128)(2,1)S(1)}, bf16[128,4096]{1,0:T(8,128)(2,1)S(1)}) custom-call(bf16[128,4096]{1,0:T(8,128)(2,1)S(1)} %get-tuple-element.75.refs_0_, bf16[128,4096]{1,0:T(8,128)(2,1)S(1)} %get-tuple-element.76.refs_1_, bf16[1792,4096]{1,0:T(8,128)(2,1)S(1)} %get-tuple-element.59.refs_4_.refs_2_, ...), custom_call_target="tpu_custom_call" | custom-call | flops 5637144576 | tf_op jit(solution)/shard_map/ffn/pallas_call | solution.py:187
  146.5 3.3 %collective-permute-done.41 = bf16[64,4096]{1,0:T(8,128)(2,1)S(1)} collective-permute-done((bf16[64,4096]{1,0:T(8,128)(2,1)S(1)}, bf16[64,4096]{1,0:T(8,128)(2,1)S(1)}, u32[]{:S(2)}, u32[]{:S(2)}) %collective-permute-start.41) | collective-permute-done | bytes 524320 | tf_op jit(solution)/shard_map/ppermute | solution.py:18
  153.2 2.7 %collective-permute-start.44 = (bf16[16,4096]{1,0:T(8,128)(2,1)S(1)}, bf16[16,4096]{1,0:T(8,128)(2,1)S(1)}, u32[]{:S(2)}, u32[]{:S(2)}) collective-permute-start(bf16[16,4096]{1,0:T(8,128)(2,1)S(1)} %get-tuple-element.99), channel_id=1, source_target_pairs={{0,6},{2,0},{4,2},{6,4},{1,7},{3,1},{5,3},{7,5},{8,14},{10,8},{12,... | collective-permute-start | bytes 393224 | tf_op jit(solution)/shard_map/ppermute | solution.py:18
  156.1 3.3 %collective-permute-start.36 = (bf16[32,4096]{1,0:T(8,128)(2,1)S(1)}, bf16[32,4096]{1,0:T(8,128)(2,1)S(1)}, u32[]{:S(2)}, u32[]{:S(2)}) collective-permute-start(bf16[32,4096]{1,0:T(8,128)(2,1)S(1)} %pad_maximum_fusion.2), channel_id=1, source_target_pairs={{0,24},{8,0},{16,8},{24,16},{1,25},{9,1},{17,9},{25,17},{2,26},{10... | collective-permute-start | bytes 786440 | tf_op jit(solution)/shard_map/ppermute | solution.py:18
  159.5 3.3 %collective-permute-start.45 = (bf16[32,4096]{1,0:T(8,128)(2,1)S(1)}, bf16[32,4096]{1,0:T(8,128)(2,1)S(1)}, u32[]{:S(2)}, u32[]{:S(2)}) collective-permute-start(bf16[32,4096]{1,0:T(8,128)(2,1)S(1)} %pad_maximum_fusion.4), channel_id=1, source_target_pairs={{0,6},{2,0},{4,2},{6,4},{1,7},{3,1},{5,3},{7,5},{8,14},{10,8},{12,... | collective-permute-start | bytes 786440 | tf_op jit(solution)/shard_map/ppermute | solution.py:18
  163.2 3.8 %collective-permute-done.38 = bf16[32,4096]{1,0:T(8,128)(2,1)S(1)} collective-permute-done((bf16[32,4096]{1,0:T(8,128)(2,1)S(1)}, bf16[32,4096]{1,0:T(8,128)(2,1)S(1)}, u32[]{:S(2)}, u32[]{:S(2)}) %collective-permute-start.38) | collective-permute-done | bytes 262176 | tf_op jit(solution)/shard_map/ppermute | solution.py:18
  173.6 3.8 %collective-permute-done.48 = bf16[16,4096]{1,0:T(8,128)(2,1)S(1)} collective-permute-done((bf16[16,4096]{1,0:T(8,128)(2,1)S(1)}, bf16[16,4096]{1,0:T(8,128)(2,1)S(1)}, u32[]{:S(2)}, u32[]{:S(2)}) %collective-permute-start.48) | collective-permute-done | bytes 131104 | tf_op jit(solution)/shard_map/ppermute | solution.py:18
  (149 shorter events, 44.2 us)
Async XLA Ops:
  6.5 58.2 %collective-permute-start.20 = (bf16[2,448,4096]{2,1,0:T(8,128)(2,1)}, bf16[2,448,4096]{2,1,0:T(8,128)(2,1)S(1)}, u32[]{:S(2)}, u32[]{:S(2)}) collective-permute-start(bf16[2,448,4096]{2,1,0:T(8,128)(2,1)} %bitcast.6), channel_id=1, source_target_pairs={{0,1},{1,0},{2,3},{3,2},{4,5},{5,4},{6,7},{7,6},{8,9},{9,8},{10,11... | collective-permute-start | bytes 22020104 | tf_op jit(solution)/shard_map/ppermute | solution.py:22
  6.5 64.4 %collective-permute-start.21 = (bf16[2,448,4096]{2,1,0:T(8,128)(2,1)}, bf16[2,448,4096]{2,1,0:T(8,128)(2,1)S(1)}, u32[]{:S(2)}, u32[]{:S(2)}) collective-permute-start(bf16[2,448,4096]{2,1,0:T(8,128)(2,1)} %bitcast.8), channel_id=1, source_target_pairs={{0,1},{1,0},{2,3},{3,2},{4,5},{5,4},{6,7},{7,6},{8,9},{9,8},{10,11... | collective-permute-start | bytes 22020104 | tf_op jit(solution)/shard_map/ppermute | solution.py:22
  8.2 69.0 %collective-permute-start.22 = (bf16[2,448,4096]{2,1,0:T(8,128)(2,1)}, bf16[2,448,4096]{2,1,0:T(8,128)(2,1)}, u32[]{:S(2)}, u32[]{:S(2)}) collective-permute-start(bf16[2,448,4096]{2,1,0:T(8,128)(2,1)} %wd.1), channel_id=1, source_target_pairs={{0,1},{1,0},{2,3},{3,2},{4,5},{5,4},{6,7},{7,6},{8,9},{9,8},{10,11... | collective-permute-start | bytes 22020104 | tf_op jit(solution)/shard_map/ppermute | solution.py:22
  13.6 9.9 %collective-permute-start.12 = (bf16[32,4096]{1,0:T(8,128)(2,1)S(1)}, bf16[32,4096]{1,0:T(8,128)(2,1)S(1)}, u32[]{:S(2)}, u32[]{:S(2)}) collective-permute-start(bf16[32,4096]{1,0:T(8,128)(2,1)S(1)} %get-tuple-element.137), channel_id=1, source_target_pairs={{0,2},{2,4},{4,6},{6,0},{1,3},{3,5},{5,7},{7,1},{8,10},{10,12},{12... | collective-permute-start | bytes 786440 | tf_op jit(solution)/shard_map/ppermute | solution.py:18
  17.2 7.9 %collective-permute-start.15 = (bf16[32,4096]{1,0:T(8,128)(2,1)S(1)}, bf16[32,4096]{1,0:T(8,128)(2,1)S(1)}, u32[]{:S(2)}, u32[]{:S(2)}) collective-permute-start(bf16[32,4096]{1,0:T(8,128)(2,1)S(1)} %get-tuple-element.137), channel_id=1, source_target_pairs={{0,6},{2,0},{4,2},{6,4},{1,7},{3,1},{5,3},{7,5},{8,14},{10,8},{12,... | collective-permute-start | bytes 786440 | tf_op jit(solution)/shard_map/ppermute | solution.py:18
  23.4 8.1 %collective-permute-start.2 = (bf16[32,4096]{1,0:T(8,128)(2,1)S(1)}, bf16[32,4096]{1,0:T(8,128)(2,1)S(1)}, u32[]{:S(2)}, u32[]{:S(2)}) collective-permute-start(bf16[32,4096]{1,0:T(8,128)(2,1)S(1)} %pad_maximum_fusion.1), channel_id=1, source_target_pairs={{0,8},{8,16},{16,24},{24,0},{1,9},{9,17},{17,25},{25,1},{2,10},{10... | collective-permute-start | bytes 786440 | tf_op jit(solution)/shard_map/ppermute | solution.py:18
  44.5 10.6 %collective-permute-start.13 = (bf16[64,4096]{1,0:T(8,128)(2,1)S(1)}, bf16[64,4096]{1,0:T(8,128)(2,1)S(1)}, u32[]{:S(2)}, u32[]{:S(2)}) collective-permute-start(bf16[64,4096]{1,0:T(8,128)(2,1)S(1)} %get-tuple-element.117), channel_id=1, source_target_pairs={{0,8},{8,16},{16,24},{24,0},{1,9},{9,17},{17,25},{25,1},{2,10},{10... | collective-permute-start | bytes 1572872 | tf_op jit(solution)/shard_map/ppermute | solution.py:18
  44.6 10.8 %collective-permute-start.3 = (bf16[64,4096]{1,0:T(8,128)(2,1)S(1)}, bf16[64,4096]{1,0:T(8,128)(2,1)S(1)}, u32[]{:S(2)}, u32[]{:S(2)}) collective-permute-start(bf16[64,4096]{1,0:T(8,128)(2,1)S(1)} %pad_maximum_fusion), channel_id=1, source_target_pairs={{0,2},{2,4},{4,6},{6,0},{1,3},{3,5},{5,7},{7,1},{8,10},{10,12},{12... | collective-permute-start | bytes 1572872 | tf_op jit(solution)/shard_map/ppermute | solution.py:18
  55.1 9.5 %collective-permute-start.18 = (bf16[64,4096]{1,0:T(8,128)(2,1)S(1)}, bf16[64,4096]{1,0:T(8,128)(2,1)}, u32[]{:S(2)}, u32[]{:S(2)}) collective-permute-start(bf16[64,4096]{1,0:T(8,128)(2,1)S(1)} %get-tuple-element.132), channel_id=1, source_target_pairs={{0,24},{8,0},{16,8},{24,16},{1,25},{9,1},{17,9},{25,17},{2,26},{10... | collective-permute-start | bytes 1572872 | tf_op jit(solution)/shard_map/ppermute | solution.py:18
  55.3 9.4 %collective-permute-start.8 = (bf16[64,4096]{1,0:T(8,128)(2,1)S(1)}, bf16[64,4096]{1,0:T(8,128)(2,1)}, u32[]{:S(2)}, u32[]{:S(2)}) collective-permute-start(bf16[64,4096]{1,0:T(8,128)(2,1)S(1)} %get-tuple-element.142), channel_id=1, source_target_pairs={{0,6},{2,0},{4,2},{6,4},{1,7},{3,1},{5,3},{7,5},{8,14},{10,8},{12,... | collective-permute-start | bytes 1572872 | tf_op jit(solution)/shard_map/ppermute | solution.py:18
  64.7 24.2 %collective-permute-start.14 = (bf16[64,4096]{1,0:T(8,128)(2,1)S(1)}, bf16[64,4096]{1,0:T(8,128)(2,1)}, u32[]{:S(2)}, u32[]{:S(2)}) collective-permute-start(bf16[64,4096]{1,0:T(8,128)(2,1)S(1)} %collective-permute-done.13.refs_2_), channel_id=1, source_target_pairs={{0,8},{8,16},{16,24},{24,0},{1,9},{9,17},{17,25},{25,1},{2,10},{10... | collective-permute-start | bytes 1572872 | tf_op jit(solution)/shard_map/ppermute | solution.py:18
  64.7 26.3 %collective-permute-start.4 = (bf16[64,4096]{1,0:T(8,128)(2,1)S(1)}, bf16[64,4096]{1,0:T(8,128)(2,1)}, u32[]{:S(2)}, u32[]{:S(2)}) collective-permute-start(bf16[64,4096]{1,0:T(8,128)(2,1)S(1)} %collective-permute-done.3.refs_0_), channel_id=1, source_target_pairs={{0,2},{2,4},{4,6},{6,0},{1,3},{3,5},{5,7},{7,1},{8,10},{10,12},{12... | collective-permute-start | bytes 1572872 | tf_op jit(solution)/shard_map/ppermute | solution.py:18
  67.7 25.4 %collective-permute-start.19 = (bf16[64,4096]{1,0:T(8,128)(2,1)}, bf16[64,4096]{1,0:T(8,128)(2,1)}, u32[]{:S(2)}, u32[]{:S(2)}) collective-permute-start(bf16[64,4096]{1,0:T(8,128)(2,1)} %collective-permute-done.18.refs_3_), channel_id=1, source_target_pairs={{0,24},{8,0},{16,8},{24,16},{1,25},{9,1},{17,9},{25,17},{2,26},{10... | collective-permute-start | bytes 1572872 | tf_op jit(solution)/shard_map/ppermute | solution.py:18
  73.9 19.2 %collective-permute-start.9 = (bf16[64,4096]{1,0:T(8,128)(2,1)}, bf16[64,4096]{1,0:T(8,128)(2,1)}, u32[]{:S(2)}, u32[]{:S(2)}) collective-permute-start(bf16[64,4096]{1,0:T(8,128)(2,1)} %collective-permute-done.8.refs_1_), channel_id=1, source_target_pairs={{0,6},{2,0},{4,2},{6,4},{1,7},{3,1},{5,3},{7,5},{8,14},{10,8},{12,... | collective-permute-start | bytes 1572872 | tf_op jit(solution)/shard_map/ppermute | solution.py:18
  77.1 27.7 %collective-permute-start.28 = (bf16[64,4096]{1,0:T(8,128)(2,1)}, bf16[64,4096]{1,0:T(8,128)(2,1)S(1)}, u32[]{:S(2)}, u32[]{:S(2)}) collective-permute-start(bf16[64,4096]{1,0:T(8,128)(2,1)} %copy-done.10), channel_id=1, source_target_pairs={{0,24},{8,0},{16,8},{24,16},{1,25},{9,1},{17,9},{25,17},{2,26},{10... | collective-permute-start | bytes 1572872 | tf_op jit(solution)/shard_map/ppermute | solution.py:18
  88.9 15.9 %collective-permute-start.26 = (bf16[64,4096]{1,0:T(8,128)(2,1)S(1)}, bf16[64,4096]{1,0:T(8,128)(2,1)S(1)}, u32[]{:S(2)}, u32[]{:S(2)}) collective-permute-start(bf16[64,4096]{1,0:T(8,128)(2,1)S(1)} %copy-done.5), channel_id=1, source_target_pairs={{0,6},{2,0},{4,2},{6,4},{1,7},{3,1},{5,3},{7,5},{8,14},{10,8},{12,... | collective-permute-start | bytes 1572872 | tf_op jit(solution)/shard_map/ppermute | solution.py:18
  91.0 15.1 %collective-permute-start.27 = (bf16[64,4096]{1,0:T(8,128)(2,1)S(1)}, bf16[64,4096]{1,0:T(8,128)(2,1)S(1)}, u32[]{:S(2)}, u32[]{:S(2)}) collective-permute-start(bf16[64,4096]{1,0:T(8,128)(2,1)S(1)} %copy-done.9), channel_id=1, source_target_pairs={{0,8},{8,16},{16,24},{24,0},{1,9},{9,17},{17,25},{25,1},{2,10},{10... | collective-permute-start | bytes 1572872 | tf_op jit(solution)/shard_map/ppermute | solution.py:18
  93.1 15.9 %collective-permute-start.25 = (bf16[64,4096]{1,0:T(8,128)(2,1)S(1)}, bf16[64,4096]{1,0:T(8,128)(2,1)S(1)}, u32[]{:S(2)}, u32[]{:S(2)}) collective-permute-start(bf16[64,4096]{1,0:T(8,128)(2,1)S(1)} %copy-done.7), channel_id=1, source_target_pairs={{0,2},{2,4},{4,6},{6,0},{1,3},{3,5},{5,7},{7,1},{8,10},{10,12},{12... | collective-permute-start | bytes 1572872 | tf_op jit(solution)/shard_map/ppermute | solution.py:18
  101.5 22.8 %collective-permute-start.30 = (bf16[64,4096]{1,0:T(8,128)(2,1)S(1)}, bf16[64,4096]{1,0:T(8,128)(2,1)S(1)}, u32[]{:S(2)}, u32[]{:S(2)}) collective-permute-start(bf16[64,4096]{1,0:T(8,128)(2,1)S(1)} %get-tuple-element.79), channel_id=1, source_target_pairs={{0,6},{2,0},{4,2},{6,4},{1,7},{3,1},{5,3},{7,5},{8,14},{10,8},{12,... | collective-permute-start | bytes 1572872 | tf_op jit(solution)/shard_map/ppermute | solution.py:18
  104.8 22.8 %collective-permute-start.31 = (bf16[64,4096]{1,0:T(8,128)(2,1)S(1)}, bf16[64,4096]{1,0:T(8,128)(2,1)S(1)}, u32[]{:S(2)}, u32[]{:S(2)}) collective-permute-start(bf16[64,4096]{1,0:T(8,128)(2,1)S(1)} %get-tuple-element.80), channel_id=1, source_target_pairs={{0,2},{2,4},{4,6},{6,0},{1,3},{3,5},{5,7},{7,1},{8,10},{10,12},{12... | collective-permute-start | bytes 1572872 | tf_op jit(solution)/shard_map/ppermute | solution.py:18
  104.8 22.9 %collective-permute-start.23 = (bf16[64,4096]{1,0:T(8,128)(2,1)S(1)}, bf16[64,4096]{1,0:T(8,128)(2,1)S(1)}, u32[]{:S(2)}, u32[]{:S(2)}) collective-permute-start(bf16[64,4096]{1,0:T(8,128)(2,1)S(1)} %get-tuple-element.65), channel_id=1, source_target_pairs={{0,24},{8,0},{16,8},{24,16},{1,25},{9,1},{17,9},{25,17},{2,26},{10... | collective-permute-start | bytes 1572872 | tf_op jit(solution)/shard_map/ppermute | solution.py:18
  106.1 24.9 %collective-permute-start.24 = (bf16[64,4096]{1,0:T(8,128)(2,1)S(1)}, bf16[64,4096]{1,0:T(8,128)(2,1)S(1)}, u32[]{:S(2)}, u32[]{:S(2)}) collective-permute-start(bf16[64,4096]{1,0:T(8,128)(2,1)S(1)} %get-tuple-element.66), channel_id=1, source_target_pairs={{0,8},{8,16},{16,24},{24,0},{1,9},{9,17},{17,25},{25,1},{2,10},{10... | collective-permute-start | bytes 1572872 | tf_op jit(solution)/shard_map/ppermute | solution.py:18
  115.9 15.7 %collective-permute-start.29 = (bf16[64,4096]{1,0:T(8,128)(2,1)S(1)}, bf16[64,4096]{1,0:T(8,128)(2,1)S(1)}, u32[]{:S(2)}, u32[]{:S(2)}) collective-permute-start(bf16[64,4096]{1,0:T(8,128)(2,1)S(1)} %get-tuple-element.78), channel_id=1, source_target_pairs={{0,2},{2,4},{4,6},{6,0},{1,3},{3,5},{5,7},{7,1},{8,10},{10,12},{12... | collective-permute-start | bytes 1572872 | tf_op jit(solution)/shard_map/ppermute | solution.py:18
  124.3 10.0 %collective-permute-start.33 = (bf16[64,4096]{1,0:T(8,128)(2,1)S(1)}, bf16[64,4096]{1,0:T(8,128)(2,1)S(1)}, u32[]{:S(2)}, u32[]{:S(2)}) collective-permute-start(bf16[64,4096]{1,0:T(8,128)(2,1)S(1)} %get-tuple-element.85), channel_id=1, source_target_pairs={{0,6},{2,0},{4,2},{6,4},{1,7},{3,1},{5,3},{7,5},{8,14},{10,8},{12,... | collective-permute-start | bytes 1572872 | tf_op jit(solution)/shard_map/ppermute | solution.py:18
  127.6 10.4 %collective-permute-start.40 = (bf16[64,4096]{1,0:T(8,128)(2,1)S(1)}, bf16[64,4096]{1,0:T(8,128)(2,1)S(1)}, u32[]{:S(2)}, u32[]{:S(2)}) collective-permute-start(bf16[64,4096]{1,0:T(8,128)(2,1)S(1)} %get-tuple-element.89), channel_id=1, source_target_pairs={{0,8},{8,16},{16,24},{24,0},{1,9},{9,17},{17,25},{25,1},{2,10},{10... | collective-permute-start | bytes 1572872 | tf_op jit(solution)/shard_map/ppermute | solution.py:18
  127.7 18.8 %collective-permute-start.42 = (bf16[64,4096]{1,0:T(8,128)(2,1)S(1)}, bf16[64,4096]{1,0:T(8,128)(2,1)S(1)}, u32[]{:S(2)}, u32[]{:S(2)}) collective-permute-start(bf16[64,4096]{1,0:T(8,128)(2,1)S(1)} %get-tuple-element.92), channel_id=1, source_target_pairs={{0,24},{8,0},{16,8},{24,16},{1,25},{9,1},{17,9},{25,17},{2,26},{10... | collective-permute-start | bytes 1572872 | tf_op jit(solution)/shard_map/ppermute | solution.py:18
  131.0 15.5 %collective-permute-start.32 = (bf16[64,4096]{1,0:T(8,128)(2,1)S(1)}, bf16[64,4096]{1,0:T(8,128)(2,1)S(1)}, u32[]{:S(2)}, u32[]{:S(2)}) collective-permute-start(bf16[64,4096]{1,0:T(8,128)(2,1)S(1)} %add_convert_fusion.7), channel_id=1, source_target_pairs={{0,6},{2,0},{4,2},{6,4},{1,7},{3,1},{5,3},{7,5},{8,14},{10,8},{12,... | collective-permute-start | bytes 1572872 | tf_op jit(solution)/shard_map/ppermute | solution.py:18
  131.5 15.0 %collective-permute-start.34 = (bf16[64,4096]{1,0:T(8,128)(2,1)S(1)}, bf16[64,4096]{1,0:T(8,128)(2,1)S(1)}, u32[]{:S(2)}, u32[]{:S(2)}) collective-permute-start(bf16[64,4096]{1,0:T(8,128)(2,1)S(1)} %add_convert_fusion.5), channel_id=1, source_target_pairs={{0,2},{2,4},{4,6},{6,0},{1,3},{3,5},{5,7},{7,1},{8,10},{10,12},{12... | collective-permute-start | bytes 1572872 | tf_op jit(solution)/shard_map/ppermute | solution.py:18
  134.3 12.3 %collective-permute-start.43 = (bf16[64,4096]{1,0:T(8,128)(2,1)S(1)}, bf16[64,4096]{1,0:T(8,128)(2,1)S(1)}, u32[]{:S(2)}, u32[]{:S(2)}) collective-permute-start(bf16[64,4096]{1,0:T(8,128)(2,1)S(1)} %add_convert_fusion.1), channel_id=1, source_target_pairs={{0,8},{8,16},{16,24},{24,0},{1,9},{9,17},{17,25},{25,1},{2,10},{10... | collective-permute-start | bytes 1572872 | tf_op jit(solution)/shard_map/ppermute | solution.py:18
  138.0 11.8 %collective-permute-start.41 = (bf16[64,4096]{1,0:T(8,128)(2,1)S(1)}, bf16[64,4096]{1,0:T(8,128)(2,1)S(1)}, u32[]{:S(2)}, u32[]{:S(2)}) collective-permute-start(bf16[64,4096]{1,0:T(8,128)(2,1)S(1)} %add_convert_fusion.3), channel_id=1, source_target_pairs={{0,24},{8,0},{16,8},{24,16},{1,25},{9,1},{17,9},{25,17},{2,26},{10... | collective-permute-start | bytes 1572872 | tf_op jit(solution)/shard_map/ppermute | solution.py:18
  159.5 9.6 %collective-permute-start.45 = (bf16[32,4096]{1,0:T(8,128)(2,1)S(1)}, bf16[32,4096]{1,0:T(8,128)(2,1)S(1)}, u32[]{:S(2)}, u32[]{:S(2)}) collective-permute-start(bf16[32,4096]{1,0:T(8,128)(2,1)S(1)} %pad_maximum_fusion.4), channel_id=1, source_target_pairs={{0,6},{2,0},{4,2},{6,4},{1,7},{3,1},{5,3},{7,5},{8,14},{10,8},{12,... | collective-permute-start | bytes 786440 | tf_op jit(solution)/shard_map/ppermute | solution.py:18
  162.9 7.7 %collective-permute-start.47 = (bf16[32,4096]{1,0:T(8,128)(2,1)S(1)}, bf16[32,4096]{1,0:T(8,128)(2,1)S(1)}, u32[]{:S(2)}, u32[]{:S(2)}) collective-permute-start(bf16[32,4096]{1,0:T(8,128)(2,1)S(1)} %pad_maximum_fusion.5), channel_id=1, source_target_pairs={{0,2},{2,4},{4,6},{6,0},{1,3},{3,5},{5,7},{7,1},{8,10},{10,12},{12... | collective-permute-start | bytes 786440 | tf_op jit(solution)/shard_map/ppermute | solution.py:18
  (30 other events, 308.0 us)

commit v2 on v0

--- a/solution.py
+++ b/solution.py
@@ -225,10 +225,8 @@
 
 
 def ring_gather(v, axis):
-    half = v.shape[0] // 2
-    plus, minus = shift(v, axis, 1), shift(v, axis, -1)
-    plus2, minus2 = shift(plus[:half], axis, 1), shift(minus[half:], axis, -1)
-    return jnp.concatenate([v, plus, minus, plus2, minus2], axis=0)
+    far, plus, minus = [shift(v, axis, step) for step in (2, 1, -1)]
+    return jnp.concatenate([v, plus, minus, far], axis=0)
 
 
 def add(*terms):
@@ -240,13 +238,9 @@
 
 def ring_scatter(v, axis):
     unit = v.shape[0] // RING
-    half = unit // 2
-    own, plus, minus = v[:unit], v[unit : 2 * unit], v[2 * unit : 3 * unit]
-    plus2, minus2 = v[3 * unit : 3 * unit + half], v[3 * unit + half :]
-    from_next, from_last = shift(plus2, axis, -1), shift(minus2, axis, 1)
-    plus = jnp.concatenate([add(plus[:half], from_next), plus[half:]], axis=0)
-    minus = jnp.concatenate([minus[:half], add(minus[half:], from_last)], axis=0)
-    return add(own, shift(plus, axis, -1), shift(minus, axis, 1))
+    own, plus, minus, far = [v[k * unit : (k + 1) * unit] for k in range(RING)]
+    far, plus, minus = shift(far, axis, 2), shift(plus, axis, -1), shift(minus, axis, 1)
+    return add(own, plus, minus, far)
 
 
 def first_halves(v, axis):
@@ -311,7 +305,6 @@
     rest_a, rest_b = second_halves(a0, "z"), second_halves(b0, "x")
     (a0, b0), peers = after([a0, b0], peers)
     w1, w2 = load(core_arg, w_gate, peers[0], w_up, peers[1], w_down, peers[2])
-    (w1, w2), lead_a, lead_b = after([w1, w2], lead_a, lead_b)
     far_a, far_b = onward(lead_a, "z"), onward(lead_b, "x")
     early = ffn(rest_a + rest_b, w1, w2)
     early_a, early_b = backward(early[:2], "z"), backward(early[2:], "x")
@@ -323,7 +316,7 @@
     far_b, late_b, (a0, b0) = after(far_b, late[2:], [a0, b0])
     late_a = backward([add(v, w) for v, w in zip(late_a, far_a)], "z")
     late_b = backward([add(v, w) for v, w in zip(late_b, far_b)], "x")
-    y0 = ffn([a0, b0], w1, w2, looped=True)
+    y0 = ffn([a0, b0], w1, w2)
     ya = collect(y0[0], early_a, late_a)
     yb = collect(y0[1], early_b, late_b)
     done_a = ring_scatter(ya, "x")
@@ -331,7 +324,9 @@
 
     both = 2 * CAP
     groups = [done_a[:both], done_a[both:], done_b[:both], done_b[both:]]
-    groups = [groups[0]] + [shift(groups[k], "task", -k) for k in range(1, RING)]
+    first = shift(groups[1], "task", -1)
+    last = [shift(groups[k], "task", -k) for k in range(2, RING)]
+    groups = [groups[0], first] + last
     kept = jnp.concatenate([v[:CAP] for v in groups], axis=0)
     swapped = swap_cores(jnp.concatenate([v[CAP:] for v in groups], axis=0))
     returned = jnp.concatenate([kept, swapped], axis=0)

time: 191 us -> 184 us (0.963)
  waiting for transfers between devices: 88 us -> 71 us
  starting transfers between devices: 58.8 us -> 70.8 us
    ppermute x46 -> x42, waiting for transfers between devices: 85 us -> 68 us  [shift(): return lax.ppermute(v, axis, [(i, (i + step) % RING) for i in range(RING)])]
    ppermute x46 -> x42, starting transfers between devices: 57.9 us -> 70 us  [shift(): return lax.ppermute(v, axis, [(i, (i + step) % RING) for i in range(RING)])]
  transfers between devices with their start and end apart: 51 -> 47, of which waited for: 22 -> 21; matrix products, arithmetic and copies ran while one was open for 1% -> 1% of each run, Pallas kernels for 20% -> 20%
where the time goes in v2:
time: 184 us; the launch traced here: 183 us
  waiting for transfers between devices  71 us (39%)
  starting transfers between devices  70.8 us (38%)
  Pallas kernels  37.4 us (20%)
  other arithmetic  1.99 us (1%)
    ppermute x42, starting transfers between devices, shift(): return lax.ppermute(v, axis, [(i, (i + step) % RING) for i in range(RING)])  70 us
    ppermute x42, waiting for transfers between devices, shift(): return lax.ppermute(v, axis, [(i, (i + step) % RING) for i in range(RING)])  68 us
    pallas_call x4, Pallas kernels, ffn(): pl.pallas_call(functools.partial(ffn_kernel, rows, looped), out_shape=[pl...  27.4 us
    pallas_call x1, Pallas kernels, load(): pl.pallas_call(load_kernel, out_shape=[pltpu.VMEM((2 * CORES * part, widt...  4.38 us
    pallas_call x1, Pallas kernels, pick(): pl.pallas_call(pick_kernel, out_shape=[pltpu.VMEM(w.shape[1:], BF16) for...  4.23 us
  transfers between devices with their start and end apart: 47, of which 21 were waited for; matrix products, arithmetic and copies ran while one was open for 1% of the time, Pallas kernels for 20%

profile of v2, /device:TPU:0, one launch (start us, length us, event | category | flops | bytes accessed | tf_op | source)
XLA Modules:
  0.0 183.1 jit_solution(9038262674951747234)
XLA Ops:
  3.1 3.4 %collective-permute-start.9 = (bf16[16,4096]{1,0:T(8,128)(2,1)S(1)}, bf16[16,4096]{1,0:T(8,128)(2,1)S(1)}, u32[]{:S(2)}, u32[]{:S(2)}) collective-permute-start(bf16[16,4096]{1,0:T(8,128)(2,1)S(1)} %pad_maximum_fusion.4), channel_id=1, source_target_pairs={{0,64},{32,96},{64,0},{96,32},{1,65},{33,97},{65,1},{97,33},{2,66}... | collective-permute-start | bytes 393224 | tf_op jit(solution)/shard_map/ppermute | solution.py:18
  8.7 4.2 %pick.1 = (bf16[448,4096]{1,0:T(8,128)(2,1)S(1)}, bf16[448,4096]{1,0:T(8,128)(2,1)S(1)}, bf16[448,4096]{1,0:T(8,128)(2,1)S(1)}) custom-call(s32[1]{0:T(128)S(6)} %sub.3.which_ref, bf16[2,448,4096]{2,1,0:T(8,128)(2,1)} %bitcast.6, bf16[2,448,4096]{2,1,0:T(8,128)(2,1)} %bitcast.8, bf16[2,448,4096]{2,1,0:T(8,128)(2,1)} %wd.3), custom_call_target="tpu_custom_call" | custom-call | tf_op jit(solution)/shard_map/pick/pallas_call | solution.py:126
  17.3 8.1 %collective-permute-done.2 = bf16[32,4096]{1,0:T(8,128)(2,1)S(1)} collective-permute-done((bf16[32,4096]{1,0:T(8,128)(2,1)S(1)}, bf16[32,4096]{1,0:T(8,128)(2,1)S(1)}, u32[]{:S(2)}, u32[]{:S(2)}) %collective-permute-start.2) | collective-permute-done | bytes 262176 | tf_op jit(solution)/shard_map/ppermute | solution.py:18
  25.4 2.4 %collective-permute-start.14 = (bf16[32,4096]{1,0:T(8,128)(2,1)S(1)}, bf16[32,4096]{1,0:T(8,128)(2,1)S(1)}, u32[]{:S(2)}, u32[]{:S(2)}) collective-permute-start(bf16[32,4096]{1,0:T(8,128)(2,1)S(1)} %get-tuple-element.137), channel_id=1, source_target_pairs={{0,6},{2,0},{4,2},{6,4},{1,7},{3,1},{5,3},{7,5},{8,14},{10,8},{12,... | collective-permute-start | bytes 786440 | tf_op jit(solution)/shard_map/ppermute | solution.py:18
  29.5 9.1 %collective-permute-done.14 = bf16[32,4096]{1,0:T(8,128)(2,1)S(1)} collective-permute-done((bf16[32,4096]{1,0:T(8,128)(2,1)S(1)}, bf16[32,4096]{1,0:T(8,128)(2,1)S(1)}, u32[]{:S(2)}, u32[]{:S(2)}) %collective-permute-start.14) | collective-permute-done | bytes 262176 | tf_op jit(solution)/shard_map/ppermute | solution.py:18
  41.2 6.6 %collective-permute-done.5 = bf16[32,4096]{1,0:T(8,128)(2,1)S(1)} collective-permute-done((bf16[32,4096]{1,0:T(8,128)(2,1)S(1)}, bf16[32,4096]{1,0:T(8,128)(2,1)S(1)}, u32[]{:S(2)}, u32[]{:S(2)}) %collective-permute-start.5) | collective-permute-done | bytes 262176 | tf_op jit(solution)/shard_map/ppermute | solution.py:18
  47.8 2.8 %collective-permute-start.16 = (bf16[64,4096]{1,0:T(8,128)(2,1)S(1)}, bf16[64,4096]{1,0:T(8,128)(2,1)S(1)}, u32[]{:S(2)}, u32[]{:S(2)}) collective-permute-start(bf16[64,4096]{1,0:T(8,128)(2,1)S(1)} %get-tuple-element.115), channel_id=1, source_target_pairs={{0,24},{8,0},{16,8},{24,16},{1,25},{9,1},{17,9},{25,17},{2,26},{10... | collective-permute-start | bytes 1572872 | tf_op jit(solution)/shard_map/ppermute | solution.py:18
  50.9 2.7 %collective-permute-start.12 = (bf16[64,4096]{1,0:T(8,128)(2,1)S(1)}, bf16[64,4096]{1,0:T(8,128)(2,1)S(1)}, u32[]{:S(2)}, u32[]{:S(2)}) collective-permute-start(bf16[64,4096]{1,0:T(8,128)(2,1)S(1)} %get-tuple-element.119), channel_id=1, source_target_pairs={{0,8},{8,16},{16,24},{24,0},{1,9},{9,17},{17,25},{25,1},{2,10},{10... | collective-permute-start | bytes 1572872 | tf_op jit(solution)/shard_map/ppermute | solution.py:18
  53.8 4.0 %collective-permute-done.16.refs_3_ = bf16[64,4096]{1,0:T(8,128)(2,1)S(1)} collective-permute-done((bf16[64,4096]{1,0:T(8,128)(2,1)S(1)}, bf16[64,4096]{1,0:T(8,128)(2,1)S(1)}, u32[]{:S(2)}, u32[]{:S(2)}) %collective-permute-start.16) | collective-permute-done | bytes 524320 | tf_op jit(solution)/shard_map/ppermute | solution.py:18
  57.8 4.8 %collective-permute-start.7 = (bf16[64,4096]{1,0:T(8,128)(2,1)S(1)}, bf16[64,4096]{1,0:T(8,128)(2,1)S(1)}, u32[]{:S(2)}, u32[]{:S(2)}) collective-permute-start(bf16[64,4096]{1,0:T(8,128)(2,1)S(1)} %get-tuple-element.121), channel_id=1, source_target_pairs={{0,6},{2,0},{4,2},{6,4},{1,7},{3,1},{5,3},{7,5},{8,14},{10,8},{12,... | collective-permute-start | bytes 1572872 | tf_op jit(solution)/shard_map/ppermute | solution.py:18
  62.6 7.9 %collective-permute-done.7.refs_1_ = bf16[64,4096]{1,0:T(8,128)(2,1)S(1)} collective-permute-done((bf16[64,4096]{1,0:T(8,128)(2,1)S(1)}, bf16[64,4096]{1,0:T(8,128)(2,1)S(1)}, u32[]{:S(2)}, u32[]{:S(2)}) %collective-permute-start.7) | collective-permute-done | bytes 524320 | tf_op jit(solution)/shard_map/ppermute | solution.py:18
  70.5 3.7 %collective-permute-start.17 = (bf16[64,4096]{1,0:T(8,128)(2,1)S(1)}, bf16[64,4096]{1,0:T(8,128)(2,1)S(1)}, u32[]{:S(2)}, u32[]{:S(2)}) collective-permute-start(bf16[64,4096]{1,0:T(8,128)(2,1)S(1)} %collective-permute-done.16.refs_3_), channel_id=1, source_target_pairs={{0,24},{8,0},{16,8},{24,16},{1,25},{9,1},{17,9},{25,17},{2,26},{10... | collective-permute-start | bytes 1572872 | tf_op jit(solution)/shard_map/ppermute | solution.py:18
  74.6 2.0 %collective-permute-start.8 = (bf16[64,4096]{1,0:T(8,128)(2,1)S(1)}, bf16[64,4096]{1,0:T(8,128)(2,1)S(1)}, u32[]{:S(2)}, u32[]{:S(2)}) collective-permute-start(bf16[64,4096]{1,0:T(8,128)(2,1)S(1)} %collective-permute-done.7.refs_1_), channel_id=1, source_target_pairs={{0,6},{2,0},{4,2},{6,4},{1,7},{3,1},{5,3},{7,5},{8,14},{10,8},{12,... | collective-permute-start | bytes 1572872 | tf_op jit(solution)/shard_map/ppermute | solution.py:18
  77.3 4.4 %load.1 = (bf16[1792,4096]{1,0:T(8,128)(2,1)S(1)}, bf16[896,4096]{1,0:T(8,128)(2,1)S(1)}) custom-call(s32[1]{0:T(128)} %bitcast.1.core_ref, bf16[2,448,4096]{2,1,0:T(8,128)(2,1)} %bitcast.7, bf16[448,4096]{1,0:T(8,128)(2,1)S(1)} %collective-permute-done.18.wpg, bf16[2,448,4096]{2,1,0:T(8,128)(2,1)} %bitcast.9, ...), custom_call_target="tpu_custom_call" | custom-call | tf_op jit(solution)/shard_map/load/pallas_call | solution.py:154
  81.7 3.0 %collective-permute-done.17.refs_3_ = bf16[64,4096]{1,0:T(8,128)(2,1)S(1)} collective-permute-done((bf16[64,4096]{1,0:T(8,128)(2,1)S(1)}, bf16[64,4096]{1,0:T(8,128)(2,1)S(1)}, u32[]{:S(2)}, u32[]{:S(2)}) %collective-permute-start.17) | collective-permute-done | bytes 524320 | tf_op jit(solution)/shard_map/ppermute | solution.py:18
  84.7 3.1 %collective-permute-start.26 = (bf16[64,4096]{1,0:T(8,128)(2,1)S(1)}, bf16[64,4096]{1,0:T(8,128)(2,1)S(1)}, u32[]{:S(2)}, u32[]{:S(2)}) collective-permute-start(bf16[64,4096]{1,0:T(8,128)(2,1)S(1)} %get-tuple-element.119), channel_id=1, source_target_pairs={{0,24},{8,0},{16,8},{24,16},{1,25},{9,1},{17,9},{25,17},{2,26},{10... | collective-permute-start | bytes 1572872 | tf_op jit(solution)/shard_map/ppermute | solution.py:18
  87.7 2.5 %collective-permute-done.13.refs_2_ = bf16[64,4096]{1,0:T(8,128)(2,1)S(1)} collective-permute-done((bf16[64,4096]{1,0:T(8,128)(2,1)S(1)}, bf16[64,4096]{1,0:T(8,128)(2,1)S(1)}, u32[]{:S(2)}, u32[]{:S(2)}) %collective-permute-start.13) | collective-permute-done | bytes 524320 | tf_op jit(solution)/shard_map/ppermute | solution.py:18
  93.4 6.8 %ffn.4 = (bf16[64,4096]{1,0:T(8,128)(2,1)S(1)}, bf16[64,4096]{1,0:T(8,128)(2,1)S(1)}, bf16[64,4096]{1,0:T(8,128)(2,1)S(1)}, bf16[64,4096]{1,0:T(8,128)(2,1)S(1)}) custom-call(bf16[64,4096]{1,0:T(8,128)(2,1)S(1)} %collective-permute-done.4.refs_0_, bf16[64,4096]{1,0:T(8,128)(2,1)S(1)} %collective-permute-done.8.refs_1_, ...), custom_call_target="tpu_custom_call" | custom-call | flops 5637144576 | tf_op jit(solution)/shard_map/ffn/pallas_call | solution.py:209
  105.2 6.8 %ffn.7 = (bf16[64,4096]{1,0:T(8,128)(2,1)S(1)}, bf16[64,4096]{1,0:T(8,128)(2,1)S(1)}, bf16[64,4096]{1,0:T(8,128)(2,1)S(1)}, bf16[64,4096]{1,0:T(8,128)(2,1)S(1)}) custom-call(bf16[64,4096]{1,0:T(8,128)(2,1)S(1)} %collective-permute-done.23.refs_0_, bf16[64,4096]{1,0:T(8,128)(2,1)S(1)} %collective-permute-done.24.refs_1_, ...), custom_call_target="tpu_custom_call" | custom-call | flops 5637144576 | tf_op jit(solution)/shard_map/ffn/pallas_call | solution.py:209
  112.3 6.9 %ffn.5 = (bf16[64,4096]{1,0:T(8,128)(2,1)S(1)}, bf16[64,4096]{1,0:T(8,128)(2,1)S(1)}, bf16[64,4096]{1,0:T(8,128)(2,1)S(1)}, bf16[64,4096]{1,0:T(8,128)(2,1)S(1)}) custom-call(bf16[64,4096]{1,0:T(8,128)(2,1)S(1)} %collective-permute-done.3.refs_0_, bf16[64,4096]{1,0:T(8,128)(2,1)S(1)} %collective-permute-done.7.refs_1_, ...), custom_call_target="tpu_custom_call" | custom-call | flops 5637144576 | tf_op jit(solution)/shard_map/ffn/pallas_call | solution.py:209
  119.2 3.8 %collective-permute-start.32 = (bf16[64,4096]{1,0:T(8,128)(2,1)S(1)}, bf16[64,4096]{1,0:T(8,128)(2,1)S(1)}, u32[]{:S(2)}, u32[]{:S(2)}) collective-permute-start(bf16[64,4096]{1,0:T(8,128)(2,1)S(1)} %get-tuple-element.87), channel_id=1, source_target_pairs={{0,6},{2,0},{4,2},{6,4},{1,7},{3,1},{5,3},{7,5},{8,14},{10,8},{12,... | collective-permute-start | bytes 1572872 | tf_op jit(solution)/shard_map/ppermute | solution.py:18
  123.1 3.3 %collective-permute-start.40 = (bf16[64,4096]{1,0:T(8,128)(2,1)S(1)}, bf16[64,4096]{1,0:T(8,128)(2,1)S(1)}, u32[]{:S(2)}, u32[]{:S(2)}) collective-permute-start(bf16[64,4096]{1,0:T(8,128)(2,1)S(1)} %get-tuple-element.94), channel_id=1, source_target_pairs={{0,24},{8,0},{16,8},{24,16},{1,25},{9,1},{17,9},{25,17},{2,26},{10... | collective-permute-start | bytes 1572872 | tf_op jit(solution)/shard_map/ppermute | solution.py:18
  128.9 4.8 %collective-permute-done.32 = bf16[64,4096]{1,0:T(8,128)(2,1)S(1)} collective-permute-done((bf16[64,4096]{1,0:T(8,128)(2,1)S(1)}, bf16[64,4096]{1,0:T(8,128)(2,1)S(1)}, u32[]{:S(2)}, u32[]{:S(2)}) %collective-permute-start.32) | collective-permute-done | bytes 524320 | tf_op jit(solution)/shard_map/ppermute | solution.py:18
  134.1 3.6 %collective-permute-done.37 = bf16[64,4096]{1,0:T(8,128)(2,1)S(1)} collective-permute-done((bf16[64,4096]{1,0:T(8,128)(2,1)S(1)}, bf16[64,4096]{1,0:T(8,128)(2,1)S(1)}, u32[]{:S(2)}, u32[]{:S(2)}) %collective-permute-start.37) | collective-permute-done | bytes 524320 | tf_op jit(solution)/shard_map/ppermute | solution.py:18
  137.7 6.8 %ffn.6 = (bf16[128,4096]{1,0:T(8,128)(2,1)S(1)}, bf16[128,4096]{1,0:T(8,128)(2,1)S(1)}) custom-call(bf16[128,4096]{1,0:T(8,128)(2,1)S(1)} %get-tuple-element.77.refs_0_, bf16[128,4096]{1,0:T(8,128)(2,1)S(1)} %get-tuple-element.78.refs_1_, bf16[1792,4096]{1,0:T(8,128)(2,1)S(1)} %get-tuple-element.61.refs_4_.refs_2_, ...), custom_call_target="tpu_custom_call" | custom-call | flops 5637144576 | tf_op jit(solution)/shard_map/ffn/pallas_call | solution.py:209
  145.2 4.8 %collective-permute-done.38 = bf16[64,4096]{1,0:T(8,128)(2,1)S(1)} collective-permute-done((bf16[64,4096]{1,0:T(8,128)(2,1)S(1)}, bf16[64,4096]{1,0:T(8,128)(2,1)S(1)}, u32[]{:S(2)}, u32[]{:S(2)}) %collective-permute-start.38) | collective-permute-done | bytes 524320 | tf_op jit(solution)/shard_map/ppermute | solution.py:18
  151.3 3.1 %collective-permute-start.35 = (bf16[32,4096]{1,0:T(8,128)(2,1)S(1)}, bf16[32,4096]{1,0:T(8,128)(2,1)S(1)}, u32[]{:S(2)}, u32[]{:S(2)}) collective-permute-start(bf16[32,4096]{1,0:T(8,128)(2,1)S(1)} %get-tuple-element.104), channel_id=1, source_target_pairs={{0,16},{8,24},{16,0},{24,8},{1,17},{9,25},{17,1},{25,9},{2,18},{10... | collective-permute-start | bytes 786440 | tf_op jit(solution)/shard_map/ppermute | solution.py:18
  154.7 5.4 %collective-permute-start.43 = (bf16[32,4096]{1,0:T(8,128)(2,1)S(1)}, bf16[32,4096]{1,0:T(8,128)(2,1)S(1)}, u32[]{:S(2)}, u32[]{:S(2)}) collective-permute-start(bf16[32,4096]{1,0:T(8,128)(2,1)S(1)} %get-tuple-element.102), channel_id=1, source_target_pairs={{0,4},{2,6},{4,0},{6,2},{1,5},{3,7},{5,1},{7,3},{8,12},{10,14},{12... | collective-permute-start | bytes 786440 | tf_op jit(solution)/shard_map/ppermute | solution.py:18
  164.2 3.0 %collective-permute-done.43 = bf16[32,4096]{1,0:T(8,128)(2,1)S(1)} collective-permute-done((bf16[32,4096]{1,0:T(8,128)(2,1)S(1)}, bf16[32,4096]{1,0:T(8,128)(2,1)S(1)}, u32[]{:S(2)}, u32[]{:S(2)}) %collective-permute-start.43) | collective-permute-done | bytes 262176 | tf_op jit(solution)/shard_map/ppermute | solution.py:18
  168.2 6.2 %collective-permute-start.44 = (bf16[16,4096]{1,0:T(8,128)(2,1)S(1)}, bf16[16,4096]{1,0:T(8,128)(2,1)S(1)}, u32[]{:S(2)}, u32[]{:S(2)}) collective-permute-start(bf16[16,4096]{1,0:T(8,128)(2,1)S(1)} %get-tuple-element.113), channel_id=1, source_target_pairs={{0,64},{32,96},{64,0},{96,32},{1,65},{33,97},{65,1},{97,33},{2,66}... | collective-permute-start | bytes 393224 | tf_op jit(solution)/shard_map/ppermute | solution.py:18
  174.4 2.9 %collective-permute-done.44 = bf16[16,4096]{1,0:T(8,128)(2,1)S(1)} collective-permute-done((bf16[16,4096]{1,0:T(8,128)(2,1)S(1)}, bf16[16,4096]{1,0:T(8,128)(2,1)S(1)}, u32[]{:S(2)}, u32[]{:S(2)}) %collective-permute-start.44) | collective-permute-done | bytes 131104 | tf_op jit(solution)/shard_map/ppermute | solution.py:18
  177.3 3.2 %collective-permute-done.45 = bf16[16,4096]{1,0:T(8,128)(2,1)S(1)} collective-permute-done((bf16[16,4096]{1,0:T(8,128)(2,1)S(1)}, bf16[16,4096]{1,0:T(8,128)(2,1)S(1)}, u32[]{:S(2)}, u32[]{:S(2)}) %collective-permute-start.45) | collective-permute-done | bytes 131104 | tf_op jit(solution)/shard_map/ppermute | solution.py:18
  (106 shorter events, 36.5 us)
Async XLA Ops:
  13.0 61.7 %collective-permute-start.18 = (bf16[448,4096]{1,0:T(8,128)(2,1)S(1)}, bf16[448,4096]{1,0:T(8,128)(2,1)S(1)}, u32[]{:S(2)}, u32[]{:S(2)}) collective-permute-start(bf16[448,4096]{1,0:T(8,128)(2,1)S(1)} %get-tuple-element.55), channel_id=1, source_target_pairs={{0,1},{1,0},{2,3},{3,2},{4,5},{5,4},{6,7},{7,6},{8,9},{9,8},{10,11... | collective-permute-start | bytes 11010056 | tf_op jit(solution)/shard_map/ppermute | solution.py:22
  13.0 63.6 %collective-permute-start.19 = (bf16[448,4096]{1,0:T(8,128)(2,1)S(1)}, bf16[448,4096]{1,0:T(8,128)(2,1)S(1)}, u32[]{:S(2)}, u32[]{:S(2)}) collective-permute-start(bf16[448,4096]{1,0:T(8,128)(2,1)S(1)} %get-tuple-element.56), channel_id=1, source_target_pairs={{0,1},{1,0},{2,3},{3,2},{4,5},{5,4},{6,7},{7,6},{8,9},{9,8},{10,11... | collective-permute-start | bytes 11010056 | tf_op jit(solution)/shard_map/ppermute | solution.py:22
  13.5 63.1 %collective-permute-start.20 = (bf16[448,4096]{1,0:T(8,128)(2,1)S(1)}, bf16[448,4096]{1,0:T(8,128)(2,1)S(1)}, u32[]{:S(2)}, u32[]{:S(2)}) collective-permute-start(bf16[448,4096]{1,0:T(8,128)(2,1)S(1)} %get-tuple-element.57), channel_id=1, source_target_pairs={{0,1},{1,0},{2,3},{3,2},{4,5},{5,4},{6,7},{7,6},{8,9},{9,8},{10,11... | collective-permute-start | bytes 11010056 | tf_op jit(solution)/shard_map/ppermute | solution.py:22
  13.7 14.1 %collective-permute-start.11 = (bf16[32,4096]{1,0:T(8,128)(2,1)S(1)}, bf16[32,4096]{1,0:T(8,128)(2,1)S(1)}, u32[]{:S(2)}, u32[]{:S(2)}) collective-permute-start(bf16[32,4096]{1,0:T(8,128)(2,1)S(1)} %get-tuple-element.137), channel_id=1, source_target_pairs={{0,2},{2,4},{4,6},{6,0},{1,3},{3,5},{5,7},{7,1},{8,10},{10,12},{12... | collective-permute-start | bytes 786440 | tf_op jit(solution)/shard_map/ppermute | solution.py:18
  25.4 13.2 %collective-permute-start.14 = (bf16[32,4096]{1,0:T(8,128)(2,1)S(1)}, bf16[32,4096]{1,0:T(8,128)(2,1)S(1)}, u32[]{:S(2)}, u32[]{:S(2)}) collective-permute-start(bf16[32,4096]{1,0:T(8,128)(2,1)S(1)} %get-tuple-element.137), channel_id=1, source_target_pairs={{0,6},{2,0},{4,2},{6,4},{1,7},{3,1},{5,3},{7,5},{8,14},{10,8},{12,... | collective-permute-start | bytes 786440 | tf_op jit(solution)/shard_map/ppermute | solution.py:18
  27.8 12.4 %collective-permute-start.15 = (bf16[32,4096]{1,0:T(8,128)(2,1)S(1)}, bf16[32,4096]{1,0:T(8,128)(2,1)S(1)}, u32[]{:S(2)}, u32[]{:S(2)}) collective-permute-start(bf16[32,4096]{1,0:T(8,128)(2,1)S(1)} %get-tuple-element.137), channel_id=1, source_target_pairs={{0,4},{2,6},{4,0},{6,2},{1,5},{3,7},{5,1},{7,3},{8,12},{10,14},{12... | collective-permute-start | bytes 786440 | tf_op jit(solution)/shard_map/ppermute | solution.py:18
  50.9 11.7 %collective-permute-start.12 = (bf16[64,4096]{1,0:T(8,128)(2,1)S(1)}, bf16[64,4096]{1,0:T(8,128)(2,1)S(1)}, u32[]{:S(2)}, u32[]{:S(2)}) collective-permute-start(bf16[64,4096]{1,0:T(8,128)(2,1)S(1)} %get-tuple-element.119), channel_id=1, source_target_pairs={{0,8},{8,16},{16,24},{24,0},{1,9},{9,17},{17,25},{25,1},{2,10},{10... | collective-permute-start | bytes 1572872 | tf_op jit(solution)/shard_map/ppermute | solution.py:18
  57.8 12.7 %collective-permute-start.7 = (bf16[64,4096]{1,0:T(8,128)(2,1)S(1)}, bf16[64,4096]{1,0:T(8,128)(2,1)S(1)}, u32[]{:S(2)}, u32[]{:S(2)}) collective-permute-start(bf16[64,4096]{1,0:T(8,128)(2,1)S(1)} %get-tuple-element.121), channel_id=1, source_target_pairs={{0,6},{2,0},{4,2},{6,4},{1,7},{3,1},{5,3},{7,5},{8,14},{10,8},{12,... | collective-permute-start | bytes 1572872 | tf_op jit(solution)/shard_map/ppermute | solution.py:18
  62.6 11.6 %collective-permute-start.3 = (bf16[64,4096]{1,0:T(8,128)(2,1)S(1)}, bf16[64,4096]{1,0:T(8,128)(2,1)S(1)}, u32[]{:S(2)}, u32[]{:S(2)}) collective-permute-start(bf16[64,4096]{1,0:T(8,128)(2,1)S(1)} %pad_maximum_fusion), channel_id=1, source_target_pairs={{0,2},{2,4},{4,6},{6,0},{1,3},{3,5},{5,7},{7,1},{8,10},{10,12},{12... | collective-permute-start | bytes 1572872 | tf_op jit(solution)/shard_map/ppermute | solution.py:18
  70.5 14.2 %collective-permute-start.17 = (bf16[64,4096]{1,0:T(8,128)(2,1)S(1)}, bf16[64,4096]{1,0:T(8,128)(2,1)S(1)}, u32[]{:S(2)}, u32[]{:S(2)}) collective-permute-start(bf16[64,4096]{1,0:T(8,128)(2,1)S(1)} %collective-permute-done.16.refs_3_), channel_id=1, source_target_pairs={{0,24},{8,0},{16,8},{24,16},{1,25},{9,1},{17,9},{25,17},{2,26},{10... | collective-permute-start | bytes 1572872 | tf_op jit(solution)/shard_map/ppermute | solution.py:18
  74.2 16.0 %collective-permute-start.13 = (bf16[64,4096]{1,0:T(8,128)(2,1)S(1)}, bf16[64,4096]{1,0:T(8,128)(2,1)S(1)}, u32[]{:S(2)}, u32[]{:S(2)}) collective-permute-start(bf16[64,4096]{1,0:T(8,128)(2,1)S(1)} %collective-permute-done.12.refs_2_), channel_id=1, source_target_pairs={{0,8},{8,16},{16,24},{24,0},{1,9},{9,17},{17,25},{25,1},{2,10},{10... | collective-permute-start | bytes 1572872 | tf_op jit(solution)/shard_map/ppermute | solution.py:18
  74.6 17.3 %collective-permute-start.8 = (bf16[64,4096]{1,0:T(8,128)(2,1)S(1)}, bf16[64,4096]{1,0:T(8,128)(2,1)S(1)}, u32[]{:S(2)}, u32[]{:S(2)}) collective-permute-start(bf16[64,4096]{1,0:T(8,128)(2,1)S(1)} %collective-permute-done.7.refs_1_), channel_id=1, source_target_pairs={{0,6},{2,0},{4,2},{6,4},{1,7},{3,1},{5,3},{7,5},{8,14},{10,8},{12,... | collective-permute-start | bytes 1572872 | tf_op jit(solution)/shard_map/ppermute | solution.py:18
  76.7 16.8 %collective-permute-start.4 = (bf16[64,4096]{1,0:T(8,128)(2,1)S(1)}, bf16[64,4096]{1,0:T(8,128)(2,1)S(1)}, u32[]{:S(2)}, u32[]{:S(2)}) collective-permute-start(bf16[64,4096]{1,0:T(8,128)(2,1)S(1)} %collective-permute-done.3.refs_0_), channel_id=1, source_target_pairs={{0,2},{2,4},{4,6},{6,0},{1,3},{3,5},{5,7},{7,1},{8,10},{10,12},{12... | collective-permute-start | bytes 1572872 | tf_op jit(solution)/shard_map/ppermute | solution.py:18
  76.7 23.7 %collective-permute-start.25 = (bf16[64,4096]{1,0:T(8,128)(2,1)S(1)}, bf16[64,4096]{1,0:T(8,128)(2,1)S(1)}, u32[]{:S(2)}, u32[]{:S(2)}) collective-permute-start(bf16[64,4096]{1,0:T(8,128)(2,1)S(1)} %get-tuple-element.115), channel_id=1, source_target_pairs={{0,8},{8,16},{16,24},{24,0},{1,9},{9,17},{17,25},{25,1},{2,10},{10... | collective-permute-start | bytes 1572872 | tf_op jit(solution)/shard_map/ppermute | solution.py:18
  84.7 17.7 %collective-permute-start.26 = (bf16[64,4096]{1,0:T(8,128)(2,1)S(1)}, bf16[64,4096]{1,0:T(8,128)(2,1)S(1)}, u32[]{:S(2)}, u32[]{:S(2)}) collective-permute-start(bf16[64,4096]{1,0:T(8,128)(2,1)S(1)} %get-tuple-element.119), channel_id=1, source_target_pairs={{0,24},{8,0},{16,8},{24,16},{1,25},{9,1},{17,9},{25,17},{2,26},{10... | collective-permute-start | bytes 1572872 | tf_op jit(solution)/shard_map/ppermute | solution.py:18
  90.2 12.9 %collective-permute-start.23 = (bf16[64,4096]{1,0:T(8,128)(2,1)S(1)}, bf16[64,4096]{1,0:T(8,128)(2,1)S(1)}, u32[]{:S(2)}, u32[]{:S(2)}) collective-permute-start(bf16[64,4096]{1,0:T(8,128)(2,1)S(1)} %get-tuple-element.121), channel_id=1, source_target_pairs={{0,2},{2,4},{4,6},{6,0},{1,3},{3,5},{5,7},{7,1},{8,10},{10,12},{12... | collective-permute-start | bytes 1572872 | tf_op jit(solution)/shard_map/ppermute | solution.py:18
  91.9 13.2 %collective-permute-start.24 = (bf16[64,4096]{1,0:T(8,128)(2,1)S(1)}, bf16[64,4096]{1,0:T(8,128)(2,1)S(1)}, u32[]{:S(2)}, u32[]{:S(2)}) collective-permute-start(bf16[64,4096]{1,0:T(8,128)(2,1)S(1)} %pad_maximum_fusion), channel_id=1, source_target_pairs={{0,6},{2,0},{4,2},{6,4},{1,7},{3,1},{5,3},{7,5},{8,14},{10,8},{12,... | collective-permute-start | bytes 1572872 | tf_op jit(solution)/shard_map/ppermute | solution.py:18
  100.3 18.9 %collective-permute-start.28 = (bf16[64,4096]{1,0:T(8,128)(2,1)S(1)}, bf16[64,4096]{1,0:T(8,128)(2,1)S(1)}, u32[]{:S(2)}, u32[]{:S(2)}) collective-permute-start(bf16[64,4096]{1,0:T(8,128)(2,1)S(1)} %get-tuple-element.81), channel_id=1, source_target_pairs={{0,6},{2,0},{4,2},{6,4},{1,7},{3,1},{5,3},{7,5},{8,14},{10,8},{12,... | collective-permute-start | bytes 1572872 | tf_op jit(solution)/shard_map/ppermute | solution.py:18
  100.4 22.6 %collective-permute-start.29 = (bf16[64,4096]{1,0:T(8,128)(2,1)S(1)}, bf16[64,4096]{1,0:T(8,128)(2,1)S(1)}, u32[]{:S(2)}, u32[]{:S(2)}) collective-permute-start(bf16[64,4096]{1,0:T(8,128)(2,1)S(1)} %get-tuple-element.82), channel_id=1, source_target_pairs={{0,2},{2,4},{4,6},{6,0},{1,3},{3,5},{5,7},{7,1},{8,10},{10,12},{12... | collective-permute-start | bytes 1572872 | tf_op jit(solution)/shard_map/ppermute | solution.py:18
  102.4 20.7 %collective-permute-start.21 = (bf16[64,4096]{1,0:T(8,128)(2,1)S(1)}, bf16[64,4096]{1,0:T(8,128)(2,1)S(1)}, u32[]{:S(2)}, u32[]{:S(2)}) collective-permute-start(bf16[64,4096]{1,0:T(8,128)(2,1)S(1)} %get-tuple-element.67), channel_id=1, source_target_pairs={{0,24},{8,0},{16,8},{24,16},{1,25},{9,1},{17,9},{25,17},{2,26},{10... | collective-permute-start | bytes 1572872 | tf_op jit(solution)/shard_map/ppermute | solution.py:18
  103.1 23.3 %collective-permute-start.22 = (bf16[64,4096]{1,0:T(8,128)(2,1)S(1)}, bf16[64,4096]{1,0:T(8,128)(2,1)S(1)}, u32[]{:S(2)}, u32[]{:S(2)}) collective-permute-start(bf16[64,4096]{1,0:T(8,128)(2,1)S(1)} %get-tuple-element.68), channel_id=1, source_target_pairs={{0,8},{8,16},{16,24},{24,0},{1,9},{9,17},{17,25},{25,1},{2,10},{10... | collective-permute-start | bytes 1572872 | tf_op jit(solution)/shard_map/ppermute | solution.py:18
  112.0 16.8 %collective-permute-start.27 = (bf16[64,4096]{1,0:T(8,128)(2,1)S(1)}, bf16[64,4096]{1,0:T(8,128)(2,1)S(1)}, u32[]{:S(2)}, u32[]{:S(2)}) collective-permute-start(bf16[64,4096]{1,0:T(8,128)(2,1)S(1)} %get-tuple-element.80), channel_id=1, source_target_pairs={{0,2},{2,4},{4,6},{6,0},{1,3},{3,5},{5,7},{7,1},{8,10},{10,12},{12... | collective-permute-start | bytes 1572872 | tf_op jit(solution)/shard_map/ppermute | solution.py:18
  119.2 14.6 %collective-permute-start.32 = (bf16[64,4096]{1,0:T(8,128)(2,1)S(1)}, bf16[64,4096]{1,0:T(8,128)(2,1)S(1)}, u32[]{:S(2)}, u32[]{:S(2)}) collective-permute-start(bf16[64,4096]{1,0:T(8,128)(2,1)S(1)} %get-tuple-element.87), channel_id=1, source_target_pairs={{0,6},{2,0},{4,2},{6,4},{1,7},{3,1},{5,3},{7,5},{8,14},{10,8},{12,... | collective-permute-start | bytes 1572872 | tf_op jit(solution)/shard_map/ppermute | solution.py:18
  123.0 14.7 %collective-permute-start.37 = (bf16[64,4096]{1,0:T(8,128)(2,1)S(1)}, bf16[64,4096]{1,0:T(8,128)(2,1)S(1)}, u32[]{:S(2)}, u32[]{:S(2)}) collective-permute-start(bf16[64,4096]{1,0:T(8,128)(2,1)S(1)} %get-tuple-element.91), channel_id=1, source_target_pairs={{0,8},{8,16},{16,24},{24,0},{1,9},{9,17},{17,25},{25,1},{2,10},{10... | collective-permute-start | bytes 1572872 | tf_op jit(solution)/shard_map/ppermute | solution.py:18
  123.1 21.4 %collective-permute-start.40 = (bf16[64,4096]{1,0:T(8,128)(2,1)S(1)}, bf16[64,4096]{1,0:T(8,128)(2,1)S(1)}, u32[]{:S(2)}, u32[]{:S(2)}) collective-permute-start(bf16[64,4096]{1,0:T(8,128)(2,1)S(1)} %get-tuple-element.94), channel_id=1, source_target_pairs={{0,24},{8,0},{16,8},{24,16},{1,25},{9,1},{17,9},{25,17},{2,26},{10... | collective-permute-start | bytes 1572872 | tf_op jit(solution)/shard_map/ppermute | solution.py:18
  126.4 18.1 %collective-permute-start.30 = (bf16[64,4096]{1,0:T(8,128)(2,1)S(1)}, bf16[64,4096]{1,0:T(8,128)(2,1)S(1)}, u32[]{:S(2)}, u32[]{:S(2)}) collective-permute-start(bf16[64,4096]{1,0:T(8,128)(2,1)S(1)} %add_convert_fusion.7), channel_id=1, source_target_pairs={{0,6},{2,0},{4,2},{6,4},{1,7},{3,1},{5,3},{7,5},{8,14},{10,8},{12,... | collective-permute-start | bytes 1572872 | tf_op jit(solution)/shard_map/ppermute | solution.py:18
  128.8 15.7 %collective-permute-start.33 = (bf16[64,4096]{1,0:T(8,128)(2,1)S(1)}, bf16[64,4096]{1,0:T(8,128)(2,1)S(1)}, u32[]{:S(2)}, u32[]{:S(2)}) collective-permute-start(bf16[64,4096]{1,0:T(8,128)(2,1)S(1)} %add_convert_fusion.5), channel_id=1, source_target_pairs={{0,2},{2,4},{4,6},{6,0},{1,3},{3,5},{5,7},{7,1},{8,10},{10,12},{12... | collective-permute-start | bytes 1572872 | tf_op jit(solution)/shard_map/ppermute | solution.py:18
  133.8 11.4 %collective-permute-start.41 = (bf16[64,4096]{1,0:T(8,128)(2,1)S(1)}, bf16[64,4096]{1,0:T(8,128)(2,1)S(1)}, u32[]{:S(2)}, u32[]{:S(2)}) collective-permute-start(bf16[64,4096]{1,0:T(8,128)(2,1)S(1)} %add_convert_fusion.1), channel_id=1, source_target_pairs={{0,8},{8,16},{16,24},{24,0},{1,9},{9,17},{17,25},{25,1},{2,10},{10... | collective-permute-start | bytes 1572872 | tf_op jit(solution)/shard_map/ppermute | solution.py:18
  137.7 12.3 %collective-permute-start.38 = (bf16[64,4096]{1,0:T(8,128)(2,1)S(1)}, bf16[64,4096]{1,0:T(8,128)(2,1)S(1)}, u32[]{:S(2)}, u32[]{:S(2)}) collective-permute-start(bf16[64,4096]{1,0:T(8,128)(2,1)S(1)} %add_convert_fusion.3), channel_id=1, source_target_pairs={{0,24},{8,0},{16,8},{24,16},{1,25},{9,1},{17,9},{25,17},{2,26},{10... | collective-permute-start | bytes 1572872 | tf_op jit(solution)/shard_map/ppermute | solution.py:18
  151.3 11.0 %collective-permute-start.35 = (bf16[32,4096]{1,0:T(8,128)(2,1)S(1)}, bf16[32,4096]{1,0:T(8,128)(2,1)S(1)}, u32[]{:S(2)}, u32[]{:S(2)}) collective-permute-start(bf16[32,4096]{1,0:T(8,128)(2,1)S(1)} %get-tuple-element.104), channel_id=1, source_target_pairs={{0,16},{8,24},{16,0},{24,8},{1,17},{9,25},{17,1},{25,9},{2,18},{10... | collective-permute-start | bytes 786440 | tf_op jit(solution)/shard_map/ppermute | solution.py:18
  154.7 12.5 %collective-permute-start.43 = (bf16[32,4096]{1,0:T(8,128)(2,1)S(1)}, bf16[32,4096]{1,0:T(8,128)(2,1)S(1)}, u32[]{:S(2)}, u32[]{:S(2)}) collective-permute-start(bf16[32,4096]{1,0:T(8,128)(2,1)S(1)} %get-tuple-element.102), channel_id=1, source_target_pairs={{0,4},{2,6},{4,0},{6,2},{1,5},{3,7},{5,1},{7,3},{8,12},{10,14},{12... | collective-permute-start | bytes 786440 | tf_op jit(solution)/shard_map/ppermute | solution.py:18
  162.7 11.7 %collective-permute-start.36 = (bf16[16,4096]{1,0:T(8,128)(2,1)S(1)}, bf16[16,4096]{1,0:T(8,128)(2,1)S(1)}, u32[]{:S(2)}, u32[]{:S(2)}) collective-permute-start(bf16[16,4096]{1,0:T(8,128)(2,1)S(1)} %slice.153), channel_id=1, source_target_pairs={{0,96},{32,0},{64,32},{96,64},{1,97},{33,1},{65,33},{97,65},{2,98}... | collective-permute-start | bytes 393224 | tf_op jit(solution)/shard_map/ppermute | solution.py:18
  (15 other events, 118.2 us)

commit v3 on v2

--- a/solution.py
+++ b/solution.py
@@ -225,8 +225,10 @@
 
 
 def ring_gather(v, axis):
-    far, plus, minus = [shift(v, axis, step) for step in (2, 1, -1)]
-    return jnp.concatenate([v, plus, minus, far], axis=0)
+    half = v.shape[0] // 2
+    plus, minus = shift(v, axis, 1), shift(v, axis, -1)
+    plus2, minus2 = shift(plus[:half], axis, 1), shift(minus[half:], axis, -1)
+    return jnp.concatenate([v, plus, minus, plus2, minus2], axis=0)
 
 
 def add(*terms):
@@ -305,6 +307,7 @@
     rest_a, rest_b = second_halves(a0, "z"), second_halves(b0, "x")
     (a0, b0), peers = after([a0, b0], peers)
     w1, w2 = load(core_arg, w_gate, peers[0], w_up, peers[1], w_down, peers[2])
+    (w1, w2), lead_a, lead_b = after([w1, w2], lead_a, lead_b)
     far_a, far_b = onward(lead_a, "z"), onward(lead_b, "x")
     early = ffn(rest_a + rest_b, w1, w2)
     early_a, early_b = backward(early[:2], "z"), backward(early[2:], "x")
@@ -316,7 +319,7 @@
     far_b, late_b, (a0, b0) = after(far_b, late[2:], [a0, b0])
     late_a = backward([add(v, w) for v, w in zip(late_a, far_a)], "z")
     late_b = backward([add(v, w) for v, w in zip(late_b, far_b)], "x")
-    y0 = ffn([a0, b0], w1, w2)
+    y0 = ffn([a0, b0], w1, w2, looped=True)
     ya = collect(y0[0], early_a, late_a)
     yb = collect(y0[1], early_b, late_b)
     done_a = ring_scatter(ya, "x")

time: 184 us -> 191 us (1.038)
  waiting for transfers between devices: 71 us -> 94 us
  starting transfers between devices: 70.8 us -> 53.3 us
    ppermute x42 -> x44, waiting for transfers between devices: 68 us -> 91 us  [shift(): return lax.ppermute(v, axis, [(i, (i + step) % RING) for i in range(RING)])]
    ppermute x42 -> x44, starting transfers between devices: 70 us -> 52.5 us  [shift(): return lax.ppermute(v, axis, [(i, (i + step) % RING) for i in range(RING)])]
  transfers between devices with their start and end apart: 47 -> 49, of which waited for: 21 -> 25; matrix products, arithmetic and copies ran while one was open for 1% -> 1% of each run, Pallas kernels for 20% -> 20%
where the time goes in v3:
time: 191 us; the launch traced here: 190 us
  waiting for transfers between devices  94 us (49%)
  starting transfers between devices  53.3 us (28%)
  Pallas kernels  39 us (20%)
  other arithmetic  1.99 us (1%)
    ppermute x44, waiting for transfers between devices, shift(): return lax.ppermute(v, axis, [(i, (i + step) % RING) for i in range(RING)])  91 us
    ppermute x44, starting transfers between devices, shift(): return lax.ppermute(v, axis, [(i, (i + step) % RING) for i in range(RING)])  52.5 us
    pallas_call x4, Pallas kernels, ffn(): pl.pallas_call(functools.partial(ffn_kernel, rows, looped), out_shape=[pl...  29 us
    pallas_call x1, Pallas kernels, load(): pl.pallas_call(load_kernel, out_shape=[pltpu.VMEM((2 * CORES * part, widt...  4.38 us
    pallas_call x1, Pallas kernels, pick(): pl.pallas_call(pick_kernel, out_shape=[pltpu.VMEM(w.shape[1:], BF16) for...  4.23 us
  transfers between devices with their start and end apart: 49, of which 25 were waited for; matrix products, arithmetic and copies ran while one was open for 1% of the time, Pallas kernels for 20%

profile of v3, /device:TPU:0, one launch (start us, length us, event | category | flops | bytes accessed | tf_op | source)
XLA Modules:
  0.0 190.3 jit_solution(4855638167295138772)
XLA Ops:
  4.9 3.0 %collective-permute-start.6 = (bf16[16,4096]{1,0:T(8,128)(2,1)S(1)}, bf16[16,4096]{1,0:T(8,128)(2,1)S(1)}, u32[]{:S(2)}, u32[]{:S(2)}) collective-permute-start(bf16[16,4096]{1,0:T(8,128)(2,1)S(1)} %pad_maximum_fusion.4), channel_id=1, source_target_pairs={{0,64},{32,96},{64,0},{96,32},{1,65},{33,97},{65,1},{97,33},{2,66}... | collective-permute-start | bytes 393224 | tf_op jit(solution)/shard_map/ppermute | solution.py:18
  9.3 4.2 %pick.1 = (bf16[448,4096]{1,0:T(8,128)(2,1)S(1)}, bf16[448,4096]{1,0:T(8,128)(2,1)S(1)}, bf16[448,4096]{1,0:T(8,128)(2,1)S(1)}) custom-call(s32[1]{0:T(128)S(6)} %sub.3.which_ref, bf16[2,448,4096]{2,1,0:T(8,128)(2,1)} %bitcast.6, bf16[2,448,4096]{2,1,0:T(8,128)(2,1)} %bitcast.8, bf16[2,448,4096]{2,1,0:T(8,128)(2,1)} %wd.3), custom_call_target="tpu_custom_call" | custom-call | tf_op jit(solution)/shard_map/pick/pallas_call | solution.py:126
  14.3 2.8 %collective-permute-start.3 = (bf16[32,4096]{1,0:T(8,128)(2,1)S(1)}, bf16[32,4096]{1,0:T(8,128)(2,1)S(1)}, u32[]{:S(2)}, u32[]{:S(2)}) collective-permute-start(bf16[32,4096]{1,0:T(8,128)(2,1)S(1)} %pad_maximum_fusion.1), channel_id=1, source_target_pairs={{0,24},{8,0},{16,8},{24,16},{1,25},{9,1},{17,9},{25,17},{2,26},{10... | collective-permute-start | bytes 786440 | tf_op jit(solution)/shard_map/ppermute | solution.py:18
  17.3 9.5 %collective-permute-done.2 = bf16[32,4096]{1,0:T(8,128)(2,1)S(1)} collective-permute-done((bf16[32,4096]{1,0:T(8,128)(2,1)S(1)}, bf16[32,4096]{1,0:T(8,128)(2,1)S(1)}, u32[]{:S(2)}, u32[]{:S(2)}) %collective-permute-start.2) | collective-permute-done | bytes 262176 | tf_op jit(solution)/shard_map/ppermute | solution.py:18
  26.8 4.0 %collective-permute-start.9 = (bf16[32,4096]{1,0:T(8,128)(2,1)S(1)}, bf16[32,4096]{1,0:T(8,128)(2,1)S(1)}, u32[]{:S(2)}, u32[]{:S(2)}) collective-permute-start(bf16[32,4096]{1,0:T(8,128)(2,1)S(1)} %get-tuple-element.149), channel_id=1, source_target_pairs={{0,6},{2,0},{4,2},{6,4},{1,7},{3,1},{5,3},{7,5},{8,14},{10,8},{12,... | collective-permute-start | bytes 786440 | tf_op jit(solution)/shard_map/ppermute | solution.py:18
  31.1 8.3 %collective-permute-done.8 = bf16[32,4096]{1,0:T(8,128)(2,1)S(1)} collective-permute-done((bf16[32,4096]{1,0:T(8,128)(2,1)S(1)}, bf16[32,4096]{1,0:T(8,128)(2,1)S(1)}, u32[]{:S(2)}, u32[]{:S(2)}) %collective-permute-start.8) | collective-permute-done | bytes 262176 | tf_op jit(solution)/shard_map/ppermute | solution.py:18
  39.4 3.3 %collective-permute-start.5 = (bf16[16,4096]{1,0:T(8,128)(2,1)S(1)}, bf16[16,4096]{1,0:T(8,128)(2,1)S(1)}, u32[]{:S(2)}, u32[]{:S(2)}) collective-permute-start(bf16[16,4096]{1,0:T(8,128)(2,1)S(1)} %slice.165), channel_id=1, source_target_pairs={{0,24},{8,0},{16,8},{24,16},{1,25},{9,1},{17,9},{25,17},{2,26},{10... | collective-permute-start | bytes 393224 | tf_op jit(solution)/shard_map/ppermute | solution.py:18
  42.8 2.7 %collective-permute-done.4 = bf16[16,4096]{1,0:T(8,128)(2,1)S(1)} collective-permute-done((bf16[16,4096]{1,0:T(8,128)(2,1)S(1)}, bf16[16,4096]{1,0:T(8,128)(2,1)S(1)}, u32[]{:S(2)}, u32[]{:S(2)}) %collective-permute-start.4) | collective-permute-done | bytes 131104 | tf_op jit(solution)/shard_map/ppermute | solution.py:18
  45.6 7.5 %collective-permute-done.10 = bf16[16,4096]{1,0:T(8,128)(2,1)S(1)} collective-permute-done((bf16[16,4096]{1,0:T(8,128)(2,1)S(1)}, bf16[16,4096]{1,0:T(8,128)(2,1)S(1)}, u32[]{:S(2)}, u32[]{:S(2)}) %collective-permute-start.10) | collective-permute-done | bytes 131104 | tf_op jit(solution)/shard_map/ppermute | solution.py:18
  53.1 4.9 %collective-permute-done.11 = bf16[16,4096]{1,0:T(8,128)(2,1)S(1)} collective-permute-done((bf16[16,4096]{1,0:T(8,128)(2,1)S(1)}, bf16[16,4096]{1,0:T(8,128)(2,1)S(1)}, u32[]{:S(2)}, u32[]{:S(2)}) %collective-permute-start.11) | collective-permute-done | bytes 131104 | tf_op jit(solution)/shard_map/ppermute | solution.py:18
  58.1 2.3 %collective-permute-done.15.refs_0_ = bf16[64,4096]{1,0:T(8,128)(2,1)S(1)} collective-permute-done((bf16[64,4096]{1,0:T(8,128)(2,1)S(1)}, bf16[64,4096]{1,0:T(8,128)(2,1)S(1)}, u32[]{:S(2)}, u32[]{:S(2)}) %collective-permute-start.15) | collective-permute-done | bytes 524320 | tf_op jit(solution)/shard_map/ppermute | solution.py:18
  60.8 7.7 %collective-permute-done.17.refs_2_ = bf16[64,4096]{1,0:T(8,128)(2,1)S(1)} collective-permute-done((bf16[64,4096]{1,0:T(8,128)(2,1)S(1)}, bf16[64,4096]{1,0:T(8,128)(2,1)S(1)}, u32[]{:S(2)}, u32[]{:S(2)}) %collective-permute-start.17) | collective-permute-done | bytes 524320 | tf_op jit(solution)/shard_map/ppermute | solution.py:18
  68.5 3.9 %collective-permute-done.16.refs_1_ = bf16[64,4096]{1,0:T(8,128)(2,1)S(1)} collective-permute-done((bf16[64,4096]{1,0:T(8,128)(2,1)S(1)}, bf16[64,4096]{1,0:T(8,128)(2,1)S(1)}, u32[]{:S(2)}, u32[]{:S(2)}) %collective-permute-start.16) | collective-permute-done | bytes 524320 | tf_op jit(solution)/shard_map/ppermute | solution.py:18
  76.4 4.4 %load.1 = (bf16[1792,4096]{1,0:T(8,128)(2,1)S(1)}, bf16[896,4096]{1,0:T(8,128)(2,1)S(1)}) custom-call(s32[1]{0:T(128)} %bitcast.1.core_ref, bf16[2,448,4096]{2,1,0:T(8,128)(2,1)} %bitcast.7, bf16[448,4096]{1,0:T(8,128)(2,1)S(1)} %collective-permute-done.12.wpg, bf16[2,448,4096]{2,1,0:T(8,128)(2,1)} %bitcast.9, ...), custom_call_target="tpu_custom_call" | custom-call | tf_op jit(solution)/shard_map/load/pallas_call | solution.py:154
  80.8 2.2 %collective-permute-done.18.refs_3_ = bf16[64,4096]{1,0:T(8,128)(2,1)S(1)} collective-permute-done((bf16[64,4096]{1,0:T(8,128)(2,1)S(1)}, bf16[64,4096]{1,0:T(8,128)(2,1)S(1)}, u32[]{:S(2)}, u32[]{:S(2)}) %collective-permute-start.18) | collective-permute-done | bytes 524320 | tf_op jit(solution)/shard_map/ppermute | solution.py:18
  86.2 5.6 %collective-permute-done.28.refs_3_ = bf16[64,4096]{1,0:T(8,128)(2,1)S(1)} collective-permute-done((bf16[64,4096]{1,0:T(8,128)(2,1)S(1)}, bf16[64,4096]{1,0:T(8,128)(2,1)S(1)}, u32[]{:S(2)}, u32[]{:S(2)}) %collective-permute-start.28) | collective-permute-done | bytes 524320 | tf_op jit(solution)/shard_map/ppermute | solution.py:18
  91.8 3.2 %collective-permute-start.22 = (bf16[64,4096]{1,0:T(8,128)(2,1)S(1)}, bf16[64,4096]{1,0:T(8,128)(2,1)S(1)}, u32[]{:S(2)}, u32[]{:S(2)}) collective-permute-start(bf16[64,4096]{1,0:T(8,128)(2,1)S(1)} %collective-permute-done.18.refs_3_), channel_id=1, source_target_pairs={{0,24},{8,0},{16,8},{24,16},{1,25},{9,1},{17,9},{25,17},{2,26},{10... | collective-permute-start | bytes 1572872 | tf_op jit(solution)/shard_map/ppermute | solution.py:18
  95.0 6.8 %ffn.7 = (bf16[64,4096]{1,0:T(8,128)(2,1)S(1)}, bf16[64,4096]{1,0:T(8,128)(2,1)S(1)}, bf16[64,4096]{1,0:T(8,128)(2,1)S(1)}, bf16[64,4096]{1,0:T(8,128)(2,1)S(1)}) custom-call(bf16[64,4096]{1,0:T(8,128)(2,1)S(1)} %collective-permute-done.25.refs_0_, bf16[64,4096]{1,0:T(8,128)(2,1)S(1)} %collective-permute-done.26.refs_1_, ...), custom_call_target="tpu_custom_call" | custom-call | flops 5637144576 | tf_op jit(solution)/shard_map/ffn/pallas_call | solution.py:209
  102.0 3.2 %collective-permute-start.42 = (bf16[64,4096]{1,0:T(8,128)(2,1)S(1)}, bf16[64,4096]{1,0:T(8,128)(2,1)S(1)}, u32[]{:S(2)}, u32[]{:S(2)}) collective-permute-start(bf16[64,4096]{1,0:T(8,128)(2,1)S(1)} %get-tuple-element.106), channel_id=1, source_target_pairs={{0,24},{8,0},{16,8},{24,16},{1,25},{9,1},{17,9},{25,17},{2,26},{10... | collective-permute-start | bytes 1572872 | tf_op jit(solution)/shard_map/ppermute | solution.py:18
  107.8 6.9 %ffn.4 = (bf16[64,4096]{1,0:T(8,128)(2,1)S(1)}, bf16[64,4096]{1,0:T(8,128)(2,1)S(1)}, bf16[64,4096]{1,0:T(8,128)(2,1)S(1)}, bf16[64,4096]{1,0:T(8,128)(2,1)S(1)}) custom-call(bf16[64,4096]{1,0:T(8,128)(2,1)S(1)} %collective-permute-done.19.refs_0_, bf16[64,4096]{1,0:T(8,128)(2,1)S(1)} %collective-permute-done.20.refs_1_, ...), custom_call_target="tpu_custom_call" | custom-call | flops 5637144576 | tf_op jit(solution)/shard_map/ffn/pallas_call | solution.py:209
  114.7 3.3 %collective-permute-start.23 = (bf16[64,4096]{1,0:T(8,128)(2,1)S(1)}, bf16[64,4096]{1,0:T(8,128)(2,1)S(1)}, u32[]{:S(2)}, u32[]{:S(2)}) collective-permute-start(bf16[64,4096]{1,0:T(8,128)(2,1)S(1)} %get-tuple-element.79), channel_id=1, source_target_pairs={{0,24},{8,0},{16,8},{24,16},{1,25},{9,1},{17,9},{25,17},{2,26},{10... | collective-permute-start | bytes 1572872 | tf_op jit(solution)/shard_map/ppermute | solution.py:18
  118.0 6.9 %ffn.5 = (bf16[64,4096]{1,0:T(8,128)(2,1)S(1)}, bf16[64,4096]{1,0:T(8,128)(2,1)S(1)}, bf16[64,4096]{1,0:T(8,128)(2,1)S(1)}, bf16[64,4096]{1,0:T(8,128)(2,1)S(1)}) custom-call(bf16[64,4096]{1,0:T(8,128)(2,1)S(1)} %collective-permute-done.15.refs_0_, bf16[64,4096]{1,0:T(8,128)(2,1)S(1)} %collective-permute-done.16.refs_1_, ...), custom_call_target="tpu_custom_call" | custom-call | flops 5637144576 | tf_op jit(solution)/shard_map/ffn/pallas_call | solution.py:209
  125.9 2.5 %collective-permute-done.24 = bf16[64,4096]{1,0:T(8,128)(2,1)S(1)} collective-permute-done((bf16[64,4096]{1,0:T(8,128)(2,1)S(1)}, bf16[64,4096]{1,0:T(8,128)(2,1)S(1)}, u32[]{:S(2)}, u32[]{:S(2)}) %collective-permute-start.24) | collective-permute-done | bytes 524320 | tf_op jit(solution)/shard_map/ppermute | solution.py:18
  128.5 5.9 %collective-permute-done.30 = bf16[64,4096]{1,0:T(8,128)(2,1)S(1)} collective-permute-done((bf16[64,4096]{1,0:T(8,128)(2,1)S(1)}, bf16[64,4096]{1,0:T(8,128)(2,1)S(1)}, u32[]{:S(2)}, u32[]{:S(2)}) %collective-permute-start.30) | collective-permute-done | bytes 524320 | tf_op jit(solution)/shard_map/ppermute | solution.py:18
  134.4 10.0 %collective-permute-done.31 = bf16[64,4096]{1,0:T(8,128)(2,1)S(1)} collective-permute-done((bf16[64,4096]{1,0:T(8,128)(2,1)S(1)}, bf16[64,4096]{1,0:T(8,128)(2,1)S(1)}, u32[]{:S(2)}, u32[]{:S(2)}) %collective-permute-start.31) | collective-permute-done | bytes 524320 | tf_op jit(solution)/shard_map/ppermute | solution.py:18
  146.9 3.2 %collective-permute-start.32 = (bf16[64,4096]{1,0:T(8,128)(2,1)S(1)}, bf16[64,4096]{1,0:T(8,128)(2,1)S(1)}, u32[]{:S(2)}, u32[]{:S(2)}) collective-permute-start(bf16[64,4096]{1,0:T(8,128)(2,1)S(1)} %add_convert_fusion.7), channel_id=1, source_target_pairs={{0,6},{2,0},{4,2},{6,4},{1,7},{3,1},{5,3},{7,5},{8,14},{10,8},{12,... | collective-permute-start | bytes 1572872 | tf_op jit(solution)/shard_map/ppermute | solution.py:18
  150.1 8.4 %ffn.6 = (bf16[128,4096]{1,0:T(8,128)(2,1)S(1)}, bf16[128,4096]{1,0:T(8,128)(2,1)S(1)}) custom-call(bf16[128,4096]{1,0:T(8,128)(2,1)S(1)} %get-tuple-element.89.refs_0_, bf16[128,4096]{1,0:T(8,128)(2,1)S(1)} %get-tuple-element.90.refs_1_, bf16[1792,4096]{1,0:T(8,128)(2,1)S(1)} %get-tuple-element.73.refs_4_.refs_2_, ...), custom_call_target="tpu_custom_call" | custom-call | flops 5637144576 | tf_op jit(solution)/shard_map/ffn/pallas_call | solution.py:209
  158.6 4.7 %collective-permute-done.35 = bf16[64,4096]{1,0:T(8,128)(2,1)S(1)} collective-permute-done((bf16[64,4096]{1,0:T(8,128)(2,1)S(1)}, bf16[64,4096]{1,0:T(8,128)(2,1)S(1)}, u32[]{:S(2)}, u32[]{:S(2)}) %collective-permute-start.35) | collective-permute-done | bytes 524320 | tf_op jit(solution)/shard_map/ppermute | solution.py:18
  164.8 3.4 %collective-permute-start.44 = (bf16[32,4096]{1,0:T(8,128)(2,1)S(1)}, bf16[32,4096]{1,0:T(8,128)(2,1)S(1)}, u32[]{:S(2)}, u32[]{:S(2)}) collective-permute-start(bf16[32,4096]{1,0:T(8,128)(2,1)S(1)} %get-tuple-element.113), channel_id=1, source_target_pairs={{0,2},{2,4},{4,6},{6,0},{1,3},{3,5},{5,7},{7,1},{8,10},{10,12},{12... | collective-permute-start | bytes 786440 | tf_op jit(solution)/shard_map/ppermute | solution.py:18
  168.4 2.5 %collective-permute-start.36 = (bf16[32,4096]{1,0:T(8,128)(2,1)S(1)}, bf16[32,4096]{1,0:T(8,128)(2,1)S(1)}, u32[]{:S(2)}, u32[]{:S(2)}) collective-permute-start(bf16[32,4096]{1,0:T(8,128)(2,1)S(1)} %get-tuple-element.115), channel_id=1, source_target_pairs={{0,8},{8,16},{16,24},{24,0},{1,9},{9,17},{17,25},{25,1},{2,10},{10... | collective-permute-start | bytes 786440 | tf_op jit(solution)/shard_map/ppermute | solution.py:18
  176.4 2.5 %collective-permute-done.36 = bf16[32,4096]{1,0:T(8,128)(2,1)S(1)} collective-permute-done((bf16[32,4096]{1,0:T(8,128)(2,1)S(1)}, bf16[32,4096]{1,0:T(8,128)(2,1)S(1)}, u32[]{:S(2)}, u32[]{:S(2)}) %collective-permute-start.36) | collective-permute-done | bytes 262176 | tf_op jit(solution)/shard_map/ppermute | solution.py:18
  184.1 3.6 %collective-permute-done.46 = bf16[16,4096]{1,0:T(8,128)(2,1)S(1)} collective-permute-done((bf16[16,4096]{1,0:T(8,128)(2,1)S(1)}, bf16[16,4096]{1,0:T(8,128)(2,1)S(1)}, u32[]{:S(2)}, u32[]{:S(2)}) %collective-permute-start.46) | collective-permute-done | bytes 131104 | tf_op jit(solution)/shard_map/ppermute | solution.py:18
  (116 shorter events, 36.4 us)
Async XLA Ops:
  3.1 11.0 %collective-permute-start.1 = (bf16[16,4096]{1,0:T(8,128)(2,1)S(1)}, bf16[16,4096]{1,0:T(8,128)(2,1)S(1)}, u32[]{:S(2)}, u32[]{:S(2)}) collective-permute-start(bf16[16,4096]{1,0:T(8,128)(2,1)S(1)} %pad_maximum_fusion.3), channel_id=1, source_target_pairs={{0,32},{32,64},{64,96},{96,0},{1,33},{33,65},{65,97},{97,1},{2,34}... | collective-permute-start | bytes 393224 | tf_op jit(solution)/shard_map/ppermute | solution.py:18
  13.6 59.5 %collective-permute-start.12 = (bf16[448,4096]{1,0:T(8,128)(2,1)S(1)}, bf16[448,4096]{1,0:T(8,128)(2,1)S(1)}, u32[]{:S(2)}, u32[]{:S(2)}) collective-permute-start(bf16[448,4096]{1,0:T(8,128)(2,1)S(1)} %get-tuple-element.61), channel_id=1, source_target_pairs={{0,1},{1,0},{2,3},{3,2},{4,5},{5,4},{6,7},{7,6},{8,9},{9,8},{10,11... | collective-permute-start | bytes 11010056 | tf_op jit(solution)/shard_map/ppermute | solution.py:22
  13.7 61.0 %collective-permute-start.13 = (bf16[448,4096]{1,0:T(8,128)(2,1)S(1)}, bf16[448,4096]{1,0:T(8,128)(2,1)S(1)}, u32[]{:S(2)}, u32[]{:S(2)}) collective-permute-start(bf16[448,4096]{1,0:T(8,128)(2,1)S(1)} %get-tuple-element.62), channel_id=1, source_target_pairs={{0,1},{1,0},{2,3},{3,2},{4,5},{5,4},{6,7},{7,6},{8,9},{9,8},{10,11... | collective-permute-start | bytes 11010056 | tf_op jit(solution)/shard_map/ppermute | solution.py:22
  14.2 62.0 %collective-permute-start.14 = (bf16[448,4096]{1,0:T(8,128)(2,1)S(1)}, bf16[448,4096]{1,0:T(8,128)(2,1)S(1)}, u32[]{:S(2)}, u32[]{:S(2)}) collective-permute-start(bf16[448,4096]{1,0:T(8,128)(2,1)S(1)} %get-tuple-element.63), channel_id=1, source_target_pairs={{0,1},{1,0},{2,3},{3,2},{4,5},{5,4},{6,7},{7,6},{8,9},{9,8},{10,11... | collective-permute-start | bytes 11010056 | tf_op jit(solution)/shard_map/ppermute | solution.py:22
  14.3 16.6 %collective-permute-start.3 = (bf16[32,4096]{1,0:T(8,128)(2,1)S(1)}, bf16[32,4096]{1,0:T(8,128)(2,1)S(1)}, u32[]{:S(2)}, u32[]{:S(2)}) collective-permute-start(bf16[32,4096]{1,0:T(8,128)(2,1)S(1)} %pad_maximum_fusion.1), channel_id=1, source_target_pairs={{0,24},{8,0},{16,8},{24,16},{1,25},{9,1},{17,9},{25,17},{2,26},{10... | collective-permute-start | bytes 786440 | tf_op jit(solution)/shard_map/ppermute | solution.py:18
  17.2 9.6 %collective-permute-start.2 = (bf16[32,4096]{1,0:T(8,128)(2,1)S(1)}, bf16[32,4096]{1,0:T(8,128)(2,1)S(1)}, u32[]{:S(2)}, u32[]{:S(2)}) collective-permute-start(bf16[32,4096]{1,0:T(8,128)(2,1)S(1)} %pad_maximum_fusion.1), channel_id=1, source_target_pairs={{0,8},{8,16},{16,24},{24,0},{1,9},{9,17},{17,25},{25,1},{2,10},{10... | collective-permute-start | bytes 786440 | tf_op jit(solution)/shard_map/ppermute | solution.py:18
  26.8 12.6 %collective-permute-start.9 = (bf16[32,4096]{1,0:T(8,128)(2,1)S(1)}, bf16[32,4096]{1,0:T(8,128)(2,1)S(1)}, u32[]{:S(2)}, u32[]{:S(2)}) collective-permute-start(bf16[32,4096]{1,0:T(8,128)(2,1)S(1)} %get-tuple-element.149), channel_id=1, source_target_pairs={{0,6},{2,0},{4,2},{6,4},{1,7},{3,1},{5,3},{7,5},{8,14},{10,8},{12,... | collective-permute-start | bytes 786440 | tf_op jit(solution)/shard_map/ppermute | solution.py:18
  45.5 14.8 %collective-permute-start.15 = (bf16[64,4096]{1,0:T(8,128)(2,1)S(1)}, bf16[64,4096]{1,0:T(8,128)(2,1)S(1)}, u32[]{:S(2)}, u32[]{:S(2)}) collective-permute-start(bf16[64,4096]{1,0:T(8,128)(2,1)S(1)} %pad_maximum_fusion), channel_id=1, source_target_pairs={{0,2},{2,4},{4,6},{6,0},{1,3},{3,5},{5,7},{7,1},{8,10},{10,12},{12... | collective-permute-start | bytes 1572872 | tf_op jit(solution)/shard_map/ppermute | solution.py:18
  58.1 10.4 %collective-permute-start.17 = (bf16[64,4096]{1,0:T(8,128)(2,1)S(1)}, bf16[64,4096]{1,0:T(8,128)(2,1)S(1)}, u32[]{:S(2)}, u32[]{:S(2)}) collective-permute-start(bf16[64,4096]{1,0:T(8,128)(2,1)S(1)} %get-tuple-element.128), channel_id=1, source_target_pairs={{0,8},{8,16},{16,24},{24,0},{1,9},{9,17},{17,25},{25,1},{2,10},{10... | collective-permute-start | bytes 1572872 | tf_op jit(solution)/shard_map/ppermute | solution.py:18
  60.4 12.0 %collective-permute-start.16 = (bf16[64,4096]{1,0:T(8,128)(2,1)S(1)}, bf16[64,4096]{1,0:T(8,128)(2,1)S(1)}, u32[]{:S(2)}, u32[]{:S(2)}) collective-permute-start(bf16[64,4096]{1,0:T(8,128)(2,1)S(1)} %get-tuple-element.153), channel_id=1, source_target_pairs={{0,6},{2,0},{4,2},{6,4},{1,7},{3,1},{5,3},{7,5},{8,14},{10,8},{12,... | collective-permute-start | bytes 1572872 | tf_op jit(solution)/shard_map/ppermute | solution.py:18
  68.5 14.5 %collective-permute-start.18 = (bf16[64,4096]{1,0:T(8,128)(2,1)S(1)}, bf16[64,4096]{1,0:T(8,128)(2,1)S(1)}, u32[]{:S(2)}, u32[]{:S(2)}) collective-permute-start(bf16[64,4096]{1,0:T(8,128)(2,1)S(1)} %get-tuple-element.143), channel_id=1, source_target_pairs={{0,24},{8,0},{16,8},{24,16},{1,25},{9,1},{17,9},{25,17},{2,26},{10... | collective-permute-start | bytes 1572872 | tf_op jit(solution)/shard_map/ppermute | solution.py:18
  72.4 11.9 %collective-permute-start.26 = (bf16[64,4096]{1,0:T(8,128)(2,1)S(1)}, bf16[64,4096]{1,0:T(8,128)(2,1)S(1)}, u32[]{:S(2)}, u32[]{:S(2)}) collective-permute-start(bf16[64,4096]{1,0:T(8,128)(2,1)S(1)} %pad_maximum_fusion), channel_id=1, source_target_pairs={{0,6},{2,0},{4,2},{6,4},{1,7},{3,1},{5,3},{7,5},{8,14},{10,8},{12,... | collective-permute-start | bytes 1572872 | tf_op jit(solution)/shard_map/ppermute | solution.py:18
  73.0 18.8 %collective-permute-start.28 = (bf16[64,4096]{1,0:T(8,128)(2,1)S(1)}, bf16[64,4096]{1,0:T(8,128)(2,1)S(1)}, u32[]{:S(2)}, u32[]{:S(2)}) collective-permute-start(bf16[64,4096]{1,0:T(8,128)(2,1)S(1)} %get-tuple-element.128), channel_id=1, source_target_pairs={{0,24},{8,0},{16,8},{24,16},{1,25},{9,1},{17,9},{25,17},{2,26},{10... | collective-permute-start | bytes 1572872 | tf_op jit(solution)/shard_map/ppermute | solution.py:18
  74.6 17.2 %collective-permute-start.25 = (bf16[64,4096]{1,0:T(8,128)(2,1)S(1)}, bf16[64,4096]{1,0:T(8,128)(2,1)S(1)}, u32[]{:S(2)}, u32[]{:S(2)}) collective-permute-start(bf16[64,4096]{1,0:T(8,128)(2,1)S(1)} %get-tuple-element.153), channel_id=1, source_target_pairs={{0,2},{2,4},{4,6},{6,0},{1,3},{3,5},{5,7},{7,1},{8,10},{10,12},{12... | collective-permute-start | bytes 1572872 | tf_op jit(solution)/shard_map/ppermute | solution.py:18
  76.2 18.9 %collective-permute-start.27 = (bf16[64,4096]{1,0:T(8,128)(2,1)S(1)}, bf16[64,4096]{1,0:T(8,128)(2,1)S(1)}, u32[]{:S(2)}, u32[]{:S(2)}) collective-permute-start(bf16[64,4096]{1,0:T(8,128)(2,1)S(1)} %get-tuple-element.143), channel_id=1, source_target_pairs={{0,8},{8,16},{16,24},{24,0},{1,9},{9,17},{17,25},{25,1},{2,10},{10... | collective-permute-start | bytes 1572872 | tf_op jit(solution)/shard_map/ppermute | solution.py:18
  83.0 19.0 %collective-permute-start.19 = (bf16[64,4096]{1,0:T(8,128)(2,1)S(1)}, bf16[64,4096]{1,0:T(8,128)(2,1)S(1)}, u32[]{:S(2)}, u32[]{:S(2)}) collective-permute-start(bf16[64,4096]{1,0:T(8,128)(2,1)S(1)} %collective-permute-done.15.refs_0_), channel_id=1, source_target_pairs={{0,2},{2,4},{4,6},{6,0},{1,3},{3,5},{5,7},{7,1},{8,10},{10,12},{12... | collective-permute-start | bytes 1572872 | tf_op jit(solution)/shard_map/ppermute | solution.py:18
  84.2 21.0 %collective-permute-start.20 = (bf16[64,4096]{1,0:T(8,128)(2,1)S(1)}, bf16[64,4096]{1,0:T(8,128)(2,1)S(1)}, u32[]{:S(2)}, u32[]{:S(2)}) collective-permute-start(bf16[64,4096]{1,0:T(8,128)(2,1)S(1)} %collective-permute-done.16.refs_1_), channel_id=1, source_target_pairs={{0,6},{2,0},{4,2},{6,4},{1,7},{3,1},{5,3},{7,5},{8,14},{10,8},{12,... | collective-permute-start | bytes 1572872 | tf_op jit(solution)/shard_map/ppermute | solution.py:18
  91.8 16.0 %collective-permute-start.21 = (bf16[64,4096]{1,0:T(8,128)(2,1)S(1)}, bf16[64,4096]{1,0:T(8,128)(2,1)S(1)}, u32[]{:S(2)}, u32[]{:S(2)}) collective-permute-start(bf16[64,4096]{1,0:T(8,128)(2,1)S(1)} %collective-permute-done.17.refs_2_), channel_id=1, source_target_pairs={{0,8},{8,16},{16,24},{24,0},{1,9},{9,17},{17,25},{25,1},{2,10},{10... | collective-permute-start | bytes 1572872 | tf_op jit(solution)/shard_map/ppermute | solution.py:18
  91.8 16.0 %collective-permute-start.22 = (bf16[64,4096]{1,0:T(8,128)(2,1)S(1)}, bf16[64,4096]{1,0:T(8,128)(2,1)S(1)}, u32[]{:S(2)}, u32[]{:S(2)}) collective-permute-start(bf16[64,4096]{1,0:T(8,128)(2,1)S(1)} %collective-permute-done.18.refs_3_), channel_id=1, source_target_pairs={{0,24},{8,0},{16,8},{24,16},{1,25},{9,1},{17,9},{25,17},{2,26},{10... | collective-permute-start | bytes 1572872 | tf_op jit(solution)/shard_map/ppermute | solution.py:18
  101.9 43.8 %collective-permute-start.39 = (bf16[64,4096]{1,0:T(8,128)(2,1)S(1)}, bf16[64,4096]{1,0:T(8,128)(2,1)S(1)}, u32[]{:S(2)}, u32[]{:S(2)}) collective-permute-start(bf16[64,4096]{1,0:T(8,128)(2,1)S(1)} %get-tuple-element.103), channel_id=1, source_target_pairs={{0,8},{8,16},{16,24},{24,0},{1,9},{9,17},{17,25},{25,1},{2,10},{10... | collective-permute-start | bytes 1572872 | tf_op jit(solution)/shard_map/ppermute | solution.py:18
  102.0 44.9 %collective-permute-start.42 = (bf16[64,4096]{1,0:T(8,128)(2,1)S(1)}, bf16[64,4096]{1,0:T(8,128)(2,1)S(1)}, u32[]{:S(2)}, u32[]{:S(2)}) collective-permute-start(bf16[64,4096]{1,0:T(8,128)(2,1)S(1)} %get-tuple-element.106), channel_id=1, source_target_pairs={{0,24},{8,0},{16,8},{24,16},{1,25},{9,1},{17,9},{25,17},{2,26},{10... | collective-permute-start | bytes 1572872 | tf_op jit(solution)/shard_map/ppermute | solution.py:18
  105.2 41.7 %collective-permute-start.34 = (bf16[64,4096]{1,0:T(8,128)(2,1)S(1)}, bf16[64,4096]{1,0:T(8,128)(2,1)S(1)}, u32[]{:S(2)}, u32[]{:S(2)}) collective-permute-start(bf16[64,4096]{1,0:T(8,128)(2,1)S(1)} %get-tuple-element.99), channel_id=1, source_target_pairs={{0,6},{2,0},{4,2},{6,4},{1,7},{3,1},{5,3},{7,5},{8,14},{10,8},{12,... | collective-permute-start | bytes 1572872 | tf_op jit(solution)/shard_map/ppermute | solution.py:18
  114.7 10.2 %collective-permute-start.23 = (bf16[64,4096]{1,0:T(8,128)(2,1)S(1)}, bf16[64,4096]{1,0:T(8,128)(2,1)S(1)}, u32[]{:S(2)}, u32[]{:S(2)}) collective-permute-start(bf16[64,4096]{1,0:T(8,128)(2,1)S(1)} %get-tuple-element.79), channel_id=1, source_target_pairs={{0,24},{8,0},{16,8},{24,16},{1,25},{9,1},{17,9},{25,17},{2,26},{10... | collective-permute-start | bytes 1572872 | tf_op jit(solution)/shard_map/ppermute | solution.py:18
  118.0 10.4 %collective-permute-start.24 = (bf16[64,4096]{1,0:T(8,128)(2,1)S(1)}, bf16[64,4096]{1,0:T(8,128)(2,1)S(1)}, u32[]{:S(2)}, u32[]{:S(2)}) collective-permute-start(bf16[64,4096]{1,0:T(8,128)(2,1)S(1)} %get-tuple-element.80), channel_id=1, source_target_pairs={{0,8},{8,16},{16,24},{24,0},{1,9},{9,17},{17,25},{25,1},{2,10},{10... | collective-permute-start | bytes 1572872 | tf_op jit(solution)/shard_map/ppermute | solution.py:18
  128.4 16.0 %collective-permute-start.31 = (bf16[64,4096]{1,0:T(8,128)(2,1)S(1)}, bf16[64,4096]{1,0:T(8,128)(2,1)S(1)}, u32[]{:S(2)}, u32[]{:S(2)}) collective-permute-start(bf16[64,4096]{1,0:T(8,128)(2,1)S(1)} %get-tuple-element.94), channel_id=1, source_target_pairs={{0,2},{2,4},{4,6},{6,0},{1,3},{3,5},{5,7},{7,1},{8,10},{10,12},{12... | collective-permute-start | bytes 1572872 | tf_op jit(solution)/shard_map/ppermute | solution.py:18
  134.4 24.1 %collective-permute-start.29 = (bf16[64,4096]{1,0:T(8,128)(2,1)S(1)}, bf16[64,4096]{1,0:T(8,128)(2,1)S(1)}, u32[]{:S(2)}, u32[]{:S(2)}) collective-permute-start(bf16[64,4096]{1,0:T(8,128)(2,1)S(1)} %get-tuple-element.92), channel_id=1, source_target_pairs={{0,2},{2,4},{4,6},{6,0},{1,3},{3,5},{5,7},{7,1},{8,10},{10,12},{12... | collective-permute-start | bytes 1572872 | tf_op jit(solution)/shard_map/ppermute | solution.py:18
  144.4 14.2 %collective-permute-start.40 = (bf16[64,4096]{1,0:T(8,128)(2,1)S(1)}, bf16[64,4096]{1,0:T(8,128)(2,1)S(1)}, u32[]{:S(2)}, u32[]{:S(2)}) collective-permute-start(bf16[64,4096]{1,0:T(8,128)(2,1)S(1)} %add_convert_fusion.3), channel_id=1, source_target_pairs={{0,24},{8,0},{16,8},{24,16},{1,25},{9,1},{17,9},{25,17},{2,26},{10... | collective-permute-start | bytes 1572872 | tf_op jit(solution)/shard_map/ppermute | solution.py:18
  145.7 12.8 %collective-permute-start.43 = (bf16[64,4096]{1,0:T(8,128)(2,1)S(1)}, bf16[64,4096]{1,0:T(8,128)(2,1)S(1)}, u32[]{:S(2)}, u32[]{:S(2)}) collective-permute-start(bf16[64,4096]{1,0:T(8,128)(2,1)S(1)} %add_convert_fusion.1), channel_id=1, source_target_pairs={{0,8},{8,16},{16,24},{24,0},{1,9},{9,17},{17,25},{25,1},{2,10},{10... | collective-permute-start | bytes 1572872 | tf_op jit(solution)/shard_map/ppermute | solution.py:18
  146.9 16.4 %collective-permute-start.35 = (bf16[64,4096]{1,0:T(8,128)(2,1)S(1)}, bf16[64,4096]{1,0:T(8,128)(2,1)S(1)}, u32[]{:S(2)}, u32[]{:S(2)}) collective-permute-start(bf16[64,4096]{1,0:T(8,128)(2,1)S(1)} %add_convert_fusion.5), channel_id=1, source_target_pairs={{0,2},{2,4},{4,6},{6,0},{1,3},{3,5},{5,7},{7,1},{8,10},{10,12},{12... | collective-permute-start | bytes 1572872 | tf_op jit(solution)/shard_map/ppermute | solution.py:18
  146.9 16.4 %collective-permute-start.32 = (bf16[64,4096]{1,0:T(8,128)(2,1)S(1)}, bf16[64,4096]{1,0:T(8,128)(2,1)S(1)}, u32[]{:S(2)}, u32[]{:S(2)}) collective-permute-start(bf16[64,4096]{1,0:T(8,128)(2,1)S(1)} %add_convert_fusion.7), channel_id=1, source_target_pairs={{0,6},{2,0},{4,2},{6,4},{1,7},{3,1},{5,3},{7,5},{8,14},{10,8},{12,... | collective-permute-start | bytes 1572872 | tf_op jit(solution)/shard_map/ppermute | solution.py:18
  164.8 10.4 %collective-permute-start.44 = (bf16[32,4096]{1,0:T(8,128)(2,1)S(1)}, bf16[32,4096]{1,0:T(8,128)(2,1)S(1)}, u32[]{:S(2)}, u32[]{:S(2)}) collective-permute-start(bf16[32,4096]{1,0:T(8,128)(2,1)S(1)} %get-tuple-element.113), channel_id=1, source_target_pairs={{0,2},{2,4},{4,6},{6,0},{1,3},{3,5},{5,7},{7,1},{8,10},{10,12},{12... | collective-permute-start | bytes 786440 | tf_op jit(solution)/shard_map/ppermute | solution.py:18
  168.4 10.5 %collective-permute-start.36 = (bf16[32,4096]{1,0:T(8,128)(2,1)S(1)}, bf16[32,4096]{1,0:T(8,128)(2,1)S(1)}, u32[]{:S(2)}, u32[]{:S(2)}) collective-permute-start(bf16[32,4096]{1,0:T(8,128)(2,1)S(1)} %get-tuple-element.115), channel_id=1, source_target_pairs={{0,8},{8,16},{16,24},{24,0},{1,9},{9,17},{17,25},{25,1},{2,10},{10... | collective-permute-start | bytes 786440 | tf_op jit(solution)/shard_map/ppermute | solution.py:18
  (17 other events, 114.5 us)

commit v4 on v3

--- a/solution.py
+++ b/solution.py
@@ -319,7 +319,7 @@
     far_b, late_b, (a0, b0) = after(far_b, late[2:], [a0, b0])
     late_a = backward([add(v, w) for v, w in zip(late_a, far_a)], "z")
     late_b = backward([add(v, w) for v, w in zip(late_b, far_b)], "x")
-    y0 = ffn([a0, b0], w1, w2, looped=True)
+    y0 = ffn([a0, b0], w1, w2)
     ya = collect(y0[0], early_a, late_a)
     yb = collect(y0[1], early_b, late_b)
     done_a = ring_scatter(ya, "x")
@@ -328,8 +328,9 @@
     both = 2 * CAP
     groups = [done_a[:both], done_a[both:], done_b[:both], done_b[both:]]
     first = shift(groups[1], "task", -1)
-    last = [shift(groups[k], "task", -k) for k in range(2, RING)]
-    groups = [groups[0], first] + last
+    second = shift(groups[2], "task", -2)
+    last = shift(groups[3], "task", -3)
+    groups = [groups[0], first, second, last]
     kept = jnp.concatenate([v[:CAP] for v in groups], axis=0)
     swapped = swap_cores(jnp.concatenate([v[CAP:] for v in groups], axis=0))
     returned = jnp.concatenate([kept, swapped], axis=0)

time: 191 us -> 191 us (level)
  waiting for transfers between devices: 94 us -> 96 us
    ppermute x44, waiting for transfers between devices: 91 us -> 93 us  [shift(): return lax.ppermute(v, axis, [(i, (i + step) % RING) for i in range(RING)])]
  transfers between devices with their start and end apart: 49 -> 49, of which waited for: 25 -> 25; matrix products, arithmetic and copies ran while one was open for 1% -> 1% of each run, Pallas kernels for 20% -> 19%
where the time goes in v4:
time: 191 us; the launch traced here: 190 us
  waiting for transfers between devices  96 us (50%)
  starting transfers between devices  52.9 us (28%)
  Pallas kernels  37.4 us (20%)
  other arithmetic  1.99 us (1%)
    ppermute x44, waiting for transfers between devices, shift(): return lax.ppermute(v, axis, [(i, (i + step) % RING) for i in range(RING)])  93 us
    ppermute x44, starting transfers between devices, shift(): return lax.ppermute(v, axis, [(i, (i + step) % RING) for i in range(RING)])  52.1 us
    pallas_call x4, Pallas kernels, ffn(): pl.pallas_call(functools.partial(ffn_kernel, rows, looped), out_shape=[pl...  27.4 us
    pallas_call x1, Pallas kernels, load(): pl.pallas_call(load_kernel, out_shape=[pltpu.VMEM((2 * CORES * part, widt...  4.38 us
    pallas_call x1, Pallas kernels, pick(): pl.pallas_call(pick_kernel, out_shape=[pltpu.VMEM(w.shape[1:], BF16) for...  4.23 us
  transfers between devices with their start and end apart: 49, of which 25 were waited for; matrix products, arithmetic and copies ran while one was open for 1% of the time, Pallas kernels for 19%

profile of v4, /device:TPU:0, one launch (start us, length us, event | category | flops | bytes accessed | tf_op | source)
XLA Modules:
  0.0 190.3 jit_solution(16396498205640362025)
XLA Ops:
  4.9 3.0 %collective-permute-start.6 = (bf16[16,4096]{1,0:T(8,128)(2,1)S(1)}, bf16[16,4096]{1,0:T(8,128)(2,1)S(1)}, u32[]{:S(2)}, u32[]{:S(2)}) collective-permute-start(bf16[16,4096]{1,0:T(8,128)(2,1)S(1)} %pad_maximum_fusion.4), channel_id=1, source_target_pairs={{0,64},{32,96},{64,0},{96,32},{1,65},{33,97},{65,1},{97,33},{2,66}... | collective-permute-start | bytes 393224 | tf_op jit(solution)/shard_map/ppermute | solution.py:18
  9.3 4.2 %pick.1 = (bf16[448,4096]{1,0:T(8,128)(2,1)S(1)}, bf16[448,4096]{1,0:T(8,128)(2,1)S(1)}, bf16[448,4096]{1,0:T(8,128)(2,1)S(1)}) custom-call(s32[1]{0:T(128)S(6)} %sub.3.which_ref, bf16[2,448,4096]{2,1,0:T(8,128)(2,1)} %bitcast.6, bf16[2,448,4096]{2,1,0:T(8,128)(2,1)} %bitcast.8, bf16[2,448,4096]{2,1,0:T(8,128)(2,1)} %wd.3), custom_call_target="tpu_custom_call" | custom-call | tf_op jit(solution)/shard_map/pick/pallas_call | solution.py:126
  14.3 2.8 %collective-permute-start.3 = (bf16[32,4096]{1,0:T(8,128)(2,1)S(1)}, bf16[32,4096]{1,0:T(8,128)(2,1)S(1)}, u32[]{:S(2)}, u32[]{:S(2)}) collective-permute-start(bf16[32,4096]{1,0:T(8,128)(2,1)S(1)} %pad_maximum_fusion.1), channel_id=1, source_target_pairs={{0,24},{8,0},{16,8},{24,16},{1,25},{9,1},{17,9},{25,17},{2,26},{10... | collective-permute-start | bytes 786440 | tf_op jit(solution)/shard_map/ppermute | solution.py:18
  17.3 9.5 %collective-permute-done.2 = bf16[32,4096]{1,0:T(8,128)(2,1)S(1)} collective-permute-done((bf16[32,4096]{1,0:T(8,128)(2,1)S(1)}, bf16[32,4096]{1,0:T(8,128)(2,1)S(1)}, u32[]{:S(2)}, u32[]{:S(2)}) %collective-permute-start.2) | collective-permute-done | bytes 262176 | tf_op jit(solution)/shard_map/ppermute | solution.py:18
  26.8 4.0 %collective-permute-start.9 = (bf16[32,4096]{1,0:T(8,128)(2,1)S(1)}, bf16[32,4096]{1,0:T(8,128)(2,1)S(1)}, u32[]{:S(2)}, u32[]{:S(2)}) collective-permute-start(bf16[32,4096]{1,0:T(8,128)(2,1)S(1)} %get-tuple-element.149), channel_id=1, source_target_pairs={{0,6},{2,0},{4,2},{6,4},{1,7},{3,1},{5,3},{7,5},{8,14},{10,8},{12,... | collective-permute-start | bytes 786440 | tf_op jit(solution)/shard_map/ppermute | solution.py:18
  31.1 8.3 %collective-permute-done.8 = bf16[32,4096]{1,0:T(8,128)(2,1)S(1)} collective-permute-done((bf16[32,4096]{1,0:T(8,128)(2,1)S(1)}, bf16[32,4096]{1,0:T(8,128)(2,1)S(1)}, u32[]{:S(2)}, u32[]{:S(2)}) %collective-permute-start.8) | collective-permute-done | bytes 262176 | tf_op jit(solution)/shard_map/ppermute | solution.py:18
  39.4 3.3 %collective-permute-start.5 = (bf16[16,4096]{1,0:T(8,128)(2,1)S(1)}, bf16[16,4096]{1,0:T(8,128)(2,1)S(1)}, u32[]{:S(2)}, u32[]{:S(2)}) collective-permute-start(bf16[16,4096]{1,0:T(8,128)(2,1)S(1)} %slice.165), channel_id=1, source_target_pairs={{0,24},{8,0},{16,8},{24,16},{1,25},{9,1},{17,9},{25,17},{2,26},{10... | collective-permute-start | bytes 393224 | tf_op jit(solution)/shard_map/ppermute | solution.py:18
  42.8 2.7 %collective-permute-done.4 = bf16[16,4096]{1,0:T(8,128)(2,1)S(1)} collective-permute-done((bf16[16,4096]{1,0:T(8,128)(2,1)S(1)}, bf16[16,4096]{1,0:T(8,128)(2,1)S(1)}, u32[]{:S(2)}, u32[]{:S(2)}) %collective-permute-start.4) | collective-permute-done | bytes 131104 | tf_op jit(solution)/shard_map/ppermute | solution.py:18
  45.6 7.5 %collective-permute-done.10 = bf16[16,4096]{1,0:T(8,128)(2,1)S(1)} collective-permute-done((bf16[16,4096]{1,0:T(8,128)(2,1)S(1)}, bf16[16,4096]{1,0:T(8,128)(2,1)S(1)}, u32[]{:S(2)}, u32[]{:S(2)}) %collective-permute-start.10) | collective-permute-done | bytes 131104 | tf_op jit(solution)/shard_map/ppermute | solution.py:18
  53.1 4.9 %collective-permute-done.11 = bf16[16,4096]{1,0:T(8,128)(2,1)S(1)} collective-permute-done((bf16[16,4096]{1,0:T(8,128)(2,1)S(1)}, bf16[16,4096]{1,0:T(8,128)(2,1)S(1)}, u32[]{:S(2)}, u32[]{:S(2)}) %collective-permute-start.11) | collective-permute-done | bytes 131104 | tf_op jit(solution)/shard_map/ppermute | solution.py:18
  58.1 2.3 %collective-permute-done.15.refs_0_ = bf16[64,4096]{1,0:T(8,128)(2,1)S(1)} collective-permute-done((bf16[64,4096]{1,0:T(8,128)(2,1)S(1)}, bf16[64,4096]{1,0:T(8,128)(2,1)S(1)}, u32[]{:S(2)}, u32[]{:S(2)}) %collective-permute-start.15) | collective-permute-done | bytes 524320 | tf_op jit(solution)/shard_map/ppermute | solution.py:18
  60.8 7.7 %collective-permute-done.17.refs_2_ = bf16[64,4096]{1,0:T(8,128)(2,1)S(1)} collective-permute-done((bf16[64,4096]{1,0:T(8,128)(2,1)S(1)}, bf16[64,4096]{1,0:T(8,128)(2,1)S(1)}, u32[]{:S(2)}, u32[]{:S(2)}) %collective-permute-start.17) | collective-permute-done | bytes 524320 | tf_op jit(solution)/shard_map/ppermute | solution.py:18
  68.5 3.9 %collective-permute-done.16.refs_1_ = bf16[64,4096]{1,0:T(8,128)(2,1)S(1)} collective-permute-done((bf16[64,4096]{1,0:T(8,128)(2,1)S(1)}, bf16[64,4096]{1,0:T(8,128)(2,1)S(1)}, u32[]{:S(2)}, u32[]{:S(2)}) %collective-permute-start.16) | collective-permute-done | bytes 524320 | tf_op jit(solution)/shard_map/ppermute | solution.py:18
  76.4 4.4 %load.1 = (bf16[1792,4096]{1,0:T(8,128)(2,1)S(1)}, bf16[896,4096]{1,0:T(8,128)(2,1)S(1)}) custom-call(s32[1]{0:T(128)} %bitcast.1.core_ref, bf16[2,448,4096]{2,1,0:T(8,128)(2,1)} %bitcast.7, bf16[448,4096]{1,0:T(8,128)(2,1)S(1)} %collective-permute-done.12.wpg, bf16[2,448,4096]{2,1,0:T(8,128)(2,1)} %bitcast.9, ...), custom_call_target="tpu_custom_call" | custom-call | tf_op jit(solution)/shard_map/load/pallas_call | solution.py:154
  80.8 2.2 %collective-permute-done.18.refs_3_ = bf16[64,4096]{1,0:T(8,128)(2,1)S(1)} collective-permute-done((bf16[64,4096]{1,0:T(8,128)(2,1)S(1)}, bf16[64,4096]{1,0:T(8,128)(2,1)S(1)}, u32[]{:S(2)}, u32[]{:S(2)}) %collective-permute-start.18) | collective-permute-done | bytes 524320 | tf_op jit(solution)/shard_map/ppermute | solution.py:18
  86.2 5.6 %collective-permute-done.28.refs_3_ = bf16[64,4096]{1,0:T(8,128)(2,1)S(1)} collective-permute-done((bf16[64,4096]{1,0:T(8,128)(2,1)S(1)}, bf16[64,4096]{1,0:T(8,128)(2,1)S(1)}, u32[]{:S(2)}, u32[]{:S(2)}) %collective-permute-start.28) | collective-permute-done | bytes 524320 | tf_op jit(solution)/shard_map/ppermute | solution.py:18
  91.8 3.2 %collective-permute-start.22 = (bf16[64,4096]{1,0:T(8,128)(2,1)S(1)}, bf16[64,4096]{1,0:T(8,128)(2,1)S(1)}, u32[]{:S(2)}, u32[]{:S(2)}) collective-permute-start(bf16[64,4096]{1,0:T(8,128)(2,1)S(1)} %collective-permute-done.18.refs_3_), channel_id=1, source_target_pairs={{0,24},{8,0},{16,8},{24,16},{1,25},{9,1},{17,9},{25,17},{2,26},{10... | collective-permute-start | bytes 1572872 | tf_op jit(solution)/shard_map/ppermute | solution.py:18
  95.0 6.8 %ffn.7 = (bf16[64,4096]{1,0:T(8,128)(2,1)S(1)}, bf16[64,4096]{1,0:T(8,128)(2,1)S(1)}, bf16[64,4096]{1,0:T(8,128)(2,1)S(1)}, bf16[64,4096]{1,0:T(8,128)(2,1)S(1)}) custom-call(bf16[64,4096]{1,0:T(8,128)(2,1)S(1)} %collective-permute-done.25.refs_0_, bf16[64,4096]{1,0:T(8,128)(2,1)S(1)} %collective-permute-done.26.refs_1_, ...), custom_call_target="tpu_custom_call" | custom-call | flops 5637144576 | tf_op jit(solution)/shard_map/ffn/pallas_call | solution.py:209
  102.0 3.2 %collective-permute-start.42 = (bf16[64,4096]{1,0:T(8,128)(2,1)S(1)}, bf16[64,4096]{1,0:T(8,128)(2,1)S(1)}, u32[]{:S(2)}, u32[]{:S(2)}) collective-permute-start(bf16[64,4096]{1,0:T(8,128)(2,1)S(1)} %get-tuple-element.106), channel_id=1, source_target_pairs={{0,24},{8,0},{16,8},{24,16},{1,25},{9,1},{17,9},{25,17},{2,26},{10... | collective-permute-start | bytes 1572872 | tf_op jit(solution)/shard_map/ppermute | solution.py:18
  107.8 6.9 %ffn.4 = (bf16[64,4096]{1,0:T(8,128)(2,1)S(1)}, bf16[64,4096]{1,0:T(8,128)(2,1)S(1)}, bf16[64,4096]{1,0:T(8,128)(2,1)S(1)}, bf16[64,4096]{1,0:T(8,128)(2,1)S(1)}) custom-call(bf16[64,4096]{1,0:T(8,128)(2,1)S(1)} %collective-permute-done.19.refs_0_, bf16[64,4096]{1,0:T(8,128)(2,1)S(1)} %collective-permute-done.20.refs_1_, ...), custom_call_target="tpu_custom_call" | custom-call | flops 5637144576 | tf_op jit(solution)/shard_map/ffn/pallas_call | solution.py:209
  114.7 3.3 %collective-permute-start.23 = (bf16[64,4096]{1,0:T(8,128)(2,1)S(1)}, bf16[64,4096]{1,0:T(8,128)(2,1)S(1)}, u32[]{:S(2)}, u32[]{:S(2)}) collective-permute-start(bf16[64,4096]{1,0:T(8,128)(2,1)S(1)} %get-tuple-element.79), channel_id=1, source_target_pairs={{0,24},{8,0},{16,8},{24,16},{1,25},{9,1},{17,9},{25,17},{2,26},{10... | collective-permute-start | bytes 1572872 | tf_op jit(solution)/shard_map/ppermute | solution.py:18
  118.0 6.9 %ffn.5 = (bf16[64,4096]{1,0:T(8,128)(2,1)S(1)}, bf16[64,4096]{1,0:T(8,128)(2,1)S(1)}, bf16[64,4096]{1,0:T(8,128)(2,1)S(1)}, bf16[64,4096]{1,0:T(8,128)(2,1)S(1)}) custom-call(bf16[64,4096]{1,0:T(8,128)(2,1)S(1)} %collective-permute-done.15.refs_0_, bf16[64,4096]{1,0:T(8,128)(2,1)S(1)} %collective-permute-done.16.refs_1_, ...), custom_call_target="tpu_custom_call" | custom-call | flops 5637144576 | tf_op jit(solution)/shard_map/ffn/pallas_call | solution.py:209
  125.9 2.5 %collective-permute-done.24 = bf16[64,4096]{1,0:T(8,128)(2,1)S(1)} collective-permute-done((bf16[64,4096]{1,0:T(8,128)(2,1)S(1)}, bf16[64,4096]{1,0:T(8,128)(2,1)S(1)}, u32[]{:S(2)}, u32[]{:S(2)}) %collective-permute-start.24) | collective-permute-done | bytes 524320 | tf_op jit(solution)/shard_map/ppermute | solution.py:18
  128.5 5.9 %collective-permute-done.30 = bf16[64,4096]{1,0:T(8,128)(2,1)S(1)} collective-permute-done((bf16[64,4096]{1,0:T(8,128)(2,1)S(1)}, bf16[64,4096]{1,0:T(8,128)(2,1)S(1)}, u32[]{:S(2)}, u32[]{:S(2)}) %collective-permute-start.30) | collective-permute-done | bytes 524320 | tf_op jit(solution)/shard_map/ppermute | solution.py:18
  134.4 10.0 %collective-permute-done.31 = bf16[64,4096]{1,0:T(8,128)(2,1)S(1)} collective-permute-done((bf16[64,4096]{1,0:T(8,128)(2,1)S(1)}, bf16[64,4096]{1,0:T(8,128)(2,1)S(1)}, u32[]{:S(2)}, u32[]{:S(2)}) %collective-permute-start.31) | collective-permute-done | bytes 524320 | tf_op jit(solution)/shard_map/ppermute | solution.py:18
  146.9 3.2 %collective-permute-start.32 = (bf16[64,4096]{1,0:T(8,128)(2,1)S(1)}, bf16[64,4096]{1,0:T(8,128)(2,1)S(1)}, u32[]{:S(2)}, u32[]{:S(2)}) collective-permute-start(bf16[64,4096]{1,0:T(8,128)(2,1)S(1)} %add_convert_fusion.7), channel_id=1, source_target_pairs={{0,6},{2,0},{4,2},{6,4},{1,7},{3,1},{5,3},{7,5},{8,14},{10,8},{12,... | collective-permute-start | bytes 1572872 | tf_op jit(solution)/shard_map/ppermute | solution.py:18
  150.1 6.8 %ffn.6 = (bf16[128,4096]{1,0:T(8,128)(2,1)S(1)}, bf16[128,4096]{1,0:T(8,128)(2,1)S(1)}) custom-call(bf16[128,4096]{1,0:T(8,128)(2,1)S(1)} %get-tuple-element.89.refs_0_, bf16[128,4096]{1,0:T(8,128)(2,1)S(1)} %get-tuple-element.90.refs_1_, bf16[1792,4096]{1,0:T(8,128)(2,1)S(1)} %get-tuple-element.73.refs_4_.refs_2_, ...), custom_call_target="tpu_custom_call" | custom-call | flops 5637144576 | tf_op jit(solution)/shard_map/ffn/pallas_call | solution.py:209
  157.0 6.3 %collective-permute-done.35 = bf16[64,4096]{1,0:T(8,128)(2,1)S(1)} collective-permute-done((bf16[64,4096]{1,0:T(8,128)(2,1)S(1)}, bf16[64,4096]{1,0:T(8,128)(2,1)S(1)}, u32[]{:S(2)}, u32[]{:S(2)}) %collective-permute-start.35) | collective-permute-done | bytes 524320 | tf_op jit(solution)/shard_map/ppermute | solution.py:18
  164.8 3.4 %collective-permute-start.44 = (bf16[32,4096]{1,0:T(8,128)(2,1)S(1)}, bf16[32,4096]{1,0:T(8,128)(2,1)S(1)}, u32[]{:S(2)}, u32[]{:S(2)}) collective-permute-start(bf16[32,4096]{1,0:T(8,128)(2,1)S(1)} %get-tuple-element.113), channel_id=1, source_target_pairs={{0,2},{2,4},{4,6},{6,0},{1,3},{3,5},{5,7},{7,1},{8,10},{10,12},{12... | collective-permute-start | bytes 786440 | tf_op jit(solution)/shard_map/ppermute | solution.py:18
  168.5 2.5 %collective-permute-start.36 = (bf16[32,4096]{1,0:T(8,128)(2,1)S(1)}, bf16[32,4096]{1,0:T(8,128)(2,1)S(1)}, u32[]{:S(2)}, u32[]{:S(2)}) collective-permute-start(bf16[32,4096]{1,0:T(8,128)(2,1)S(1)} %get-tuple-element.115), channel_id=1, source_target_pairs={{0,8},{8,16},{16,24},{24,0},{1,9},{9,17},{17,25},{25,1},{2,10},{10... | collective-permute-start | bytes 786440 | tf_op jit(solution)/shard_map/ppermute | solution.py:18
  176.4 2.5 %collective-permute-done.36 = bf16[32,4096]{1,0:T(8,128)(2,1)S(1)} collective-permute-done((bf16[32,4096]{1,0:T(8,128)(2,1)S(1)}, bf16[32,4096]{1,0:T(8,128)(2,1)S(1)}, u32[]{:S(2)}, u32[]{:S(2)}) %collective-permute-start.36) | collective-permute-done | bytes 262176 | tf_op jit(solution)/shard_map/ppermute | solution.py:18
  184.1 3.6 %collective-permute-done.46 = bf16[16,4096]{1,0:T(8,128)(2,1)S(1)} collective-permute-done((bf16[16,4096]{1,0:T(8,128)(2,1)S(1)}, bf16[16,4096]{1,0:T(8,128)(2,1)S(1)}, u32[]{:S(2)}, u32[]{:S(2)}) %collective-permute-start.46) | collective-permute-done | bytes 131104 | tf_op jit(solution)/shard_map/ppermute | solution.py:18
  (116 shorter events, 36.4 us)
Async XLA Ops:
  3.1 11.0 %collective-permute-start.1 = (bf16[16,4096]{1,0:T(8,128)(2,1)S(1)}, bf16[16,4096]{1,0:T(8,128)(2,1)S(1)}, u32[]{:S(2)}, u32[]{:S(2)}) collective-permute-start(bf16[16,4096]{1,0:T(8,128)(2,1)S(1)} %pad_maximum_fusion.3), channel_id=1, source_target_pairs={{0,32},{32,64},{64,96},{96,0},{1,33},{33,65},{65,97},{97,1},{2,34}... | collective-permute-start | bytes 393224 | tf_op jit(solution)/shard_map/ppermute | solution.py:18
  13.6 59.5 %collective-permute-start.12 = (bf16[448,4096]{1,0:T(8,128)(2,1)S(1)}, bf16[448,4096]{1,0:T(8,128)(2,1)S(1)}, u32[]{:S(2)}, u32[]{:S(2)}) collective-permute-start(bf16[448,4096]{1,0:T(8,128)(2,1)S(1)} %get-tuple-element.61), channel_id=1, source_target_pairs={{0,1},{1,0},{2,3},{3,2},{4,5},{5,4},{6,7},{7,6},{8,9},{9,8},{10,11... | collective-permute-start | bytes 11010056 | tf_op jit(solution)/shard_map/ppermute | solution.py:22
  13.7 61.0 %collective-permute-start.13 = (bf16[448,4096]{1,0:T(8,128)(2,1)S(1)}, bf16[448,4096]{1,0:T(8,128)(2,1)S(1)}, u32[]{:S(2)}, u32[]{:S(2)}) collective-permute-start(bf16[448,4096]{1,0:T(8,128)(2,1)S(1)} %get-tuple-element.62), channel_id=1, source_target_pairs={{0,1},{1,0},{2,3},{3,2},{4,5},{5,4},{6,7},{7,6},{8,9},{9,8},{10,11... | collective-permute-start | bytes 11010056 | tf_op jit(solution)/shard_map/ppermute | solution.py:22
  14.2 62.0 %collective-permute-start.14 = (bf16[448,4096]{1,0:T(8,128)(2,1)S(1)}, bf16[448,4096]{1,0:T(8,128)(2,1)S(1)}, u32[]{:S(2)}, u32[]{:S(2)}) collective-permute-start(bf16[448,4096]{1,0:T(8,128)(2,1)S(1)} %get-tuple-element.63), channel_id=1, source_target_pairs={{0,1},{1,0},{2,3},{3,2},{4,5},{5,4},{6,7},{7,6},{8,9},{9,8},{10,11... | collective-permute-start | bytes 11010056 | tf_op jit(solution)/shard_map/ppermute | solution.py:22
  14.3 16.6 %collective-permute-start.3 = (bf16[32,4096]{1,0:T(8,128)(2,1)S(1)}, bf16[32,4096]{1,0:T(8,128)(2,1)S(1)}, u32[]{:S(2)}, u32[]{:S(2)}) collective-permute-start(bf16[32,4096]{1,0:T(8,128)(2,1)S(1)} %pad_maximum_fusion.1), channel_id=1, source_target_pairs={{0,24},{8,0},{16,8},{24,16},{1,25},{9,1},{17,9},{25,17},{2,26},{10... | collective-permute-start | bytes 786440 | tf_op jit(solution)/shard_map/ppermute | solution.py:18
  17.2 9.6 %collective-permute-start.2 = (bf16[32,4096]{1,0:T(8,128)(2,1)S(1)}, bf16[32,4096]{1,0:T(8,128)(2,1)S(1)}, u32[]{:S(2)}, u32[]{:S(2)}) collective-permute-start(bf16[32,4096]{1,0:T(8,128)(2,1)S(1)} %pad_maximum_fusion.1), channel_id=1, source_target_pairs={{0,8},{8,16},{16,24},{24,0},{1,9},{9,17},{17,25},{25,1},{2,10},{10... | collective-permute-start | bytes 786440 | tf_op jit(solution)/shard_map/ppermute | solution.py:18
  26.8 12.6 %collective-permute-start.9 = (bf16[32,4096]{1,0:T(8,128)(2,1)S(1)}, bf16[32,4096]{1,0:T(8,128)(2,1)S(1)}, u32[]{:S(2)}, u32[]{:S(2)}) collective-permute-start(bf16[32,4096]{1,0:T(8,128)(2,1)S(1)} %get-tuple-element.149), channel_id=1, source_target_pairs={{0,6},{2,0},{4,2},{6,4},{1,7},{3,1},{5,3},{7,5},{8,14},{10,8},{12,... | collective-permute-start | bytes 786440 | tf_op jit(solution)/shard_map/ppermute | solution.py:18
  45.5 14.8 %collective-permute-start.15 = (bf16[64,4096]{1,0:T(8,128)(2,1)S(1)}, bf16[64,4096]{1,0:T(8,128)(2,1)S(1)}, u32[]{:S(2)}, u32[]{:S(2)}) collective-permute-start(bf16[64,4096]{1,0:T(8,128)(2,1)S(1)} %pad_maximum_fusion), channel_id=1, source_target_pairs={{0,2},{2,4},{4,6},{6,0},{1,3},{3,5},{5,7},{7,1},{8,10},{10,12},{12... | collective-permute-start | bytes 1572872 | tf_op jit(solution)/shard_map/ppermute | solution.py:18
  58.1 10.4 %collective-permute-start.17 = (bf16[64,4096]{1,0:T(8,128)(2,1)S(1)}, bf16[64,4096]{1,0:T(8,128)(2,1)S(1)}, u32[]{:S(2)}, u32[]{:S(2)}) collective-permute-start(bf16[64,4096]{1,0:T(8,128)(2,1)S(1)} %get-tuple-element.128), channel_id=1, source_target_pairs={{0,8},{8,16},{16,24},{24,0},{1,9},{9,17},{17,25},{25,1},{2,10},{10... | collective-permute-start | bytes 1572872 | tf_op jit(solution)/shard_map/ppermute | solution.py:18
  60.4 12.0 %collective-permute-start.16 = (bf16[64,4096]{1,0:T(8,128)(2,1)S(1)}, bf16[64,4096]{1,0:T(8,128)(2,1)S(1)}, u32[]{:S(2)}, u32[]{:S(2)}) collective-permute-start(bf16[64,4096]{1,0:T(8,128)(2,1)S(1)} %get-tuple-element.153), channel_id=1, source_target_pairs={{0,6},{2,0},{4,2},{6,4},{1,7},{3,1},{5,3},{7,5},{8,14},{10,8},{12,... | collective-permute-start | bytes 1572872 | tf_op jit(solution)/shard_map/ppermute | solution.py:18
  68.5 14.5 %collective-permute-start.18 = (bf16[64,4096]{1,0:T(8,128)(2,1)S(1)}, bf16[64,4096]{1,0:T(8,128)(2,1)S(1)}, u32[]{:S(2)}, u32[]{:S(2)}) collective-permute-start(bf16[64,4096]{1,0:T(8,128)(2,1)S(1)} %get-tuple-element.143), channel_id=1, source_target_pairs={{0,24},{8,0},{16,8},{24,16},{1,25},{9,1},{17,9},{25,17},{2,26},{10... | collective-permute-start | bytes 1572872 | tf_op jit(solution)/shard_map/ppermute | solution.py:18
  72.4 11.9 %collective-permute-start.26 = (bf16[64,4096]{1,0:T(8,128)(2,1)S(1)}, bf16[64,4096]{1,0:T(8,128)(2,1)S(1)}, u32[]{:S(2)}, u32[]{:S(2)}) collective-permute-start(bf16[64,4096]{1,0:T(8,128)(2,1)S(1)} %pad_maximum_fusion), channel_id=1, source_target_pairs={{0,6},{2,0},{4,2},{6,4},{1,7},{3,1},{5,3},{7,5},{8,14},{10,8},{12,... | collective-permute-start | bytes 1572872 | tf_op jit(solution)/shard_map/ppermute | solution.py:18
  73.0 18.8 %collective-permute-start.28 = (bf16[64,4096]{1,0:T(8,128)(2,1)S(1)}, bf16[64,4096]{1,0:T(8,128)(2,1)S(1)}, u32[]{:S(2)}, u32[]{:S(2)}) collective-permute-start(bf16[64,4096]{1,0:T(8,128)(2,1)S(1)} %get-tuple-element.128), channel_id=1, source_target_pairs={{0,24},{8,0},{16,8},{24,16},{1,25},{9,1},{17,9},{25,17},{2,26},{10... | collective-permute-start | bytes 1572872 | tf_op jit(solution)/shard_map/ppermute | solution.py:18
  74.6 17.2 %collective-permute-start.25 = (bf16[64,4096]{1,0:T(8,128)(2,1)S(1)}, bf16[64,4096]{1,0:T(8,128)(2,1)S(1)}, u32[]{:S(2)}, u32[]{:S(2)}) collective-permute-start(bf16[64,4096]{1,0:T(8,128)(2,1)S(1)} %get-tuple-element.153), channel_id=1, source_target_pairs={{0,2},{2,4},{4,6},{6,0},{1,3},{3,5},{5,7},{7,1},{8,10},{10,12},{12... | collective-permute-start | bytes 1572872 | tf_op jit(solution)/shard_map/ppermute | solution.py:18
  76.2 18.9 %collective-permute-start.27 = (bf16[64,4096]{1,0:T(8,128)(2,1)S(1)}, bf16[64,4096]{1,0:T(8,128)(2,1)S(1)}, u32[]{:S(2)}, u32[]{:S(2)}) collective-permute-start(bf16[64,4096]{1,0:T(8,128)(2,1)S(1)} %get-tuple-element.143), channel_id=1, source_target_pairs={{0,8},{8,16},{16,24},{24,0},{1,9},{9,17},{17,25},{25,1},{2,10},{10... | collective-permute-start | bytes 1572872 | tf_op jit(solution)/shard_map/ppermute | solution.py:18
  83.0 19.0 %collective-permute-start.19 = (bf16[64,4096]{1,0:T(8,128)(2,1)S(1)}, bf16[64,4096]{1,0:T(8,128)(2,1)S(1)}, u32[]{:S(2)}, u32[]{:S(2)}) collective-permute-start(bf16[64,4096]{1,0:T(8,128)(2,1)S(1)} %collective-permute-done.15.refs_0_), channel_id=1, source_target_pairs={{0,2},{2,4},{4,6},{6,0},{1,3},{3,5},{5,7},{7,1},{8,10},{10,12},{12... | collective-permute-start | bytes 1572872 | tf_op jit(solution)/shard_map/ppermute | solution.py:18
  84.2 21.0 %collective-permute-start.20 = (bf16[64,4096]{1,0:T(8,128)(2,1)S(1)}, bf16[64,4096]{1,0:T(8,128)(2,1)S(1)}, u32[]{:S(2)}, u32[]{:S(2)}) collective-permute-start(bf16[64,4096]{1,0:T(8,128)(2,1)S(1)} %collective-permute-done.16.refs_1_), channel_id=1, source_target_pairs={{0,6},{2,0},{4,2},{6,4},{1,7},{3,1},{5,3},{7,5},{8,14},{10,8},{12,... | collective-permute-start | bytes 1572872 | tf_op jit(solution)/shard_map/ppermute | solution.py:18
  91.8 16.0 %collective-permute-start.21 = (bf16[64,4096]{1,0:T(8,128)(2,1)S(1)}, bf16[64,4096]{1,0:T(8,128)(2,1)S(1)}, u32[]{:S(2)}, u32[]{:S(2)}) collective-permute-start(bf16[64,4096]{1,0:T(8,128)(2,1)S(1)} %collective-permute-done.17.refs_2_), channel_id=1, source_target_pairs={{0,8},{8,16},{16,24},{24,0},{1,9},{9,17},{17,25},{25,1},{2,10},{10... | collective-permute-start | bytes 1572872 | tf_op jit(solution)/shard_map/ppermute | solution.py:18
  91.8 16.0 %collective-permute-start.22 = (bf16[64,4096]{1,0:T(8,128)(2,1)S(1)}, bf16[64,4096]{1,0:T(8,128)(2,1)S(1)}, u32[]{:S(2)}, u32[]{:S(2)}) collective-permute-start(bf16[64,4096]{1,0:T(8,128)(2,1)S(1)} %collective-permute-done.18.refs_3_), channel_id=1, source_target_pairs={{0,24},{8,0},{16,8},{24,16},{1,25},{9,1},{17,9},{25,17},{2,26},{10... | collective-permute-start | bytes 1572872 | tf_op jit(solution)/shard_map/ppermute | solution.py:18
  101.9 43.8 %collective-permute-start.39 = (bf16[64,4096]{1,0:T(8,128)(2,1)S(1)}, bf16[64,4096]{1,0:T(8,128)(2,1)S(1)}, u32[]{:S(2)}, u32[]{:S(2)}) collective-permute-start(bf16[64,4096]{1,0:T(8,128)(2,1)S(1)} %get-tuple-element.103), channel_id=1, source_target_pairs={{0,8},{8,16},{16,24},{24,0},{1,9},{9,17},{17,25},{25,1},{2,10},{10... | collective-permute-start | bytes 1572872 | tf_op jit(solution)/shard_map/ppermute | solution.py:18
  102.0 44.9 %collective-permute-start.42 = (bf16[64,4096]{1,0:T(8,128)(2,1)S(1)}, bf16[64,4096]{1,0:T(8,128)(2,1)S(1)}, u32[]{:S(2)}, u32[]{:S(2)}) collective-permute-start(bf16[64,4096]{1,0:T(8,128)(2,1)S(1)} %get-tuple-element.106), channel_id=1, source_target_pairs={{0,24},{8,0},{16,8},{24,16},{1,25},{9,1},{17,9},{25,17},{2,26},{10... | collective-permute-start | bytes 1572872 | tf_op jit(solution)/shard_map/ppermute | solution.py:18
  105.2 41.7 %collective-permute-start.34 = (bf16[64,4096]{1,0:T(8,128)(2,1)S(1)}, bf16[64,4096]{1,0:T(8,128)(2,1)S(1)}, u32[]{:S(2)}, u32[]{:S(2)}) collective-permute-start(bf16[64,4096]{1,0:T(8,128)(2,1)S(1)} %get-tuple-element.99), channel_id=1, source_target_pairs={{0,6},{2,0},{4,2},{6,4},{1,7},{3,1},{5,3},{7,5},{8,14},{10,8},{12,... | collective-permute-start | bytes 1572872 | tf_op jit(solution)/shard_map/ppermute | solution.py:18
  114.7 10.2 %collective-permute-start.23 = (bf16[64,4096]{1,0:T(8,128)(2,1)S(1)}, bf16[64,4096]{1,0:T(8,128)(2,1)S(1)}, u32[]{:S(2)}, u32[]{:S(2)}) collective-permute-start(bf16[64,4096]{1,0:T(8,128)(2,1)S(1)} %get-tuple-element.79), channel_id=1, source_target_pairs={{0,24},{8,0},{16,8},{24,16},{1,25},{9,1},{17,9},{25,17},{2,26},{10... | collective-permute-start | bytes 1572872 | tf_op jit(solution)/shard_map/ppermute | solution.py:18
  118.0 10.4 %collective-permute-start.24 = (bf16[64,4096]{1,0:T(8,128)(2,1)S(1)}, bf16[64,4096]{1,0:T(8,128)(2,1)S(1)}, u32[]{:S(2)}, u32[]{:S(2)}) collective-permute-start(bf16[64,4096]{1,0:T(8,128)(2,1)S(1)} %get-tuple-element.80), channel_id=1, source_target_pairs={{0,8},{8,16},{16,24},{24,0},{1,9},{9,17},{17,25},{25,1},{2,10},{10... | collective-permute-start | bytes 1572872 | tf_op jit(solution)/shard_map/ppermute | solution.py:18
  128.4 16.0 %collective-permute-start.31 = (bf16[64,4096]{1,0:T(8,128)(2,1)S(1)}, bf16[64,4096]{1,0:T(8,128)(2,1)S(1)}, u32[]{:S(2)}, u32[]{:S(2)}) collective-permute-start(bf16[64,4096]{1,0:T(8,128)(2,1)S(1)} %get-tuple-element.94), channel_id=1, source_target_pairs={{0,2},{2,4},{4,6},{6,0},{1,3},{3,5},{5,7},{7,1},{8,10},{10,12},{12... | collective-permute-start | bytes 1572872 | tf_op jit(solution)/shard_map/ppermute | solution.py:18
  134.4 22.5 %collective-permute-start.29 = (bf16[64,4096]{1,0:T(8,128)(2,1)S(1)}, bf16[64,4096]{1,0:T(8,128)(2,1)S(1)}, u32[]{:S(2)}, u32[]{:S(2)}) collective-permute-start(bf16[64,4096]{1,0:T(8,128)(2,1)S(1)} %get-tuple-element.92), channel_id=1, source_target_pairs={{0,2},{2,4},{4,6},{6,0},{1,3},{3,5},{5,7},{7,1},{8,10},{10,12},{12... | collective-permute-start | bytes 1572872 | tf_op jit(solution)/shard_map/ppermute | solution.py:18
  144.4 12.6 %collective-permute-start.40 = (bf16[64,4096]{1,0:T(8,128)(2,1)S(1)}, bf16[64,4096]{1,0:T(8,128)(2,1)S(1)}, u32[]{:S(2)}, u32[]{:S(2)}) collective-permute-start(bf16[64,4096]{1,0:T(8,128)(2,1)S(1)} %add_convert_fusion.3), channel_id=1, source_target_pairs={{0,24},{8,0},{16,8},{24,16},{1,25},{9,1},{17,9},{25,17},{2,26},{10... | collective-permute-start | bytes 1572872 | tf_op jit(solution)/shard_map/ppermute | solution.py:18
  145.7 11.3 %collective-permute-start.43 = (bf16[64,4096]{1,0:T(8,128)(2,1)S(1)}, bf16[64,4096]{1,0:T(8,128)(2,1)S(1)}, u32[]{:S(2)}, u32[]{:S(2)}) collective-permute-start(bf16[64,4096]{1,0:T(8,128)(2,1)S(1)} %add_convert_fusion.1), channel_id=1, source_target_pairs={{0,8},{8,16},{16,24},{24,0},{1,9},{9,17},{17,25},{25,1},{2,10},{10... | collective-permute-start | bytes 1572872 | tf_op jit(solution)/shard_map/ppermute | solution.py:18
  146.9 16.4 %collective-permute-start.35 = (bf16[64,4096]{1,0:T(8,128)(2,1)S(1)}, bf16[64,4096]{1,0:T(8,128)(2,1)S(1)}, u32[]{:S(2)}, u32[]{:S(2)}) collective-permute-start(bf16[64,4096]{1,0:T(8,128)(2,1)S(1)} %add_convert_fusion.5), channel_id=1, source_target_pairs={{0,2},{2,4},{4,6},{6,0},{1,3},{3,5},{5,7},{7,1},{8,10},{10,12},{12... | collective-permute-start | bytes 1572872 | tf_op jit(solution)/shard_map/ppermute | solution.py:18
  146.9 16.4 %collective-permute-start.32 = (bf16[64,4096]{1,0:T(8,128)(2,1)S(1)}, bf16[64,4096]{1,0:T(8,128)(2,1)S(1)}, u32[]{:S(2)}, u32[]{:S(2)}) collective-permute-start(bf16[64,4096]{1,0:T(8,128)(2,1)S(1)} %add_convert_fusion.7), channel_id=1, source_target_pairs={{0,6},{2,0},{4,2},{6,4},{1,7},{3,1},{5,3},{7,5},{8,14},{10,8},{12,... | collective-permute-start | bytes 1572872 | tf_op jit(solution)/shard_map/ppermute | solution.py:18
  164.8 10.4 %collective-permute-start.44 = (bf16[32,4096]{1,0:T(8,128)(2,1)S(1)}, bf16[32,4096]{1,0:T(8,128)(2,1)S(1)}, u32[]{:S(2)}, u32[]{:S(2)}) collective-permute-start(bf16[32,4096]{1,0:T(8,128)(2,1)S(1)} %get-tuple-element.113), channel_id=1, source_target_pairs={{0,2},{2,4},{4,6},{6,0},{1,3},{3,5},{5,7},{7,1},{8,10},{10,12},{12... | collective-permute-start | bytes 786440 | tf_op jit(solution)/shard_map/ppermute | solution.py:18
  168.5 10.4 %collective-permute-start.36 = (bf16[32,4096]{1,0:T(8,128)(2,1)S(1)}, bf16[32,4096]{1,0:T(8,128)(2,1)S(1)}, u32[]{:S(2)}, u32[]{:S(2)}) collective-permute-start(bf16[32,4096]{1,0:T(8,128)(2,1)S(1)} %get-tuple-element.115), channel_id=1, source_target_pairs={{0,8},{8,16},{16,24},{24,0},{1,9},{9,17},{17,25},{25,1},{2,10},{10... | collective-permute-start | bytes 786440 | tf_op jit(solution)/shard_map/ppermute | solution.py:18
  (17 other events, 114.5 us)
